TPU v7x, 32 devices: a whole 2x2x4 slice. The times are simulated.
32 devices in a mesh: grp: 2 (over y), hgt: 4 (over z), xs: 4 (over x, core).
Axes of the slice: x: 2, y: 2, z: 4, core: 2. Of those that a mesh axis runs over, the one named last changes fastest.
Arguments:
- thermal_field: float32 [512, 16384], P('hgt', ('grp', 'xs')), parts along dimension 1, may hold values from -6 to 6
- thermal_diffusivity: float32 [512, 16384], P('hgt', ('grp', 'xs')), parts along dimension 1, may hold values from 0.2 to 5
- boundary_group_lookup: int32 [128, 6], P('xs'), may hold values from 0 to 40, as said below
- boundary_entry_conductances: float32 [128, 6], P('xs'), may hold values from 0.1 to 1
- exported_boundary_groups: int32 [4, 2, 4], P('xs'), may hold values from 0 to 15, as said below
- domain_group_totals: int32 [4], P('xs'), may hold values from 16 to 32, as said below
- pipe_cavity_indicator: int32 [8192], P('xs'), may hold values 0 or 1
- boundary_vertex_matrix: float32 [64, 64], replicated, may hold values from -0.5 to 0.5
Outputs:
- charged: float32 [512, 16384], P('hgt', ('grp', 'xs')), parts along dimension 1
There are 2 independent parts, one for each index of `grp`. A program takes and returns all parts, laid end to end along the dimension named above; an argument that names none is the same for every part. Nothing has to cross between parts.
Inputs may be any that keep to these rules, and one draw needn't show every extreme that they name: `boundary_group_lookup`: each row lists its own block first, then up to 5 more extended-block indices below 40, then padding entries equal to 40; a row has one to 6 entries that are not padding. `exported_boundary_groups`: the 8 blocks of a partition are distinct and below 16. `domain_group_totals`: some partition has 32 active blocks and some has 16.
All inputs are finite; a program needn't handle non-finite values. No bound on the sum of `pipe_cavity_indicator` on one device may be relied on, other than what follows from the above.
Results may differ from a plain program's by a relative error of at most 0.0001.
Values sent between devices are 32-bit elements; how exact they have to be, the bound alone decides.
No kernel may reach another device: no remote copies, remote signals or barrier semaphores. Data moves between devices by JAX's collectives and lax.ppermute only.
A program may use at most 64 MiB of HBM per device.

v0:
```python
import functools
import math

import numpy as np
import jax
import jax.numpy as jnp
from jax import lax
from jax.experimental import pallas as pl
from jax.experimental.pallas import tpu as pltpu
from jax.sharding import PartitionSpec as P

axial_step = 0.5
lanes = 128
near_rows = 16
far_rows = 8
carried_rows = 24
unit_roundoff = 2.0**-24


def cheb_exact(order):
    index = np.arange(order, dtype=np.float64)
    angle = math.pi / (2.0 * (order - 1))
    row, col = index[:, None], index[None, :]
    difference = -2.0 * np.sin((row + col) * angle) * np.sin((row - col) * angle)
    weight = np.ones(order)
    weight[0] = weight[-1] = 2.0
    parity = np.where((row + col) % 2 == 0, 1.0, -1.0)
    off_diag = row != col
    entries = np.where(
        off_diag, weight[:, None] / weight[None, :] * parity / np.where(off_diag, difference, 1.0), 0.0
    )
    entries = entries - np.diag(entries.sum(axis=1))
    sine = np.sin(np.minimum(index, order - 1 - index) * (2.0 * angle))
    return -sine[:, None] * entries / (order - 1)


def row_basis(block, rank):
    return np.linalg.svd(block, full_matrices=False)[2][:rank]


@functools.lru_cache(maxsize=None)
def slab_factors(order, spans):
    slab = order // spans
    if spans & (spans - 1) or spans > 4 or slab < 4 * near_rows:
        return None
    full = cheb_exact(order)
    block = lambda s, t: full[s * slab : (s + 1) * slab, t * slab : (t + 1) * slab]
    ranks = [near_rows if any(abs(s - (s ^ x)) == 1 for s in range(spans)) else far_rows for x in range(1, spans)]
    first, joint = {}, {}
    carried, onward, left = {}, {}, {}
    for s in range(spans):
        others = [t for t in range(spans) if t != s]
        u, sigma, vt = np.linalg.svd(np.concatenate([block(s, t) for t in others], axis=1), full_matrices=False)
        left[s] = u[:, :carried_rows]
        rows = sigma[:carried_rows, None] * vt[:carried_rows]
        carried[s] = {t: rows[:, i * slab : (i + 1) * slab] for i, t in enumerate(others)}
        onward[s] = sum(carried[s][t] @ full[t * slab : (t + 1) * slab] for t in others)
        for t in others:
            first[s, t] = row_basis(block(s, t), ranks[(s ^ t) - 1])
            joint[s, t] = row_basis(
                np.concatenate([block(s, t), onward[s][:, t * slab : (t + 1) * slab]], axis=0), ranks[(s ^ t) - 1]
            )
    send_first, send_joint, apply_first, apply_joint, apply_carried = [], [], [], [], []
    for s in range(spans):
        partners = [s ^ x for x in range(1, spans)]
        send_first.append(np.concatenate([first[t, s] for t in partners], axis=0))
        send_joint.append(np.concatenate([joint[t, s] for t in partners], axis=0))
        own = onward[s][:, s * slab : (s + 1) * slab]
        apply_first.append(
            np.block(
                [
                    [block(s, s)] + [block(s, t) @ first[s, t].T for t in partners],
                    [np.zeros_like(own)] + [carried[s][t] @ first[s, t].T for t in partners],
                ]
            )
        )
        apply_joint.append(
            np.block(
                [
                    [block(s, s)] + [block(s, t) @ joint[s, t].T for t in partners],
                    [own] + [onward[s][:, t * slab : (t + 1) * slab] @ joint[s, t].T for t in partners],
                ]
            )
        )
        apply_carried.append(np.concatenate([block(s, s), left[s]], axis=1))
    stack = lambda parts: np.stack(parts).astype(np.float32)
    return dict(
        ranks=ranks,
        send_first=stack(send_first),
        send_joint=stack(send_joint),
        apply_first=stack(apply_first),
        apply_joint=stack(apply_joint),
        apply_carried=stack(apply_carried),
    )


def product(left, right):
    return jnp.dot(left, right, precision=lax.Precision.HIGHEST, preferred_element_type=jnp.float32)


def low_half():
    return lax.broadcasted_iota(jnp.int32, (1, lanes), 1) < lanes // 2


def tile_at(tile):
    return slice(tile * lanes, (tile + 1) * lanes)


def chunks(width):
    step = min(width, 512)
    return [slice(start, start + step) for start in range(0, width, step)]


def load(copies, sems):
    started = [pltpu.make_async_copy(source, target, sems.at[i]) for i, (source, target) in enumerate(copies)]
    for copy in started:
        copy.start()
    return started


def sides():
    first = 1 - lax.axis_index("xs") % 2
    return first, 1 - first


def take_face(source, exported, side):
    tiles = []
    for tile in range(exported.shape[1] // 2):
        parts = []
        for place in range(2):
            index = exported[side, 2 * tile + place]
            value = source[:, pl.ds(pl.multiple_of(index // 2 * lanes, lanes), lanes)]
            parts.append(jnp.where(index % 2 == place, value, pltpu.roll(value, lanes // 2, 1)))
        tiles.append(jnp.where(low_half(), parts[0], parts[1]))
    return jnp.concatenate(tiles, axis=1)


def faces_kernel(exported, field, first, second, faces, near, sems):
    got = load([(exported, faces), (field.at[:, pl.ds(0, near.shape[1])], near)], sems)
    for copy in got:
        copy.wait()
    for side, out in zip(sides(), (first, second)):
        out[...] = take_face(near, faces, side)


def prepare_kernel(sizes, total, pipe, matrix, field, *refs):
    count = len(sizes)
    stacks, (mask, spread, state, moments), outs = refs[:count], refs[count : count + 4], refs[count + 4 : 2 * count + 4]
    (sems,) = refs[2 * count + 4 :]
    where = lax.axis_index("hgt")
    got = load([(stack.at[where], out) for stack, out in zip(stacks, outs)], sems)
    width = matrix.shape[0]
    copies = spread.shape[0] // width
    wide = jnp.concatenate([matrix[...]] * copies, axis=1)
    tall = jnp.concatenate([wide] * copies, axis=0)
    row = lax.broadcasted_iota(jnp.int32, spread.shape, 0) // width
    col = lax.broadcasted_iota(jnp.int32, spread.shape, 1) // width
    spread[...] = jnp.where(row == col, tall, 0.0)
    for copy in got:
        copy.wait()
    block = lax.broadcasted_iota(jnp.int32, mask.shape, 1) // width
    live = block < total[0]
    mask[...] = jnp.where(live & (pipe[...] == 0), 1.0, 0.0).astype(jnp.float32)
    for piece in chunks(field.shape[1]):
        state[:, piece] = jnp.where(live[:, piece], field[:, piece], 0.0)
        moments[:, piece] = product(outs[0][...], state[:, piece])


def fill(extended, tile, value):
    extended[0, tile] = value
    extended[1, tile] = pltpu.roll(value, lanes // 2, 1)


def fill_own(extended, own):
    tiles = own.shape[1] // lanes
    for tile in range(tiles):
        fill(extended, tile, own[:, tile_at(tile)])
    fill(extended, extended.shape[1] - 1, jnp.zeros(extended.shape[2:], jnp.float32))


def fill_rim(extended, first, second):
    rim = first.shape[1] // lanes
    start = extended.shape[1] - 1 - 2 * rim
    for side, values in zip(sides(), (first, second)):
        for tile in range(rim):
            fill(extended, start + side * rim + tile, values[:, tile_at(tile)])


def conducted(lookup, conductance, mask, spread, extended, gathered, pieces):
    half = low_half()
    per = spread.shape[0] // lanes
    for piece in pieces:
        start = piece.start // lanes
        for tile in range(start, piece.stop // lanes):
            low, high = 2 * tile, 2 * tile + 1
            total = jnp.where(half, conductance[0, low], conductance[0, high]) * extended[0, tile]
            for slot in range(1, lookup.shape[0]):
                one, two = lookup[slot, low], lookup[slot, high]
                value = jnp.where(half, extended[one % 2, one // 2], extended[1 - two % 2, two // 2])
                total = total + jnp.where(half, conductance[slot, low], conductance[slot, high]) * value
            gathered[:, tile_at(tile)] = total
        moved = []
        for tile in range(start, piece.stop // lanes, per):
            part = slice(tile * lanes, (tile + per) * lanes)
            own = jnp.concatenate([extended[0, tile + i] for i in range(per)], axis=1)
            moved.append(own + mask[:, part] * product(gathered[:, part], spread[...]))
        yield piece, jnp.concatenate(moved, axis=1)


def store_rows(moved, outs, piece):
    start = 0
    for out in outs:
        out[:, piece] = moved[start : start + out.shape[0]]
        start += out.shape[0]


def stacked(refs, piece):
    return jnp.concatenate([ref[:, piece] for ref in refs], axis=0)


def moments_kernel(lookup, conductance, moments, first, second, mask, spread, send, *refs):
    outs, (table, weight, extended, gathered, sems) = refs[:-5], refs[-5:]
    got = load([(lookup, table), (conductance, weight)], sems)
    fill_own(extended, moments)
    fill_rim(extended, product(send[...], first[...]), product(send[...], second[...]))
    for copy in got:
        copy.wait()
    for piece, values in conducted(table, weight, mask, spread, extended, gathered, chunks(moments.shape[1])):
        store_rows(values, outs, piece)


def first_kernel(lookup, conductance, field, first, second, mask, spread, apply, out, slope, *scratch):
    table, weight, extended, gathered, sems = scratch
    got = load([(lookup, table), (conductance, weight)], sems)
    fill_own(extended, field)
    fill_rim(extended, first, second)
    for copy in got:
        copy.wait()
    local = apply[: field.shape[0], : field.shape[0]]
    for piece, values in conducted(table, weight, mask, spread, extended, gathered, chunks(field.shape[1])):
        out[:, piece] = values
        slope[:, piece] = product(local, values)


def flux_kernel(spans, slope, *refs):
    got, (kappa, apply, send), (flux, carried), outs = (
        refs[: spans - 1],
        refs[spans - 1 : spans + 2],
        refs[spans + 2 : spans + 4],
        refs[spans + 4 :],
    )
    slab = slope.shape[0]
    weights = apply[:, slab:]
    for piece in chunks(slope.shape[1]):
        far = product(weights, stacked(got, piece))
        carried[:, piece] = far[slab:]
        value = kappa[:, piece] * (slope[:, piece] + far[:slab])
        flux[:, piece] = value
        store_rows(product(send[...], value), outs, piece)


def local_kernel(field, carried, flux, mask, apply, out):
    slab = field.shape[0]
    weights = apply[:, :slab]
    for piece in chunks(field.shape[1]):
        step = axial_step * mask[:, piece] * product(weights, flux[:, piece])
        out[:slab, piece] = field[:, piece] + step[:slab]
        out[slab:, piece] = carried[:, piece] + step[slab:]


def rim_kernel(spans, exported, base, mask, apply, *refs):
    got, (first, second, faces, sems) = refs[: spans - 1], refs[spans - 1 :]
    (copy,) = load([(exported, faces)], sems)
    copy.wait()
    weights = apply[:, apply.shape[1] - sum(ref.shape[0] for ref in got) :]
    for side, out in zip(sides(), (first, second)):
        rows = jnp.concatenate([take_face(ref, faces, side) for ref in got], axis=0)
        out[...] = take_face(base, faces, side) + axial_step * take_face(mask, faces, side) * product(weights, rows)


def close_kernel(spans, base, mask, apply, onward, *refs):
    got, (out, slope) = refs[: spans - 1], refs[spans - 1 :]
    slab = out.shape[0]
    weights = apply[:, slab:]
    for piece in chunks(base.shape[1]):
        values = base[:, piece] + axial_step * mask[:, piece] * product(weights, stacked(got, piece))
        out[:, piece] = values[:slab]
        slope[:, piece] = product(onward[...], values)


def second_kernel(lookup, conductance, slope, first, second, mask, spread, kappa, onward, send, flux, *refs):
    outs, (table, weight, extended, gathered, sems) = refs[:-5], refs[-5:]
    got = load([(lookup, table), (conductance, weight)], sems)
    fill_own(extended, slope)
    fill_rim(extended, product(onward[...], first[...]), product(onward[...], second[...]))
    for copy in got:
        copy.wait()
    for piece, values in conducted(table, weight, mask, spread, extended, gathered, chunks(slope.shape[1])):
        value = kappa[:, piece] * values
        flux[:, piece] = value
        store_rows(product(send[...], value), outs, piece)


def rest_kernel(lookup, conductance, field, flux, first, second, mask, spread, apply, out, *scratch):
    table, weight, extended, gathered, sems = scratch
    slab = field.shape[0]
    got = load([(lookup, table), (conductance, weight)], sems)
    fill_own(extended, field)
    fill_rim(extended, first[:slab], second[:slab])
    for copy in got:
        copy.wait()
    local = apply[:slab, :slab]
    for piece, values in conducted(table, weight, mask, spread, extended, gathered, chunks(field.shape[1])):
        out[:, piece] = values + axial_step * mask[:, piece] * product(local, flux[:, piece])


def last_kernel(spans, base, mask, apply, *refs):
    got, (out,) = refs[: spans - 1], refs[spans - 1 :]
    slab = base.shape[0]
    weights = apply[:slab, slab:]
    for piece in chunks(base.shape[1]):
        out[:, piece] = base[:, piece] + axial_step * mask[:, piece] * product(weights, stacked(got, piece))


def in_place(array):
    return pltpu.with_memory_space_constraint(array, pltpu.HBM)


def call(kernel, far, near, shapes, scratch=(), flops=0, name=None):
    size = sum(4 * math.prod(shape) for shape in shapes) + sum(4 * a.size for a in near)
    return pl.pallas_call(
        kernel,
        in_specs=[pl.BlockSpec(memory_space=pltpu.HBM)] * len(far) + [pl.BlockSpec(memory_space=pltpu.VMEM)] * len(near),
        out_specs=[pl.BlockSpec(memory_space=pltpu.VMEM)] * len(shapes),
        out_shape=[jax.ShapeDtypeStruct(shape, jnp.float32) for shape in shapes],
        scratch_shapes=list(scratch),
        compiler_params=pltpu.CompilerParams(vmem_limit_bytes=24 * 2**20),
        cost_estimate=pl.CostEstimate(flops=flops, bytes_accessed=size, transcendentals=0),
        name=name,
    )(*[in_place(array) for array in far], *near)


def trade_faces(first, second):
    count = lax.axis_size("xs")
    swap = lambda start: [pair for i in range(start, count - 1, 2) for pair in ((i, i + 1), (i + 1, i))]
    return lax.ppermute(first, "xs", swap(0)), lax.ppermute(second, "xs", swap(1))


def trade_slabs(parts):
    count = lax.axis_size("hgt")
    return [lax.ppermute(part, "hgt", [(i, i ^ x) for i in range(count)]) for x, part in enumerate(parts, 1)]


def slab_body(factors, field, kappa, lookup, conductance, exported, totals, pipe, matrix):
    slab, nodes = field.shape
    spans = lax.axis_size("hgt")
    ranks = factors["ranks"]
    rows = sum(ranks)
    faces = exported.shape[1:]
    rim = faces[1] * matrix.shape[0]
    tables = [lookup.T, conductance.T]
    exported = exported.reshape(faces)
    tall = slab + carried_rows
    tiles = (nodes + 2 * rim) // lanes + 1
    sent = [(rank, nodes) for rank in ranks]
    whole = (slab, nodes)
    work = 2 * nodes * slab * slab

    def conduct_scratch(height):
        return [
            pltpu.SMEM(tables[0].shape, jnp.int32),
            pltpu.SMEM(tables[1].shape, jnp.float32),
            pltpu.VMEM((2, tiles, height, lanes), jnp.float32),
            pltpu.VMEM((height, nodes), jnp.float32),
            pltpu.SemaphoreType.DMA((2,)),
        ]

    face_scratch = pltpu.SMEM(faces, jnp.int32)
    first, second = call(
        faces_kernel,
        [exported, field],
        [],
        [(slab, rim)] * 2,
        [face_scratch, pltpu.VMEM((slab, nodes // 2), jnp.float32), pltpu.SemaphoreType.DMA((2,))],
        name="faces",
    )
    left, right = trade_faces(first, second)
    stacks = [factors[key] for key in ("send_first", "send_joint", "apply_first", "apply_joint", "apply_carried")]
    sizes = [stack.shape[1:] for stack in stacks]
    mask, spread, state, moments, send_first, send_joint, apply_first, apply_joint, onward = pl.pallas_call(
        functools.partial(prepare_kernel, sizes),
        in_specs=[pl.BlockSpec(memory_space=pltpu.SMEM)]
        + [pl.BlockSpec(memory_space=pltpu.VMEM)] * 3
        + [pl.BlockSpec(memory_space=pltpu.HBM)] * len(stacks),
        out_specs=[pl.BlockSpec(memory_space=pltpu.VMEM)] * (4 + len(stacks)),
        out_shape=[
            jax.ShapeDtypeStruct(shape, jnp.float32)
            for shape in [(1, nodes), (2 * lanes, 2 * lanes), whole, (rows, nodes)] + sizes
        ],
        scratch_shapes=[pltpu.SemaphoreType.DMA((len(stacks),))],
        compiler_params=pltpu.CompilerParams(vmem_limit_bytes=24 * 2**20),
        cost_estimate=pl.CostEstimate(flops=work, bytes_accessed=4 * slab * nodes, transcendentals=0),
        name="prepare",
    )(totals, pipe.reshape(1, nodes), matrix, field, *[in_place(stack) for stack in stacks])
    parts = call(
        moments_kernel, tables, [moments, left, right, mask, spread, send_first], sent, conduct_scratch(rows), name="moments"
    )
    parts = trade_slabs(parts)
    state, slope = call(
        first_kernel,
        tables,
        [state, left, right, mask, spread, apply_first],
        [whole, whole],
        conduct_scratch(slab),
        2 * work,
        name="first",
    )
    flux, carried, *joint = call(
        functools.partial(flux_kernel, spans),
        [],
        [slope, *parts, kappa, apply_first, send_joint],
        [whole, (carried_rows, nodes)] + sent,
        name="flux",
    )
    joint = trade_slabs(joint)
    (base,) = call(local_kernel, [], [state, carried, flux, mask, apply_joint], [(tall, nodes)], flops=work, name="local")
    first, second = call(
        functools.partial(rim_kernel, spans),
        [exported],
        [base, mask, apply_joint, *joint],
        [(tall, rim)] * 2,
        [face_scratch, pltpu.SemaphoreType.DMA((1,))],
        name="rim",
    )
    left, right = trade_faces(first, second)
    state, slope = call(
        functools.partial(close_kernel, spans), [], [base, mask, apply_joint, onward, *joint], [whole, whole], flops=work, name="close"
    )
    flux, *parts = call(
        second_kernel,
        tables,
        [slope, left, right, mask, spread, kappa, onward, send_first],
        [whole] + sent,
        conduct_scratch(slab),
        name="second",
    )
    parts = trade_slabs(parts)
    (base,) = call(
        rest_kernel,
        tables,
        [state, flux, left, right, mask, spread, apply_first],
        [whole],
        conduct_scratch(slab),
        2 * work,
        name="rest",
    )
    (state,) = call(functools.partial(last_kernel, spans), [], [base, mask, apply_first, *parts], [whole], name="last")
    return state


def padded_2(cells, sides, width):
    for axis, dim in sides:
        count = lax.axis_size(axis)
        ends = count - 1
        head = lax.slice_in_dim(cells, 0, width, axis=dim)
        tail = lax.slice_in_dim(cells, cells.shape[dim] - width, cells.shape[dim], axis=dim)
        cells = jnp.concatenate(
            [
                lax.ppermute(tail, axis, [(i, (i + 1) % count) for i in range(ends)]),
                cells,
                lax.ppermute(head, axis, [((i + 1) % count, i) for i in range(ends)]),
            ],
            axis=dim,
        )
    return cells


def cheb_matrix(order):
    index = jnp.arange(order)
    row_f = index[:, None].astype(jnp.float32)
    col_f = index[None, :].astype(jnp.float32)
    angle = math.pi / (2.0 * (order - 1))
    difference = -2.0 * jnp.sin((row_f + col_f) * angle) * jnp.sin((row_f - col_f) * angle)
    ends = (index == 0) | (index == order - 1)
    weight = jnp.where(ends, 2.0, 1.0).astype(jnp.float32)
    parity = jnp.where((index[:, None] + index[None, :]) % 2 == 0, 1.0, -1.0).astype(jnp.float32)
    off_diag = index[:, None] != index[None, :]
    safe_diff = jnp.where(off_diag, difference, jnp.float32(1.0))
    entries = jnp.where(
        off_diag, weight[:, None] / weight[None, :] * parity / safe_diff, jnp.float32(0.0)
    )
    entries = entries - jnp.diag(jnp.sum(entries, axis=1))
    mirror = jnp.minimum(index, order - 1 - index).astype(jnp.float32)
    sine = jnp.sin(mirror * (2.0 * angle))
    return -sine[:, None] * entries / (order - 1)


def slot_sum(source, indices, boundary_entry_conductances, total):
    for slot_index in range(indices.shape[1]):
        picked = source[:, indices[:, slot_index], :]
        total = total + boundary_entry_conductances[None, :, slot_index, None] * picked
    return total


def conduct(
    present_solution,
    boundary_group_lookup,
    boundary_entry_conductances,
    exported_boundary_groups,
    spread,
    slab_mask,
    width,
):
    height, plane_vertices = present_solution.shape
    blocks = plane_vertices // width
    face_count = exported_boundary_groups.shape[2]
    blocked = present_solution.reshape(height, blocks, width)
    outgoing = jnp.concatenate(
        [
            blocked[:, exported_boundary_groups[0, 0], :],
            blocked[:, exported_boundary_groups[0, 1], :],
        ],
        axis=1,
    )
    outgoing = outgoing.reshape(height, 2 * face_count * width)
    rim_width = face_count * width
    padded = padded_2(outgoing, (("xs", 1),), rim_width)
    from_left = padded[:, :rim_width].reshape(height, face_count, width)
    from_right = padded[:, padded.shape[1] - rim_width :].reshape(height, face_count, width)
    empty = jnp.zeros((height, 1, width), jnp.float32)
    gathered = jnp.zeros((height, blocks, width), jnp.float32)
    extended = jnp.concatenate([blocked, from_left, from_right, empty], axis=1)
    gathered = slot_sum(extended, boundary_group_lookup, boundary_entry_conductances, gathered)
    coupled = jnp.dot(
        gathered.reshape(-1, spread.shape[0]),
        spread,
        precision=lax.Precision.HIGHEST,
        preferred_element_type=jnp.float32,
    ).reshape(height, plane_vertices)
    return present_solution + slab_mask[None, :] * coupled


def axial(column_field, column_kappa, operator, column_mask):
    slope = jnp.dot(
        operator, column_field, precision=lax.Precision.HIGHEST, preferred_element_type=jnp.float32
    )
    second = jnp.dot(
        operator,
        column_kappa * slope,
        precision=lax.Precision.HIGHEST,
        preferred_element_type=jnp.float32,
    )
    return column_field + axial_step * column_mask[None, :] * second


def to_columns(moved):
    return lax.all_to_all(moved, "hgt", split_axis=1, concat_axis=0, tiled=True)


def to_slabs(result):
    return lax.all_to_all(result, "hgt", split_axis=0, concat_axis=1, tiled=True)


def column_body(
    thermal_field,
    thermal_diffusivity,
    boundary_group_lookup,
    boundary_entry_conductances,
    exported_boundary_groups,
    domain_group_totals,
    pipe_cavity_indicator,
    boundary_vertex_matrix,
):
    layer_sample_number, plane_vertices = thermal_field.shape
    width = boundary_vertex_matrix.shape[0]
    group_size = max(1, 128 // width)
    spread = jnp.kron(jnp.eye(group_size, dtype=jnp.float32), boundary_vertex_matrix)
    block_ids = jnp.arange(plane_vertices) // width
    live_groups = block_ids < domain_group_totals[0]
    slab_mask = jnp.where(live_groups & (pipe_cavity_indicator == 0), 1.0, 0.0).astype(jnp.float32)
    spans = lax.axis_size("hgt")
    column_count = plane_vertices // spans
    column_start = lax.axis_index("hgt") * column_count
    column_mask = lax.dynamic_slice_in_dim(slab_mask, column_start, column_count, 0)
    operator = cheb_matrix(layer_sample_number * spans)
    present_solution = jnp.where(live_groups[None, :], thermal_field, jnp.float32(0.0))
    moved = conduct(
        present_solution,
        boundary_group_lookup,
        boundary_entry_conductances,
        exported_boundary_groups,
        spread,
        slab_mask,
        width,
    )
    column_field, kappa_fixed = (
        lax.all_to_all(moved, "hgt", split_axis=1, concat_axis=0, tiled=True),
        lax.all_to_all(thermal_diffusivity, "hgt", split_axis=1, concat_axis=0, tiled=True),
    )
    result = axial(column_field, kappa_fixed, operator, column_mask)
    present_solution = to_slabs(result)
    moved = conduct(
        present_solution,
        boundary_group_lookup,
        boundary_entry_conductances,
        exported_boundary_groups,
        spread,
        slab_mask,
        width,
    )
    result = axial(to_columns(moved), kappa_fixed, operator, column_mask)
    present_solution = to_slabs(result)
    return present_solution


def body(field, kappa, lookup, conductance, exported, totals, pipe, matrix):
    spans = lax.axis_size("hgt")
    factors = slab_factors(field.shape[0] * spans, spans)
    args = (field, kappa, lookup, conductance, exported, totals, pipe, matrix)
    if factors is None or 2 * matrix.shape[0] != lanes:
        return column_body(*args)
    return slab_body(factors, *args)


def solution(mesh):
    in_specs = (
        P("hgt", ("grp", "xs")),
        P("hgt", ("grp", "xs")),
        P("xs", None),
        P("xs", None),
        P("xs", None, None),
        P("xs"),
        P("xs"),
        P(),
    )
    out_specs = P("hgt", ("grp", "xs"))
    return jax.shard_map(body, mesh=mesh, in_specs=in_specs, out_specs=out_specs, check_vma=False)
```

profile of v0, /device:TPU:1, one launch (start us, length us, event | category | flops | bytes accessed | tf_op | source)
XLA Modules:
  0.0 63.9 jit_solution(1358757550186262700)
XLA Ops:
  0.0 0.0 copy-start
  0.0 1.4 %faces.1 = (f32[128,256]{1,0:T(8,128)S(1)}, f32[128,256]{1,0:T(8,128)S(1)}) custom-call(s32[2,4]{1,0:T(2,128)} %bitcast.13, f32[128,2048]{1,0:T(8,128)} %field.3), custom_call_target="tpu_custom_call" | custom-call | bytes 262144 | tf_op jit(solution)/shard_map/faces/pallas_call | solution.py:331
  1.4 0.1 collective-permute-start
  1.5 4.5 %collective-permute-start.1 = (f32[128,256]{1,0:T(8,128)S(1)}, f32[128,256]{1,0:T(8,128)S(1)}, u32[]{:S(2)}, u32[]{:S(2)}) collective-permute-start(f32[128,256]{1,0:T(8,128)S(1)} %get-tuple-element.36), channel_id=1, source_target_pairs={{1,2},{2,1},{5,6},{6,5},{9,10},{10,9},{13,14},{14,13},{17,18},{18,... | collective-permute-start | bytes 393224 | tf_op jit(solution)/shard_map/ppermute | solution.py:346
  6.6 0.0 copy-done
  6.6 0.0 copy-start.2
  6.6 0.7 %copy-done.2 = f32[64,64]{1,0:T(8,128)S(1)} copy-done((f32[64,64]{1,0:T(8,128)S(1)}, f32[64,64]{1,0:T(8,128)}, u32[]{:S(2)}) %copy-start.2) | copy-done | bytes 16408
  7.4 0.0 copy-start.3
  7.4 0.7 %copy-done.3 = s32[2048]{0:T(1024)S(1)} copy-done((s32[2048]{0:T(1024)S(1)}, s32[2048]{0:T(1024)}, u32[]{:S(2)}) %copy-start.3) | copy-done | bytes 8216
  8.1 1.8 %prepare.1 = (f32[1,2048]{1,0:T(1,128)S(1)}, f32[256,256]{1,0:T(8,128)S(1)}, f32[128,2048]{1,0:T(8,128)S(1)}, f32[40,2048]{1,0:T(8,128)S(1)}, f32[40,128]{1,0:T(...) custom-call(s32[1]{0:T(128)S(6)} %copy.14.total, ...), custom_call_target="tpu_custom_call" | custom-call | flops 67108864 | bytes 1048576 | tf_op jit(solution)/shard_map/prepare/pallas_call | solution.py:390
  9.9 0.0 collective-permute-done.first
  9.9 0.0 collective-permute-done.1.second
  9.9 0.0 copy-start.1
  9.9 3.0 %moments.1 = (f32[16,2048]{1,0:T(8,128)S(1)}, f32[8,2048]{1,0:T(8,128)S(1)}, f32[16,2048]{1,0:T(8,128)S(1)}) custom-call(s32[6,32]{1,0:T(8,128)} %bitcast.5, f32[6,32]{1,0:T(8,128)} %bitcast.9, f32[40,2048]{1,0:T(8,128)S(1)} %get-tuple-element.42.moments, f32[128,256]{1,0:T(8,128)S(1)} %collective-permute-done.first, ...), custom_call_target="tpu_custom_call" | custom-call | bytes 1208320 | tf_op jit(solution)/shard_map/moments/pallas_call | solution.py:331
  12.9 1.4 %collective-permute-start.2 = (f32[16,2048]{1,0:T(8,128)S(1)}, f32[16,2048]{1,0:T(8,128)S(1)}, u32[]{:S(2)}, u32[]{:S(2)}) collective-permute-start(f32[16,2048]{1,0:T(8,128)S(1)} %get-tuple-element.44), channel_id=1, source_target_pairs={{0,4},{4,0},{8,12},{12,8},{1,5},{5,1},{9,13},{13,9},{2,6},{6,2},{1... | collective-permute-start | bytes 393224 | tf_op jit(solution)/shard_map/ppermute | solution.py:351
  14.3 2.2 %collective-permute-start.4 = (f32[16,2048]{1,0:T(8,128)S(1)}, f32[16,2048]{1,0:T(8,128)S(1)}, u32[]{:S(2)}, u32[]{:S(2)}) collective-permute-start(f32[16,2048]{1,0:T(8,128)S(1)} %get-tuple-element.46), channel_id=1, source_target_pairs={{0,12},{4,8},{8,4},{12,0},{1,13},{5,9},{9,5},{13,1},{2,14},{6,10},... | collective-permute-start | bytes 393224 | tf_op jit(solution)/shard_map/ppermute | solution.py:351
  16.5 0.1 collective-permute-start.3
  16.6 5.4 %first.1 = (f32[128,2048]{1,0:T(8,128)S(1)}, f32[128,2048]{1,0:T(8,128)S(1)}) custom-call(s32[6,32]{1,0:T(8,128)} %bitcast.6, f32[6,32]{1,0:T(8,128)} %bitcast.10, f32[128,2048]{1,0:T(8,128)S(1)} %get-tuple-element.34.field, f32[128,256]{1,0:T(8,128)S(1)} %collective-permute-done.first, f32[128,256]{1,0:T(8,128)S(1)} %collective-permute-done.1.second, ...), custom_call_target="tpu_custom_call" | custom-call | flops 134217728 | bytes 3780352 | tf_op jit(solution)/shard_map/first/pallas_call | solution.py:331
  22.0 2.1 %collective-permute-done.3.refs_1_ = f32[8,2048]{1,0:T(8,128)S(1)} collective-permute-done((f32[8,2048]{1,0:T(8,128)S(1)}, f32[8,2048]{1,0:T(8,128)S(1)}, u32[]{:S(2)}, u32[]{:S(2)}) %collective-permute-start.3) | collective-permute-done | bytes 65568 | tf_op jit(solution)/shard_map/ppermute | solution.py:351
  24.1 0.0 collective-permute-done.2.refs_0_
  24.1 0.0 collective-permute-done.4.refs_2_
  24.1 0.0 copy-done.1
  24.1 2.1 %flux.1 = (f32[128,2048]{1,0:T(8,128)S(1)}, f32[24,2048]{1,0:T(8,128)S(1)}, f32[16,2048]{1,0:T(8,128)S(1)}, f32[8,2048]{1,0:T(8,128)S(1)}, f32[16,2048]{1,0:T(8,128)S(1)}) custom-call(f32[128,2048]{1,0:T(8,128)S(1)} %get-tuple-element.41.slope, f32[16,2048]{1,0:T(8,128)S(1)} %collective-permute-done.2.refs_0_, f32[8,2048]{1,0:T(8,128)S(1)} %collective-permute-done.3.refs_1_, ...), custom_call_target="tpu_custom_call" | custom-call | bytes 4120320 | tf_op jit(solution)/shard_map/flux/pallas_call | solution.py:331
  26.2 0.2 collective-permute-start.5
  26.4 2.6 %collective-permute-start.7 = (f32[16,2048]{1,0:T(8,128)S(1)}, f32[16,2048]{1,0:T(8,128)S(1)}, u32[]{:S(2)}, u32[]{:S(2)}) collective-permute-start(f32[16,2048]{1,0:T(8,128)S(1)} %get-tuple-element.54), channel_id=1, source_target_pairs={{0,12},{4,8},{8,4},{12,0},{1,13},{5,9},{9,5},{13,1},{2,14},{6,10},... | collective-permute-start | bytes 393224 | tf_op jit(solution)/shard_map/ppermute | solution.py:351
  29.0 0.2 collective-permute-start.6
  29.2 1.1 %local.1.base = f32[152,2048]{1,0:T(8,128)S(1)} custom-call(f32[128,2048]{1,0:T(8,128)S(1)} %get-tuple-element.40.field, f32[24,2048]{1,0:T(8,128)S(1)} %get-tuple-element.48.carried, f32[128,2048]{1,0:T(8,128)S(1)} %get-tuple-element.49.flux, f32[1,2048]{1,0:T(1,128)S(1)} %get-tuple-element.37.mask, f32[152,168]{1,0:T(8,128)S(1)} %get-tuple-element.50.apply), custom_call_target="tpu_custom_call" | custom-call | flops 67108864 | bytes 3649280 | tf_op jit(solution)/shard_map/local/pallas_call | solution.py:331
  30.3 8.4 %collective-permute-done.6.refs_1_ = f32[8,2048]{1,0:T(8,128)S(1)} collective-permute-done((f32[8,2048]{1,0:T(8,128)S(1)}, f32[8,2048]{1,0:T(8,128)S(1)}, u32[]{:S(2)}, u32[]{:S(2)}) %collective-permute-start.6) | collective-permute-done | bytes 65568 | tf_op jit(solution)/shard_map/ppermute | solution.py:351
  38.8 0.0 collective-permute-done.5.refs_0_
  38.8 0.0 collective-permute-done.7.refs_2_
  38.8 1.3 %rim.1 = (f32[152,256]{1,0:T(8,128)S(1)}, f32[152,256]{1,0:T(8,128)S(1)}) custom-call(s32[2,4]{1,0:T(2,128)} %bitcast.14, f32[152,2048]{1,0:T(8,128)S(1)} %local.1.base, f32[1,2048]{1,0:T(1,128)S(1)} %get-tuple-element.37.mask, f32[152,168]{1,0:T(8,128)S(1)} %get-tuple-element.50.apply, f32[16,2048]{1,0:T(8,128)S(1)} %collective-permute-done.5.refs_0_, ...), custom_call_target="tpu_custom_call" | custom-call | bytes 1994496 | tf_op jit(solution)/shard_map/rim/pallas_call | solution.py:331
  40.0 0.6 collective-permute-start.8
  40.6 2.1 %collective-permute-start.9 = (f32[152,256]{1,0:T(8,128)S(1)}, f32[152,256]{1,0:T(8,128)S(1)}, u32[]{:S(2)}, u32[]{:S(2)}) collective-permute-start(f32[152,256]{1,0:T(8,128)S(1)} %get-tuple-element.58), channel_id=1, source_target_pairs={{1,2},{2,1},{5,6},{6,5},{9,10},{10,9},{13,14},{14,13},{17,18},{18,... | collective-permute-start | bytes 466952 | tf_op jit(solution)/shard_map/ppermute | solution.py:346
  42.7 2.6 %close.1 = (f32[128,2048]{1,0:T(8,128)S(1)}, f32[128,2048]{1,0:T(8,128)S(1)}) custom-call(f32[152,2048]{1,0:T(8,128)S(1)} %local.1.base, f32[1,2048]{1,0:T(1,128)S(1)} %get-tuple-element.37.mask, f32[152,168]{1,0:T(8,128)S(1)} %get-tuple-element.50.apply, f32[128,152]{1,0:T(8,128)S(1)} %get-tuple-element.51.onward, ...), custom_call_target="tpu_custom_call" | custom-call | flops 67108864 | bytes 3858176 | tf_op jit(solution)/shard_map/close/pallas_call | solution.py:331
  45.3 0.0 collective-permute-done.8.first
  45.3 1.8 %collective-permute-done.9.second = f32[152,256]{1,0:T(8,128)S(1)} collective-permute-done((f32[152,256]{1,0:T(8,128)S(1)}, f32[152,256]{1,0:T(8,128)S(1)}, u32[]{:S(2)}, u32[]{:S(2)}) %collective-permute-start.9) | collective-permute-done | bytes 155680 | tf_op jit(solution)/shard_map/ppermute | solution.py:346
  47.1 5.1 %second.1 = (f32[128,2048]{1,0:T(8,128)S(1)}, f32[16,2048]{1,0:T(8,128)S(1)}, f32[8,2048]{1,0:T(8,128)S(1)}, f32[16,2048]{1,0:T(8,128)S(1)}) custom-call(s32[6,32]{1,0:T(8,128)} %bitcast.7, f32[6,32]{1,0:T(8,128)} %bitcast.11, f32[128,2048]{1,0:T(8,128)S(1)} %get-tuple-element.56.slope, f32[152,256]{1,0:T(8,128)S(1)} %collective-permute-done.8.first, ...), custom_call_target="tpu_custom_call" | custom-call | bytes 4153344 | tf_op jit(solution)/shard_map/second/pallas_call | solution.py:331
  52.2 0.1 collective-permute-start.10
  52.3 2.4 %collective-permute-start.12 = (f32[16,2048]{1,0:T(8,128)S(1)}, f32[16,2048]{1,0:T(8,128)S(1)}, u32[]{:S(2)}, u32[]{:S(2)}) collective-permute-start(f32[16,2048]{1,0:T(8,128)S(1)} %get-tuple-element.62), channel_id=1, source_target_pairs={{0,12},{4,8},{8,4},{12,0},{1,13},{5,9},{9,5},{13,1},{2,14},{6,10},... | collective-permute-start | bytes 393224 | tf_op jit(solution)/shard_map/ppermute | solution.py:351
  54.7 0.2 collective-permute-start.11
  54.9 4.8 %rest.1.base = f32[128,2048]{1,0:T(8,128)S(1)} custom-call(s32[6,32]{1,0:T(8,128)} %bitcast.8, f32[6,32]{1,0:T(8,128)} %bitcast.12, f32[128,2048]{1,0:T(8,128)S(1)} %get-tuple-element.55.field, f32[128,2048]{1,0:T(8,128)S(1)} %get-tuple-element.59.flux, f32[152,256]{1,0:T(8,128)S(1)} %collective-permute-done.8.first, ...), custom_call_target="tpu_custom_call" | custom-call | flops 134217728 | bytes 3829504 | tf_op jit(solution)/shard_map/rest/pallas_call | solution.py:331
  59.7 2.3 %collective-permute-done.11.refs_1_ = f32[8,2048]{1,0:T(8,128)S(1)} collective-permute-done((f32[8,2048]{1,0:T(8,128)S(1)}, f32[8,2048]{1,0:T(8,128)S(1)}, u32[]{:S(2)}, u32[]{:S(2)}) %collective-permute-start.11) | collective-permute-done | bytes 65568 | tf_op jit(solution)/shard_map/ppermute | solution.py:351
  62.0 0.0 collective-permute-done.10.refs_0_
  62.0 0.0 collective-permute-done.12.refs_2_
  62.0 1.9 %last.1 = f32[128,2048]{1,0:T(8,128)} custom-call(f32[128,2048]{1,0:T(8,128)S(1)} %rest.1.base, f32[1,2048]{1,0:T(1,128)S(1)} %get-tuple-element.37.mask, f32[152,168]{1,0:T(8,128)S(1)} %get-tuple-element.39.apply.refs_4_, f32[16,2048]{1,0:T(8,128)S(1)} %collective-permute-done.10.refs_0_, f32[8,2048]{1,0:T(8,128)S(1)} %collective-permute-done.11.refs_1_, ...), custom_call_target="tpu_custom_call" | custom-call | bytes 2535168 | tf_op jit(solution)/shard_map/last/pallas_call | solution.py:331
Async XLA Ops:
  0.0 6.6 %copy-start = (f32[128,2048]{1,0:T(8,128)S(1)}, f32[128,2048]{1,0:T(8,128)}, u32[]{:S(2)}) copy-start(f32[128,2048]{1,0:T(8,128)} %field.3) | copy-start | bytes 3145732
  1.4 8.6 %collective-permute-start = (f32[128,256]{1,0:T(8,128)S(1)}, f32[128,256]{1,0:T(8,128)S(1)}, u32[]{:S(2)}, u32[]{:S(2)}) collective-permute-start(f32[128,256]{1,0:T(8,128)S(1)} %get-tuple-element.35), channel_id=1, source_target_pairs={{0,1},{1,0},{2,3},{3,2},{4,5},{5,4},{6,7},{7,6},{8,9},{9,8},{10,11... | collective-permute-start | bytes 393224 | tf_op jit(solution)/shard_map/ppermute | solution.py:346
  1.5 8.4 %collective-permute-start.1 = (f32[128,256]{1,0:T(8,128)S(1)}, f32[128,256]{1,0:T(8,128)S(1)}, u32[]{:S(2)}, u32[]{:S(2)}) collective-permute-start(f32[128,256]{1,0:T(8,128)S(1)} %get-tuple-element.36), channel_id=1, source_target_pairs={{1,2},{2,1},{5,6},{6,5},{9,10},{10,9},{13,14},{14,13},{17,18},{18,... | collective-permute-start | bytes 393224 | tf_op jit(solution)/shard_map/ppermute | solution.py:346
  6.6 0.8 %copy-start.2 = (f32[64,64]{1,0:T(8,128)S(1)}, f32[64,64]{1,0:T(8,128)}, u32[]{:S(2)}) copy-start(f32[64,64]{1,0:T(8,128)} %matrix.1) | copy-start | bytes 49156
  7.4 0.7 %copy-start.3 = (s32[2048]{0:T(1024)S(1)}, s32[2048]{0:T(1024)}, u32[]{:S(2)}) copy-start(s32[2048]{0:T(1024)} %param.19) | copy-start | bytes 24580
  9.9 14.2 %copy-start.1 = (f32[128,2048]{1,0:T(8,128)S(1)}, f32[128,2048]{1,0:T(8,128)}, u32[]{:S(2)}) copy-start(f32[128,2048]{1,0:T(8,128)} %kappa.1) | copy-start | bytes 3145732
  12.9 11.2 %collective-permute-start.2 = (f32[16,2048]{1,0:T(8,128)S(1)}, f32[16,2048]{1,0:T(8,128)S(1)}, u32[]{:S(2)}, u32[]{:S(2)}) collective-permute-start(f32[16,2048]{1,0:T(8,128)S(1)} %get-tuple-element.44), channel_id=1, source_target_pairs={{0,4},{4,0},{8,12},{12,8},{1,5},{5,1},{9,13},{13,9},{2,6},{6,2},{1... | collective-permute-start | bytes 393224 | tf_op jit(solution)/shard_map/ppermute | solution.py:351
  14.3 9.8 %collective-permute-start.4 = (f32[16,2048]{1,0:T(8,128)S(1)}, f32[16,2048]{1,0:T(8,128)S(1)}, u32[]{:S(2)}, u32[]{:S(2)}) collective-permute-start(f32[16,2048]{1,0:T(8,128)S(1)} %get-tuple-element.46), channel_id=1, source_target_pairs={{0,12},{4,8},{8,4},{12,0},{1,13},{5,9},{9,5},{13,1},{2,14},{6,10},... | collective-permute-start | bytes 393224 | tf_op jit(solution)/shard_map/ppermute | solution.py:351
  16.5 7.6 %collective-permute-start.3 = (f32[8,2048]{1,0:T(8,128)S(1)}, f32[8,2048]{1,0:T(8,128)S(1)}, u32[]{:S(2)}, u32[]{:S(2)}) collective-permute-start(f32[8,2048]{1,0:T(8,128)S(1)} %get-tuple-element.45), channel_id=1, source_target_pairs={{0,8},{4,12},{8,0},{12,4},{1,9},{5,13},{9,1},{13,5},{2,10},{6,14},... | collective-permute-start | bytes 196616 | tf_op jit(solution)/shard_map/ppermute | solution.py:351
  26.2 12.6 %collective-permute-start.5 = (f32[16,2048]{1,0:T(8,128)S(1)}, f32[16,2048]{1,0:T(8,128)S(1)}, u32[]{:S(2)}, u32[]{:S(2)}) collective-permute-start(f32[16,2048]{1,0:T(8,128)S(1)} %get-tuple-element.52), channel_id=1, source_target_pairs={{0,4},{4,0},{8,12},{12,8},{1,5},{5,1},{9,13},{13,9},{2,6},{6,2},{1... | collective-permute-start | bytes 393224 | tf_op jit(solution)/shard_map/ppermute | solution.py:351
  26.4 12.4 %collective-permute-start.7 = (f32[16,2048]{1,0:T(8,128)S(1)}, f32[16,2048]{1,0:T(8,128)S(1)}, u32[]{:S(2)}, u32[]{:S(2)}) collective-permute-start(f32[16,2048]{1,0:T(8,128)S(1)} %get-tuple-element.54), channel_id=1, source_target_pairs={{0,12},{4,8},{8,4},{12,0},{1,13},{5,9},{9,5},{13,1},{2,14},{6,10},... | collective-permute-start | bytes 393224 | tf_op jit(solution)/shard_map/ppermute | solution.py:351
  29.0 9.8 %collective-permute-start.6 = (f32[8,2048]{1,0:T(8,128)S(1)}, f32[8,2048]{1,0:T(8,128)S(1)}, u32[]{:S(2)}, u32[]{:S(2)}) collective-permute-start(f32[8,2048]{1,0:T(8,128)S(1)} %get-tuple-element.53), channel_id=1, source_target_pairs={{0,8},{4,12},{8,0},{12,4},{1,9},{5,13},{9,1},{13,5},{2,10},{6,14},... | collective-permute-start | bytes 196616 | tf_op jit(solution)/shard_map/ppermute | solution.py:351
  40.0 5.3 %collective-permute-start.8 = (f32[152,256]{1,0:T(8,128)S(1)}, f32[152,256]{1,0:T(8,128)S(1)}, u32[]{:S(2)}, u32[]{:S(2)}) collective-permute-start(f32[152,256]{1,0:T(8,128)S(1)} %get-tuple-element.57), channel_id=1, source_target_pairs={{0,1},{1,0},{2,3},{3,2},{4,5},{5,4},{6,7},{7,6},{8,9},{9,8},{10,11... | collective-permute-start | bytes 466952 | tf_op jit(solution)/shard_map/ppermute | solution.py:346
  40.6 6.5 %collective-permute-start.9 = (f32[152,256]{1,0:T(8,128)S(1)}, f32[152,256]{1,0:T(8,128)S(1)}, u32[]{:S(2)}, u32[]{:S(2)}) collective-permute-start(f32[152,256]{1,0:T(8,128)S(1)} %get-tuple-element.58), channel_id=1, source_target_pairs={{1,2},{2,1},{5,6},{6,5},{9,10},{10,9},{13,14},{14,13},{17,18},{18,... | collective-permute-start | bytes 466952 | tf_op jit(solution)/shard_map/ppermute | solution.py:346
  52.2 9.8 %collective-permute-start.10 = (f32[16,2048]{1,0:T(8,128)S(1)}, f32[16,2048]{1,0:T(8,128)S(1)}, u32[]{:S(2)}, u32[]{:S(2)}) collective-permute-start(f32[16,2048]{1,0:T(8,128)S(1)} %get-tuple-element.60), channel_id=1, source_target_pairs={{0,4},{4,0},{8,12},{12,8},{1,5},{5,1},{9,13},{13,9},{2,6},{6,2},{1... | collective-permute-start | bytes 393224 | tf_op jit(solution)/shard_map/ppermute | solution.py:351
  52.3 9.7 %collective-permute-start.12 = (f32[16,2048]{1,0:T(8,128)S(1)}, f32[16,2048]{1,0:T(8,128)S(1)}, u32[]{:S(2)}, u32[]{:S(2)}) collective-permute-start(f32[16,2048]{1,0:T(8,128)S(1)} %get-tuple-element.62), channel_id=1, source_target_pairs={{0,12},{4,8},{8,4},{12,0},{1,13},{5,9},{9,5},{13,1},{2,14},{6,10},... | collective-permute-start | bytes 393224 | tf_op jit(solution)/shard_map/ppermute | solution.py:351
  54.7 7.3 %collective-permute-start.11 = (f32[8,2048]{1,0:T(8,128)S(1)}, f32[8,2048]{1,0:T(8,128)S(1)}, u32[]{:S(2)}, u32[]{:S(2)}) collective-permute-start(f32[8,2048]{1,0:T(8,128)S(1)} %get-tuple-element.61), channel_id=1, source_target_pairs={{0,8},{4,12},{8,0},{12,4},{1,9},{5,13},{9,1},{13,5},{2,10},{6,14},... | collective-permute-start | bytes 196616 | tf_op jit(solution)/shard_map/ppermute | solution.py:351
where the time goes:
time: 64.3 us; the launch traced here: 63.9 us
  Pallas kernels  30.4 us (47%)
  starting transfers between devices  16.6 us (26%)
  waiting for transfers between devices  14.6 us (23%)
  local copies, waits for them, and re-layouts  1.46 us (2%)
  between operations  0.81 us (1%)
    pallas_call x10, Pallas kernels, call(): pl.pallas_call(kernel, in_specs=[pl.BlockSpec(memory_space=pltpu.HBM)] *...  28.5 us
    ppermute x9, waiting for transfers between devices, trade_slabs(): lax.ppermute(part, 'hgt', [(i, i ^ x) for i in range(count)])  12.8 us
    ppermute x9, starting transfers between devices, trade_slabs(): lax.ppermute(part, 'hgt', [(i, i ^ x) for i in range(count)])  9.38 us
    ppermute x2, starting transfers between devices, trade_faces(): lax.ppermute(second, 'xs', swap(1))  6.55 us
    ppermute x2, waiting for transfers between devices, trade_faces(): lax.ppermute(second, 'xs', swap(1))  1.85 us
    pallas_call x1, Pallas kernels, slab_body(): pl.pallas_call(functools.partial(prepare_kernel, sizes), in_specs=[pl.Blo...  1.84 us
    unnamed x8, local copies, waits for them, and re-layouts  1.46 us
  transfers between devices with their start and end apart: 13, of which 4 were waited for; matrix products, arithmetic and copies ran while one was open for 0% of the time, Pallas kernels for 25%

commit v1 on v0

--- a/solution.py
+++ b/solution.py
@@ -1,6 +1,7 @@
 import functools
 import math
 
+import ml_dtypes
 import numpy as np
 import jax
 import jax.numpy as jnp
@@ -11,10 +12,11 @@
 
 axial_step = 0.5
 lanes = 128
-near_rows = 16
-far_rows = 8
+near_rows = 12
+far_rows = 4
+joint_near_rows = 16
+joint_far_rows = 8
 carried_rows = 24
-unit_roundoff = 2.0**-24
 
 
 def cheb_exact(order):
@@ -38,14 +40,48 @@
     return np.linalg.svd(block, full_matrices=False)[2][:rank]
 
 
+def halves(matrix):
+    high = matrix.astype(ml_dtypes.bfloat16)
+    return high, (matrix - high.astype(np.float64)).astype(ml_dtypes.bfloat16)
+
+
+def pad_to(matrix, rows, cols):
+    return np.pad(matrix, ((0, rows - matrix.shape[0]), (0, cols - matrix.shape[1])))
+
+
+def round_up(size, step):
+    return -(-size // step) * step
+
+
+def as_left(matrix):
+    high, low = halves(pad_to(matrix, matrix.shape[0], round_up(matrix.shape[1], 16)))
+    return np.concatenate([high, high, low], axis=1)
+
+
+def fold(rows, half, axis):
+    whole = rows.shape[axis] // 8 * 8
+    head, tail = np.split(rows, [whole], axis=axis)
+    if not tail.shape[axis]:
+        return head, tail
+    zeros = np.zeros_like(tail)
+    return head, np.concatenate([zeros, tail] if half else [tail, zeros], axis=axis)
+
+
+def folded(parts, half, axis):
+    pairs = [fold(part, half, axis) for part in parts]
+    return np.concatenate([head for head, _ in pairs] + [tail for _, tail in pairs], axis=axis)
+
+
 @functools.lru_cache(maxsize=None)
 def slab_factors(order, spans):
     slab = order // spans
-    if spans & (spans - 1) or spans > 4 or slab < 4 * near_rows:
+    if spans & (spans - 1) or spans > 4 or slab < 128:
         return None
     full = cheb_exact(order)
     block = lambda s, t: full[s * slab : (s + 1) * slab, t * slab : (t + 1) * slab]
-    ranks = [near_rows if any(abs(s - (s ^ x)) == 1 for s in range(spans)) else far_rows for x in range(1, spans)]
+    near = [any(abs(s - (s ^ x)) == 1 for s in range(spans)) for x in range(1, spans)]
+    ranks = [near_rows if close else far_rows for close in near]
+    joint_ranks = [joint_near_rows if close else joint_far_rows for close in near]
     first, joint = {}, {}
     carried, onward, left = {}, {}, {}
     for s in range(spans):
@@ -58,44 +94,47 @@
         for t in others:
             first[s, t] = row_basis(block(s, t), ranks[(s ^ t) - 1])
             joint[s, t] = row_basis(
-                np.concatenate([block(s, t), onward[s][:, t * slab : (t + 1) * slab]], axis=0), ranks[(s ^ t) - 1]
+                np.concatenate([block(s, t), onward[s][:, t * slab : (t + 1) * slab]], axis=0), joint_ranks[(s ^ t) - 1]
             )
-    send_first, send_joint, apply_first, apply_joint, apply_carried = [], [], [], [], []
+    sets = {}
+
+    def add(name, matrix):
+        sets.setdefault(name, []).append(as_left(matrix))
+
     for s in range(spans):
         partners = [s ^ x for x in range(1, spans)]
-        send_first.append(np.concatenate([first[t, s] for t in partners], axis=0))
-        send_joint.append(np.concatenate([joint[t, s] for t in partners], axis=0))
-        own = onward[s][:, s * slab : (s + 1) * slab]
-        apply_first.append(
-            np.block(
-                [
-                    [block(s, s)] + [block(s, t) @ first[s, t].T for t in partners],
-                    [np.zeros_like(own)] + [carried[s][t] @ first[s, t].T for t in partners],
-                ]
-            )
-        )
-        apply_joint.append(
-            np.block(
-                [
-                    [block(s, s)] + [block(s, t) @ joint[s, t].T for t in partners],
-                    [own] + [onward[s][:, t * slab : (t + 1) * slab] @ joint[s, t].T for t in partners],
-                ]
-            )
-        )
-        apply_carried.append(np.concatenate([block(s, s), left[s]], axis=1))
-    stack = lambda parts: np.stack(parts).astype(np.float32)
+        cut = lambda t: slice(t * slab, (t + 1) * slab)
+        firsts = [np.concatenate([block(s, t), carried[s][t]], axis=0) @ first[s, t].T for t in partners]
+        joints = [np.concatenate([block(s, t), onward[s][:, cut(t)]], axis=0) @ joint[s, t].T for t in partners]
+        for half in range(2):
+            add("send_half%d" % half, folded([first[t, s] for t in partners], half, 0))
+            add("far_half%d" % half, folded(firsts, half, 1))
+        add("send_rows", folded([first[t, s] for t in partners], 0, 0))
+        add("send_joint", np.concatenate([joint[t, s] for t in partners], axis=0))
+        add("far_joint", np.concatenate(joints, axis=1))
+        add("local", np.concatenate([block(s, s), onward[s][:, cut(s)]], axis=0))
+        add("onward", np.concatenate([block(s, s), left[s]], axis=1))
     return dict(
-        ranks=ranks,
-        send_first=stack(send_first),
-        send_joint=stack(send_joint),
-        apply_first=stack(apply_first),
-        apply_joint=stack(apply_joint),
-        apply_carried=stack(apply_carried),
-    )
-
-
-def product(left, right):
-    return jnp.dot(left, right, precision=lax.Precision.HIGHEST, preferred_element_type=jnp.float32)
+        ranks=ranks, joint_ranks=joint_ranks, sets={name: np.stack(parts) for name, parts in sets.items()}
+    )
+
+
+def split(values):
+    high = values.astype(jnp.bfloat16)
+    return high, (values - high.astype(jnp.float32)).astype(jnp.bfloat16)
+
+
+def left_product(left, values):
+    short = left.shape[1] // 3 - values.shape[0]
+    if short:
+        values = jnp.concatenate([values, jnp.zeros((short, values.shape[1]), jnp.float32)], axis=0)
+    high, low = split(values)
+    return jnp.dot(left, jnp.concatenate([high, low, high], axis=0), preferred_element_type=jnp.float32)
+
+
+def right_product(values, right):
+    high, low = split(values)
+    return jnp.dot(jnp.concatenate([high, low, high], axis=1), right, preferred_element_type=jnp.float32)
 
 
 def low_half():
@@ -143,27 +182,30 @@
         out[...] = take_face(near, faces, side)
 
 
-def prepare_kernel(sizes, total, pipe, matrix, field, *refs):
-    count = len(sizes)
+def prepare_kernel(count, total, pipe, matrix, field, *refs):
     stacks, (mask, spread, state, moments), outs = refs[:count], refs[count : count + 4], refs[count + 4 : 2 * count + 4]
-    (sems,) = refs[2 * count + 4 :]
+    holes, block_matrix, values, sems = refs[2 * count + 4 :]
     where = lax.axis_index("hgt")
-    got = load([(stack.at[where], out) for stack, out in zip(stacks, outs)], sems)
+    pairs = [(matrix, block_matrix), (pipe, holes), (field, values)]
+    got = load(pairs + [(stack.at[where], out) for stack, out in zip(stacks, outs)], sems)
+    got[0].wait()
     width = matrix.shape[0]
-    copies = spread.shape[0] // width
-    wide = jnp.concatenate([matrix[...]] * copies, axis=1)
-    tall = jnp.concatenate([wide] * copies, axis=0)
-    row = lax.broadcasted_iota(jnp.int32, spread.shape, 0) // width
-    col = lax.broadcasted_iota(jnp.int32, spread.shape, 1) // width
-    spread[...] = jnp.where(row == col, tall, 0.0)
-    for copy in got:
-        copy.wait()
+    size = spread.shape[1]
+    wide = jnp.concatenate([block_matrix[...]] * (size // width), axis=1)
+    tall = jnp.concatenate([wide] * (size // width), axis=0)
+    row = lax.broadcasted_iota(jnp.int32, tall.shape, 0) // width
+    col = lax.broadcasted_iota(jnp.int32, tall.shape, 1) // width
+    high, low = split(jnp.where(row == col, tall, 0.0))
+    spread[...] = jnp.concatenate([high, high, low], axis=0)
+    got[1].wait()
     block = lax.broadcasted_iota(jnp.int32, mask.shape, 1) // width
     live = block < total[0]
-    mask[...] = jnp.where(live & (pipe[...] == 0), 1.0, 0.0).astype(jnp.float32)
+    mask[...] = jnp.where(live & (holes[...] == 0), 1.0, 0.0).astype(jnp.float32)
+    for copy in got[2:]:
+        copy.wait()
     for piece in chunks(field.shape[1]):
-        state[:, piece] = jnp.where(live[:, piece], field[:, piece], 0.0)
-        moments[:, piece] = product(outs[0][...], state[:, piece])
+        state[:, piece] = jnp.where(live[:, piece], values[:, piece], 0.0)
+        moments[:, piece] = left_product(outs[0][...], state[:, piece])
 
 
 def fill(extended, tile, value):
@@ -188,7 +230,7 @@
 
 def conducted(lookup, conductance, mask, spread, extended, gathered, pieces):
     half = low_half()
-    per = spread.shape[0] // lanes
+    per = spread.shape[1] // lanes
     for piece in pieces:
         start = piece.start // lanes
         for tile in range(start, piece.stop // lanes):
@@ -203,7 +245,7 @@
         for tile in range(start, piece.stop // lanes, per):
             part = slice(tile * lanes, (tile + per) * lanes)
             own = jnp.concatenate([extended[0, tile + i] for i in range(per)], axis=1)
-            moved.append(own + mask[:, part] * product(gathered[:, part], spread[...]))
+            moved.append(own + mask[:, part] * right_product(gathered[:, part], spread[...]))
         yield piece, jnp.concatenate(moved, axis=1)
 
 
@@ -218,90 +260,118 @@
     return jnp.concatenate([ref[:, piece] for ref in refs], axis=0)
 
 
+def folded_views(refs, piece, nodes):
+    half = piece.start // (nodes // 2)
+    heads = [(ref, piece) for ref in refs if ref.shape[1] >= nodes]
+    tails = []
+    for ref in refs:
+        start = (nodes if ref.shape[1] >= nodes else 0) + piece.start - half * (nodes // 2)
+        if ref.shape[1] != nodes:
+            tails.append((ref, slice(start, start + piece.stop - piece.start)))
+    return half, heads, tails
+
+
+def store_folded(moved, refs, piece, nodes):
+    half, heads, tails = folded_views(refs, piece, nodes)
+    for i, (ref, part) in enumerate(heads + tails):
+        value = moved[8 * i : 8 * i + 8]
+        ref[:, part] = ref[:, part] + value if half and i >= len(heads) else value
+
+
+def load_folded(refs, piece, nodes):
+    half, heads, tails = folded_views(refs, piece, nodes)
+    return half, jnp.concatenate([ref[:, part] for ref, part in heads + tails], axis=0)
+
+
 def moments_kernel(lookup, conductance, moments, first, second, mask, spread, send, *refs):
     outs, (table, weight, extended, gathered, sems) = refs[:-5], refs[-5:]
+    nodes = moments.shape[1]
     got = load([(lookup, table), (conductance, weight)], sems)
     fill_own(extended, moments)
-    fill_rim(extended, product(send[...], first[...]), product(send[...], second[...]))
+    fill_rim(extended, left_product(send[...], first[...]), left_product(send[...], second[...]))
     for copy in got:
         copy.wait()
-    for piece, values in conducted(table, weight, mask, spread, extended, gathered, chunks(moments.shape[1])):
-        store_rows(values, outs, piece)
-
-
-def first_kernel(lookup, conductance, field, first, second, mask, spread, apply, out, slope, *scratch):
+    whole = 8 * sum(out.shape[1] >= nodes for out in outs)
+    for piece, values in conducted(table, weight, mask, spread, extended, gathered, chunks(nodes)):
+        if piece.start >= nodes // 2:
+            tails = [pltpu.roll(values[i : i + 8], 4, 0) for i in range(whole, values.shape[0], 8)]
+            values = jnp.concatenate([values[:whole]] + tails, axis=0)
+        store_folded(values, outs, piece, nodes)
+
+
+def first_kernel(lookup, conductance, field, first, second, mask, spread, local, out, slope, *scratch):
     table, weight, extended, gathered, sems = scratch
+    slab = field.shape[0]
     got = load([(lookup, table), (conductance, weight)], sems)
     fill_own(extended, field)
     fill_rim(extended, first, second)
     for copy in got:
         copy.wait()
-    local = apply[: field.shape[0], : field.shape[0]]
     for piece, values in conducted(table, weight, mask, spread, extended, gathered, chunks(field.shape[1])):
         out[:, piece] = values
-        slope[:, piece] = product(local, values)
+        slope[:, piece] = left_product(local[:slab], values)
 
 
 def flux_kernel(spans, slope, *refs):
-    got, (kappa, apply, send), (flux, carried), outs = (
+    got, (kappa, send), fars, (flux, carried), outs = (
         refs[: spans - 1],
-        refs[spans - 1 : spans + 2],
-        refs[spans + 2 : spans + 4],
-        refs[spans + 4 :],
-    )
-    slab = slope.shape[0]
-    weights = apply[:, slab:]
-    for piece in chunks(slope.shape[1]):
-        far = product(weights, stacked(got, piece))
+        refs[spans - 1 : spans + 1],
+        refs[spans + 1 : spans + 3],
+        refs[spans + 3 : spans + 5],
+        refs[spans + 5 :],
+    )
+    slab, nodes = slope.shape
+    for piece in chunks(nodes):
+        half, rows = load_folded(got, piece, nodes)
+        far = left_product(fars[half][...], rows)
         carried[:, piece] = far[slab:]
         value = kappa[:, piece] * (slope[:, piece] + far[:slab])
         flux[:, piece] = value
-        store_rows(product(send[...], value), outs, piece)
-
-
-def local_kernel(field, carried, flux, mask, apply, out):
+        store_rows(left_product(send[...], value), outs, piece)
+
+
+def local_kernel(field, carried, flux, mask, local, out):
     slab = field.shape[0]
-    weights = apply[:, :slab]
     for piece in chunks(field.shape[1]):
-        step = axial_step * mask[:, piece] * product(weights, flux[:, piece])
+        step = axial_step * mask[:, piece] * left_product(local[...], flux[:, piece])
         out[:slab, piece] = field[:, piece] + step[:slab]
         out[slab:, piece] = carried[:, piece] + step[slab:]
 
 
-def rim_kernel(spans, exported, base, mask, apply, *refs):
+def rim_kernel(spans, exported, base, mask, far, *refs):
     got, (first, second, faces, sems) = refs[: spans - 1], refs[spans - 1 :]
     (copy,) = load([(exported, faces)], sems)
     copy.wait()
-    weights = apply[:, apply.shape[1] - sum(ref.shape[0] for ref in got) :]
     for side, out in zip(sides(), (first, second)):
         rows = jnp.concatenate([take_face(ref, faces, side) for ref in got], axis=0)
-        out[...] = take_face(base, faces, side) + axial_step * take_face(mask, faces, side) * product(weights, rows)
-
-
-def close_kernel(spans, base, mask, apply, onward, *refs):
+        out[...] = take_face(base, faces, side) + axial_step * take_face(mask, faces, side) * left_product(far[...], rows)
+
+
+def close_kernel(spans, base, mask, far, onward, *refs):
     got, (out, slope) = refs[: spans - 1], refs[spans - 1 :]
     slab = out.shape[0]
-    weights = apply[:, slab:]
     for piece in chunks(base.shape[1]):
-        values = base[:, piece] + axial_step * mask[:, piece] * product(weights, stacked(got, piece))
+        values = base[:, piece] + axial_step * mask[:, piece] * left_product(far[...], stacked(got, piece))
         out[:, piece] = values[:slab]
-        slope[:, piece] = product(onward[...], values)
-
-
-def second_kernel(lookup, conductance, slope, first, second, mask, spread, kappa, onward, send, flux, *refs):
-    outs, (table, weight, extended, gathered, sems) = refs[:-5], refs[-5:]
+        slope[:, piece] = left_product(onward[...], values)
+
+
+def second_kernel(lookup, conductance, slope, first, second, mask, spread, kappa, onward, *refs):
+    sends, flux, outs, (table, weight, extended, gathered, sems) = refs[:2], refs[2], refs[3:-5], refs[-5:]
+    nodes = slope.shape[1]
     got = load([(lookup, table), (conductance, weight)], sems)
     fill_own(extended, slope)
-    fill_rim(extended, product(onward[...], first[...]), product(onward[...], second[...]))
+    fill_rim(extended, left_product(onward[...], first[...]), left_product(onward[...], second[...]))
     for copy in got:
         copy.wait()
-    for piece, values in conducted(table, weight, mask, spread, extended, gathered, chunks(slope.shape[1])):
+    for piece, values in conducted(table, weight, mask, spread, extended, gathered, chunks(nodes)):
         value = kappa[:, piece] * values
         flux[:, piece] = value
-        store_rows(product(send[...], value), outs, piece)
-
-
-def rest_kernel(lookup, conductance, field, flux, first, second, mask, spread, apply, out, *scratch):
+        half = piece.start // (nodes // 2)
+        store_folded(left_product(sends[half][...], value), outs, piece, nodes)
+
+
+def rest_kernel(lookup, conductance, field, flux, first, second, mask, spread, local, out, *scratch):
     table, weight, extended, gathered, sems = scratch
     slab = field.shape[0]
     got = load([(lookup, table), (conductance, weight)], sems)
@@ -309,35 +379,36 @@
     fill_rim(extended, first[:slab], second[:slab])
     for copy in got:
         copy.wait()
-    local = apply[:slab, :slab]
     for piece, values in conducted(table, weight, mask, spread, extended, gathered, chunks(field.shape[1])):
-        out[:, piece] = values + axial_step * mask[:, piece] * product(local, flux[:, piece])
-
-
-def last_kernel(spans, base, mask, apply, *refs):
-    got, (out,) = refs[: spans - 1], refs[spans - 1 :]
-    slab = base.shape[0]
-    weights = apply[:slab, slab:]
-    for piece in chunks(base.shape[1]):
-        out[:, piece] = base[:, piece] + axial_step * mask[:, piece] * product(weights, stacked(got, piece))
+        out[:, piece] = values + axial_step * mask[:, piece] * left_product(local[:slab], flux[:, piece])
+
+
+def last_kernel(spans, base, mask, *refs):
+    fars, got, (out,) = refs[:2], refs[2 : spans + 1], refs[spans + 1 :]
+    slab, nodes = base.shape
+    for piece in chunks(nodes):
+        half, rows = load_folded(got, piece, nodes)
+        out[:, piece] = base[:, piece] + axial_step * mask[:, piece] * left_product(fars[half][:slab], rows)
 
 
 def in_place(array):
     return pltpu.with_memory_space_constraint(array, pltpu.HBM)
 
 
-def call(kernel, far, near, shapes, scratch=(), flops=0, name=None):
-    size = sum(4 * math.prod(shape) for shape in shapes) + sum(4 * a.size for a in near)
+def call(kernel, far, near, outs, scratch=(), flops=0, name=None, scalars=()):
+    outs = [out if isinstance(out, jax.ShapeDtypeStruct) else jax.ShapeDtypeStruct(out, jnp.float32) for out in outs]
+    size = sum(4 * array.size for array in [*near, *outs])
+    spaces = [(scalars, pltpu.SMEM), (far, pltpu.HBM), (near, pltpu.VMEM)]
     return pl.pallas_call(
         kernel,
-        in_specs=[pl.BlockSpec(memory_space=pltpu.HBM)] * len(far) + [pl.BlockSpec(memory_space=pltpu.VMEM)] * len(near),
-        out_specs=[pl.BlockSpec(memory_space=pltpu.VMEM)] * len(shapes),
-        out_shape=[jax.ShapeDtypeStruct(shape, jnp.float32) for shape in shapes],
+        in_specs=[pl.BlockSpec(memory_space=space) for arrays, space in spaces for _ in arrays],
+        out_specs=[pl.BlockSpec(memory_space=pltpu.VMEM)] * len(outs),
+        out_shape=outs,
         scratch_shapes=list(scratch),
         compiler_params=pltpu.CompilerParams(vmem_limit_bytes=24 * 2**20),
         cost_estimate=pl.CostEstimate(flops=flops, bytes_accessed=size, transcendentals=0),
         name=name,
-    )(*[in_place(array) for array in far], *near)
+    )(*scalars, *[in_place(array) for array in far], *near)
 
 
 def trade_faces(first, second):
@@ -354,15 +425,14 @@
 def slab_body(factors, field, kappa, lookup, conductance, exported, totals, pipe, matrix):
     slab, nodes = field.shape
     spans = lax.axis_size("hgt")
-    ranks = factors["ranks"]
-    rows = sum(ranks)
     faces = exported.shape[1:]
     rim = faces[1] * matrix.shape[0]
     tables = [lookup.T, conductance.T]
     exported = exported.reshape(faces)
     tall = slab + carried_rows
     tiles = (nodes + 2 * rim) // lanes + 1
-    sent = [(rank, nodes) for rank in ranks]
+    sent = [(8, rank // 8 * nodes + (rank % 8 > 0) * nodes // 2) for rank in factors["ranks"]]
+    sent_joint = [(rank, nodes) for rank in factors["joint_ranks"]]
     whole = (slab, nodes)
     work = 2 * nodes * slab * slab
 
@@ -385,61 +455,72 @@
         name="faces",
     )
     left, right = trade_faces(first, second)
-    stacks = [factors[key] for key in ("send_first", "send_joint", "apply_first", "apply_joint", "apply_carried")]
-    sizes = [stack.shape[1:] for stack in stacks]
-    mask, spread, state, moments, send_first, send_joint, apply_first, apply_joint, onward = pl.pallas_call(
-        functools.partial(prepare_kernel, sizes),
-        in_specs=[pl.BlockSpec(memory_space=pltpu.SMEM)]
-        + [pl.BlockSpec(memory_space=pltpu.VMEM)] * 3
-        + [pl.BlockSpec(memory_space=pltpu.HBM)] * len(stacks),
-        out_specs=[pl.BlockSpec(memory_space=pltpu.VMEM)] * (4 + len(stacks)),
-        out_shape=[
-            jax.ShapeDtypeStruct(shape, jnp.float32)
-            for shape in [(1, nodes), (2 * lanes, 2 * lanes), whole, (rows, nodes)] + sizes
+    names = ["send_rows"] + sorted(name for name in factors["sets"] if name != "send_rows")
+    stacks = [jnp.asarray(factors["sets"][name]) for name in names]
+    height = stacks[0].shape[1]
+    spread = jax.ShapeDtypeStruct((6 * lanes, 2 * lanes), jnp.bfloat16)
+    mask, spread, state, moments, *own = call(
+        functools.partial(prepare_kernel, len(stacks)),
+        [pipe.reshape(1, nodes), matrix, field, *stacks],
+        [],
+        [(1, nodes), spread, whole, (height, nodes)]
+        + [jax.ShapeDtypeStruct(stack.shape[1:], jnp.bfloat16) for stack in stacks],
+        [
+            pltpu.VMEM((1, nodes), jnp.int32),
+            pltpu.VMEM(matrix.shape, jnp.float32),
+            pltpu.VMEM(whole, jnp.float32),
+            pltpu.SemaphoreType.DMA((3 + len(stacks),)),
         ],
-        scratch_shapes=[pltpu.SemaphoreType.DMA((len(stacks),))],
-        compiler_params=pltpu.CompilerParams(vmem_limit_bytes=24 * 2**20),
-        cost_estimate=pl.CostEstimate(flops=work, bytes_accessed=4 * slab * nodes, transcendentals=0),
-        name="prepare",
-    )(totals, pipe.reshape(1, nodes), matrix, field, *[in_place(stack) for stack in stacks])
+        work,
+        "prepare",
+        [totals],
+    )
+    own = dict(zip(names, own))
+    sends = [own["send_half0"], own["send_half1"]]
+    fars = [own["far_half0"], own["far_half1"]]
     parts = call(
-        moments_kernel, tables, [moments, left, right, mask, spread, send_first], sent, conduct_scratch(rows), name="moments"
+        moments_kernel, tables, [moments, left, right, mask, spread, own["send_rows"]], sent, conduct_scratch(height), name="moments"
     )
     parts = trade_slabs(parts)
     state, slope = call(
         first_kernel,
         tables,
-        [state, left, right, mask, spread, apply_first],
+        [state, left, right, mask, spread, own["local"]],
         [whole, whole],
         conduct_scratch(slab),
         2 * work,
-        name="first",
+        "first",
     )
     flux, carried, *joint = call(
         functools.partial(flux_kernel, spans),
         [],
-        [slope, *parts, kappa, apply_first, send_joint],
-        [whole, (carried_rows, nodes)] + sent,
+        [slope, *parts, kappa, own["send_joint"], *fars],
+        [whole, (carried_rows, nodes)] + sent_joint,
         name="flux",
     )
     joint = trade_slabs(joint)
-    (base,) = call(local_kernel, [], [state, carried, flux, mask, apply_joint], [(tall, nodes)], flops=work, name="local")
+    (base,) = call(local_kernel, [], [state, carried, flux, mask, own["local"]], [(tall, nodes)], flops=work, name="local")
     first, second = call(
         functools.partial(rim_kernel, spans),
         [exported],
-        [base, mask, apply_joint, *joint],
+        [base, mask, own["far_joint"], *joint],
         [(tall, rim)] * 2,
         [face_scratch, pltpu.SemaphoreType.DMA((1,))],
         name="rim",
     )
     left, right = trade_faces(first, second)
     state, slope = call(
-        functools.partial(close_kernel, spans), [], [base, mask, apply_joint, onward, *joint], [whole, whole], flops=work, name="close"
+        functools.partial(close_kernel, spans),
+        [],
+        [base, mask, own["far_joint"], own["onward"], *joint],
+        [whole, whole],
+        flops=work,
+        name="close",
     )
     flux, *parts = call(
         second_kernel,
         tables,
-        [slope, left, right, mask, spread, kappa, onward, send_first],
+        [slope, left, right, mask, spread, kappa, own["onward"], *sends],
         [whole] + sent,
         conduct_scratch(slab),
         name="second",
@@ -448,13 +529,13 @@
     (base,) = call(
         rest_kernel,
         tables,
-        [state, flux, left, right, mask, spread, apply_first],
+        [state, flux, left, right, mask, spread, own["local"]],
         [whole],
         conduct_scratch(slab),
         2 * work,
-        name="rest",
-    )
-    (state,) = call(functools.partial(last_kernel, spans), [], [base, mask, apply_first, *parts], [whole], name="last")
+        "rest",
+    )
+    (state,) = call(functools.partial(last_kernel, spans), [], [base, mask, *fars, *parts], [whole], name="last")
     return state
 
 

time: 64.3 us -> 52.9 us (0.82)
  Pallas kernels: 30.4 us -> 21.8 us
  waiting for transfers between devices: 14.6 us -> 12.3 us
  local copies, waits for them, and re-layouts: 1.46 us -> 0.01 us
  starting transfers between devices: 16.6 us -> 17.6 us
    pallas_call x11, Pallas kernels: 30.4 us -> 21.8 us  [call(): pl.pallas_call(kernel, in_specs=[pl.BlockSpec(memory_space=space) for arr...]
    ppermute x9, waiting for transfers between devices: 12.8 us -> 9.12 us  [trade_slabs(): lax.ppermute(part, 'hgt', [(i, i ^ x) for i in range(count)])]
    unnamed x8 -> x2, local copies, waits for them, and re-layouts: 1.46 us -> 0.01 us
    ppermute x2, waiting for transfers between devices: 1.85 us -> 3.2 us  [trade_faces(): lax.ppermute(second, 'xs', swap(1))]
  transfers between devices with their start and end apart: 13 -> 13, of which waited for: 4 -> 4; matrix products, arithmetic and copies ran while one was open for 0% -> 0% of each run, Pallas kernels for 25% -> 21%
where the time goes in v1:
time: 52.9 us; the launch traced here: 52.5 us
  Pallas kernels  21.8 us (41%)
  starting transfers between devices  17.6 us (33%)
  waiting for transfers between devices  12.3 us (23%)
  between operations  0.79 us (1%)
    pallas_call x11, Pallas kernels, call(): pl.pallas_call(kernel, in_specs=[pl.BlockSpec(memory_space=space) for arr...  21.8 us
    ppermute x9, starting transfers between devices, trade_slabs(): lax.ppermute(part, 'hgt', [(i, i ^ x) for i in range(count)])  9.82 us
    ppermute x9, waiting for transfers between devices, trade_slabs(): lax.ppermute(part, 'hgt', [(i, i ^ x) for i in range(count)])  9.12 us
    ppermute x2, starting transfers between devices, trade_faces(): lax.ppermute(second, 'xs', swap(1))  6.55 us
    ppermute x2, waiting for transfers between devices, trade_faces(): lax.ppermute(second, 'xs', swap(1))  3.2 us
    ppermute x2, starting transfers between devices, trade_faces(): lax.ppermute(first, 'xs', swap(0))  1.23 us
  transfers between devices with their start and end apart: 13, of which 4 were waited for; matrix products, arithmetic and copies ran while one was open for 0% of the time, Pallas kernels for 21%

profile of v1, /device:TPU:1, one launch (start us, length us, event | category | flops | bytes accessed | tf_op | source)
XLA Modules:
  0.0 52.5 jit_solution(1747240131450599556)
XLA Ops:
  0.0 1.3 %faces.1 = (f32[128,256]{1,0:T(8,128)S(1)}, f32[128,256]{1,0:T(8,128)S(1)}) custom-call(s32[2,4]{1,0:T(2,128)} %bitcast.13, f32[128,2048]{1,0:T(8,128)} %field.3), custom_call_target="tpu_custom_call" | custom-call | bytes 262144 | tf_op jit(solution)/shard_map/faces/pallas_call | solution.py:402
  1.3 0.1 collective-permute-start
  1.4 4.5 %collective-permute-start.1 = (f32[128,256]{1,0:T(8,128)S(1)}, f32[128,256]{1,0:T(8,128)S(1)}, u32[]{:S(2)}, u32[]{:S(2)}) collective-permute-start(f32[128,256]{1,0:T(8,128)S(1)} %get-tuple-element.40), channel_id=1, source_target_pairs={{1,2},{2,1},{5,6},{6,5},{9,10},{10,9},{13,14},{14,13},{17,18},{18,... | collective-permute-start | bytes 393224 | tf_op jit(solution)/shard_map/ppermute | solution.py:417
  6.5 2.1 %prepare.1 = (f32[1,2048]{1,0:T(1,128)S(1)}, bf16[768,256]{1,0:T(8,128)(2,1)S(1)}, f32[128,2048]{1,0:T(8,128)S(1)}, f32[40,2048]{1,0:T(8,128)S(1)}, bf16[40,384]...) custom-call(s32[1]{0:T(128)S(6)} %copy.18.total, ...), custom_call_target="tpu_custom_call" | custom-call | flops 67108864 | bytes 3158528 | tf_op jit(solution)/shard_map/prepare/pallas_call | solution.py:402
  8.6 0.0 collective-permute-done.first
  8.6 0.0 collective-permute-done.1.second
  8.6 0.0 copy-start
  8.6 2.4 %moments.1 = (f32[8,3072]{1,0:T(8,128)S(1)}, f32[8,1024]{1,0:T(8,128)S(1)}, f32[8,3072]{1,0:T(8,128)S(1)}) custom-call(s32[6,32]{1,0:T(8,128)} %bitcast.4, f32[6,32]{1,0:T(8,128)} %bitcast.8, f32[40,2048]{1,0:T(8,128)S(1)} %get-tuple-element.46.moments, f32[128,256]{1,0:T(8,128)S(1)} %collective-permute-done.first, ...), custom_call_target="tpu_custom_call" | custom-call | bytes 1675264 | tf_op jit(solution)/shard_map/moments/pallas_call | solution.py:402
  11.0 1.9 %collective-permute-start.2 = (f32[8,3072]{1,0:T(8,128)S(1)}, f32[8,3072]{1,0:T(8,128)S(1)}, u32[]{:S(2)}, u32[]{:S(2)}) collective-permute-start(f32[8,3072]{1,0:T(8,128)S(1)} %get-tuple-element.48), channel_id=1, source_target_pairs={{0,4},{4,0},{8,12},{12,8},{1,5},{5,1},{9,13},{13,9},{2,6},{6,2},{1... | collective-permute-start | bytes 294920 | tf_op jit(solution)/shard_map/ppermute | solution.py:422
  12.9 2.2 %collective-permute-start.4 = (f32[8,3072]{1,0:T(8,128)S(1)}, f32[8,3072]{1,0:T(8,128)S(1)}, u32[]{:S(2)}, u32[]{:S(2)}) collective-permute-start(f32[8,3072]{1,0:T(8,128)S(1)} %get-tuple-element.50), channel_id=1, source_target_pairs={{0,12},{4,8},{8,4},{12,0},{1,13},{5,9},{9,5},{13,1},{2,14},{6,10},... | collective-permute-start | bytes 294920 | tf_op jit(solution)/shard_map/ppermute | solution.py:422
  15.1 0.1 collective-permute-start.3
  15.2 3.9 %first.1 = (f32[128,2048]{1,0:T(8,128)S(1)}, f32[128,2048]{1,0:T(8,128)S(1)}) custom-call(s32[6,32]{1,0:T(8,128)} %bitcast.5, f32[6,32]{1,0:T(8,128)} %bitcast.9, f32[128,2048]{1,0:T(8,128)S(1)} %get-tuple-element.38.field, f32[128,256]{1,0:T(8,128)S(1)} %collective-permute-done.first, f32[128,256]{1,0:T(8,128)S(1)} %collective-permute-done.1.second, ...), custom_call_target="tpu_custom_call" | custom-call | flops 134217728 | bytes 4435968 | tf_op jit(solution)/shard_map/first/pallas_call | solution.py:402
  19.1 0.5 %collective-permute-done.3.refs_1_ = f32[8,1024]{1,0:T(8,128)S(1)} collective-permute-done((f32[8,1024]{1,0:T(8,128)S(1)}, f32[8,1024]{1,0:T(8,128)S(1)}, u32[]{:S(2)}, u32[]{:S(2)}) %collective-permute-start.3) | collective-permute-done | bytes 32800 | tf_op jit(solution)/shard_map/ppermute | solution.py:422
  19.7 0.0 collective-permute-done.2.refs_0_
  19.7 0.0 collective-permute-done.4.refs_2_
  19.7 0.0 copy-done
  19.7 1.1 %flux.1 = (f32[128,2048]{1,0:T(8,128)S(1)}, f32[24,2048]{1,0:T(8,128)S(1)}, f32[16,2048]{1,0:T(8,128)S(1)}, f32[8,2048]{1,0:T(8,128)S(1)}, f32[16,2048]{1,0:T(8,128)S(1)}) custom-call(f32[128,2048]{1,0:T(8,128)S(1)} %get-tuple-element.45.slope, f32[8,3072]{1,0:T(8,128)S(1)} %collective-permute-done.2.refs_0_, f32[8,1024]{1,0:T(8,128)S(1)} %collective-permute-done.3.refs_1_, ...), custom_call_target="tpu_custom_call" | custom-call | bytes 4135936 | tf_op jit(solution)/shard_map/flux/pallas_call | solution.py:402
  20.7 0.7 %collective-permute-start.5 = (f32[16,2048]{1,0:T(8,128)S(1)}, f32[16,2048]{1,0:T(8,128)S(1)}, u32[]{:S(2)}, u32[]{:S(2)}) collective-permute-start(f32[16,2048]{1,0:T(8,128)S(1)} %get-tuple-element.58), channel_id=1, source_target_pairs={{0,4},{4,0},{8,12},{12,8},{1,5},{5,1},{9,13},{13,9},{2,6},{6,2},{1... | collective-permute-start | bytes 393224 | tf_op jit(solution)/shard_map/ppermute | solution.py:422
  21.5 2.2 %collective-permute-start.7 = (f32[16,2048]{1,0:T(8,128)S(1)}, f32[16,2048]{1,0:T(8,128)S(1)}, u32[]{:S(2)}, u32[]{:S(2)}) collective-permute-start(f32[16,2048]{1,0:T(8,128)S(1)} %get-tuple-element.60), channel_id=1, source_target_pairs={{0,12},{4,8},{8,4},{12,0},{1,13},{5,9},{9,5},{13,1},{2,14},{6,10},... | collective-permute-start | bytes 393224 | tf_op jit(solution)/shard_map/ppermute | solution.py:422
  23.7 0.0 collective-permute-start.6
  23.7 0.5 %local.1.base = f32[152,2048]{1,0:T(8,128)S(1)} custom-call(f32[128,2048]{1,0:T(8,128)S(1)} %get-tuple-element.44.field, f32[24,2048]{1,0:T(8,128)S(1)} %get-tuple-element.54.carried, f32[128,2048]{1,0:T(8,128)S(1)} %get-tuple-element.55.flux, f32[1,2048]{1,0:T(1,128)S(1)} %get-tuple-element.41.mask, bf16[152,384]{1,0:T(8,128)(2,1)S(1)} %get-tuple-element.43.local), custom_call_target="tpu_custom_call" | custom-call | flops 67108864 | bytes 3780608 | tf_op jit(solution)/shard_map/local/pallas_call | solution.py:402
  24.2 8.3 %collective-permute-done.6.refs_1_ = f32[8,2048]{1,0:T(8,128)S(1)} collective-permute-done((f32[8,2048]{1,0:T(8,128)S(1)}, f32[8,2048]{1,0:T(8,128)S(1)}, u32[]{:S(2)}, u32[]{:S(2)}) %collective-permute-start.6) | collective-permute-done | bytes 65568 | tf_op jit(solution)/shard_map/ppermute | solution.py:422
  32.5 0.0 collective-permute-done.5.refs_0_
  32.5 0.0 collective-permute-done.7.refs_2_
  32.5 1.1 %rim.1 = (f32[152,256]{1,0:T(8,128)S(1)}, f32[152,256]{1,0:T(8,128)S(1)}) custom-call(s32[2,4]{1,0:T(2,128)} %bitcast.14, f32[152,2048]{1,0:T(8,128)S(1)} %local.1.base, f32[1,2048]{1,0:T(1,128)S(1)} %get-tuple-element.41.mask, bf16[152,144]{1,0:T(8,128)(2,1)S(1)} %get-tuple-element.56.far, f32[16,2048]{1,0:T(8,128)S(1)} %collective-permute-done.5.refs_0_, ...), custom_call_target="tpu_custom_call" | custom-call | bytes 1979904 | tf_op jit(solution)/shard_map/rim/pallas_call | solution.py:402
  33.6 1.1 %collective-permute-start.8 = (f32[152,256]{1,0:T(8,128)S(1)}, f32[152,256]{1,0:T(8,128)S(1)}, u32[]{:S(2)}, u32[]{:S(2)}) collective-permute-start(f32[152,256]{1,0:T(8,128)S(1)} %get-tuple-element.63), channel_id=1, source_target_pairs={{0,1},{1,0},{2,3},{3,2},{4,5},{5,4},{6,7},{7,6},{8,9},{9,8},{10,11... | collective-permute-start | bytes 466952 | tf_op jit(solution)/shard_map/ppermute | solution.py:417
  34.7 2.1 %collective-permute-start.9 = (f32[152,256]{1,0:T(8,128)S(1)}, f32[152,256]{1,0:T(8,128)S(1)}, u32[]{:S(2)}, u32[]{:S(2)}) collective-permute-start(f32[152,256]{1,0:T(8,128)S(1)} %get-tuple-element.64), channel_id=1, source_target_pairs={{1,2},{2,1},{5,6},{6,5},{9,10},{10,9},{13,14},{14,13},{17,18},{18,... | collective-permute-start | bytes 466952 | tf_op jit(solution)/shard_map/ppermute | solution.py:417
  36.8 1.2 %close.1 = (f32[128,2048]{1,0:T(8,128)S(1)}, f32[128,2048]{1,0:T(8,128)S(1)}) custom-call(f32[152,2048]{1,0:T(8,128)S(1)} %local.1.base, f32[1,2048]{1,0:T(1,128)S(1)} %get-tuple-element.41.mask, bf16[152,144]{1,0:T(8,128)(2,1)S(1)} %get-tuple-element.56.far, bf16[128,480]{1,0:T(8,128)(2,1)S(1)} %get-tuple-element.57.onward, ...), custom_call_target="tpu_custom_call" | custom-call | flops 67108864 | bytes 4011520 | tf_op jit(solution)/shard_map/close/pallas_call | solution.py:402
  38.0 0.0 collective-permute-done.8.first
  38.0 3.2 %collective-permute-done.9.second = f32[152,256]{1,0:T(8,128)S(1)} collective-permute-done((f32[152,256]{1,0:T(8,128)S(1)}, f32[152,256]{1,0:T(8,128)S(1)}, u32[]{:S(2)}, u32[]{:S(2)}) %collective-permute-start.9) | collective-permute-done | bytes 155680 | tf_op jit(solution)/shard_map/ppermute | solution.py:417
  41.2 3.5 %second.1 = (f32[128,2048]{1,0:T(8,128)S(1)}, f32[8,3072]{1,0:T(8,128)S(1)}, f32[8,1024]{1,0:T(8,128)S(1)}, f32[8,3072]{1,0:T(8,128)S(1)}) custom-call(s32[6,32]{1,0:T(8,128)} %bitcast.6, f32[6,32]{1,0:T(8,128)} %bitcast.10, f32[128,2048]{1,0:T(8,128)S(1)} %get-tuple-element.62.slope, f32[152,256]{1,0:T(8,128)S(1)} %collective-permute-done.8.first, ...), custom_call_target="tpu_custom_call" | custom-call | bytes 4849664 | tf_op jit(solution)/shard_map/second/pallas_call | solution.py:402
  44.8 0.1 collective-permute-start.10
  44.9 0.7 %collective-permute-start.12 = (f32[8,3072]{1,0:T(8,128)S(1)}, f32[8,3072]{1,0:T(8,128)S(1)}, u32[]{:S(2)}, u32[]{:S(2)}) collective-permute-start(f32[8,3072]{1,0:T(8,128)S(1)} %get-tuple-element.70), channel_id=1, source_target_pairs={{0,12},{4,8},{8,4},{12,0},{1,13},{5,9},{9,5},{13,1},{2,14},{6,10},... | collective-permute-start | bytes 294920 | tf_op jit(solution)/shard_map/ppermute | solution.py:422
  45.6 1.9 %collective-permute-start.11 = (f32[8,1024]{1,0:T(8,128)S(1)}, f32[8,1024]{1,0:T(8,128)S(1)}, u32[]{:S(2)}, u32[]{:S(2)}) collective-permute-start(f32[8,1024]{1,0:T(8,128)S(1)} %get-tuple-element.69), channel_id=1, source_target_pairs={{0,8},{4,12},{8,0},{12,4},{1,9},{5,13},{9,1},{13,5},{2,10},{6,14},... | collective-permute-start | bytes 98312 | tf_op jit(solution)/shard_map/ppermute | solution.py:422
  47.5 3.4 %rest.1.base = f32[128,2048]{1,0:T(8,128)S(1)} custom-call(s32[6,32]{1,0:T(8,128)} %bitcast.7, f32[6,32]{1,0:T(8,128)} %bitcast.11, f32[128,2048]{1,0:T(8,128)S(1)} %get-tuple-element.61.field, f32[128,2048]{1,0:T(8,128)S(1)} %get-tuple-element.67.flux, f32[152,256]{1,0:T(8,128)S(1)} %collective-permute-done.8.first, ...), custom_call_target="tpu_custom_call" | custom-call | flops 134217728 | bytes 4485120 | tf_op jit(solution)/shard_map/rest/pallas_call | solution.py:402
  50.9 0.3 collective-permute-done.11.refs_3_
  51.2 0.0 collective-permute-done.10.refs_2_
  51.2 0.0 collective-permute-done.12.refs_4_
  51.3 1.3 %last.1 = f32[128,2048]{1,0:T(8,128)} custom-call(f32[128,2048]{1,0:T(8,128)S(1)} %rest.1.base, f32[1,2048]{1,0:T(1,128)S(1)} %get-tuple-element.41.mask, bf16[152,144]{1,0:T(8,128)(2,1)S(1)} %get-tuple-element.52.refs_5_.refs_0_, bf16[152,144]{1,0:T(8,128)(2,1)S(1)} %get-tuple-element.53.refs_6_.refs_1_, f32[8,3072]{1,0:T(8,128)S(1)} %collective-permute-done.10.refs_2_, ...), custom_call_target="tpu_custom_call" | custom-call | bytes 2509824 | tf_op jit(solution)/shard_map/last/pallas_call | solution.py:402
Async XLA Ops:
  1.3 7.3 %collective-permute-start = (f32[128,256]{1,0:T(8,128)S(1)}, f32[128,256]{1,0:T(8,128)S(1)}, u32[]{:S(2)}, u32[]{:S(2)}) collective-permute-start(f32[128,256]{1,0:T(8,128)S(1)} %get-tuple-element.39), channel_id=1, source_target_pairs={{0,1},{1,0},{2,3},{3,2},{4,5},{5,4},{6,7},{7,6},{8,9},{9,8},{10,11... | collective-permute-start | bytes 393224 | tf_op jit(solution)/shard_map/ppermute | solution.py:417
  1.4 7.2 %collective-permute-start.1 = (f32[128,256]{1,0:T(8,128)S(1)}, f32[128,256]{1,0:T(8,128)S(1)}, u32[]{:S(2)}, u32[]{:S(2)}) collective-permute-start(f32[128,256]{1,0:T(8,128)S(1)} %get-tuple-element.40), channel_id=1, source_target_pairs={{1,2},{2,1},{5,6},{6,5},{9,10},{10,9},{13,14},{14,13},{17,18},{18,... | collective-permute-start | bytes 393224 | tf_op jit(solution)/shard_map/ppermute | solution.py:417
  8.6 11.1 %copy-start = (f32[128,2048]{1,0:T(8,128)S(1)}, f32[128,2048]{1,0:T(8,128)}, u32[]{:S(2)}) copy-start(f32[128,2048]{1,0:T(8,128)} %kappa.1) | copy-start | bytes 3145732
  11.0 8.6 %collective-permute-start.2 = (f32[8,3072]{1,0:T(8,128)S(1)}, f32[8,3072]{1,0:T(8,128)S(1)}, u32[]{:S(2)}, u32[]{:S(2)}) collective-permute-start(f32[8,3072]{1,0:T(8,128)S(1)} %get-tuple-element.48), channel_id=1, source_target_pairs={{0,4},{4,0},{8,12},{12,8},{1,5},{5,1},{9,13},{13,9},{2,6},{6,2},{1... | collective-permute-start | bytes 294920 | tf_op jit(solution)/shard_map/ppermute | solution.py:422
  12.9 6.8 %collective-permute-start.4 = (f32[8,3072]{1,0:T(8,128)S(1)}, f32[8,3072]{1,0:T(8,128)S(1)}, u32[]{:S(2)}, u32[]{:S(2)}) collective-permute-start(f32[8,3072]{1,0:T(8,128)S(1)} %get-tuple-element.50), channel_id=1, source_target_pairs={{0,12},{4,8},{8,4},{12,0},{1,13},{5,9},{9,5},{13,1},{2,14},{6,10},... | collective-permute-start | bytes 294920 | tf_op jit(solution)/shard_map/ppermute | solution.py:422
  15.1 4.6 %collective-permute-start.3 = (f32[8,1024]{1,0:T(8,128)S(1)}, f32[8,1024]{1,0:T(8,128)S(1)}, u32[]{:S(2)}, u32[]{:S(2)}) collective-permute-start(f32[8,1024]{1,0:T(8,128)S(1)} %get-tuple-element.49), channel_id=1, source_target_pairs={{0,8},{4,12},{8,0},{12,4},{1,9},{5,13},{9,1},{13,5},{2,10},{6,14},... | collective-permute-start | bytes 98312 | tf_op jit(solution)/shard_map/ppermute | solution.py:422
  20.7 11.7 %collective-permute-start.5 = (f32[16,2048]{1,0:T(8,128)S(1)}, f32[16,2048]{1,0:T(8,128)S(1)}, u32[]{:S(2)}, u32[]{:S(2)}) collective-permute-start(f32[16,2048]{1,0:T(8,128)S(1)} %get-tuple-element.58), channel_id=1, source_target_pairs={{0,4},{4,0},{8,12},{12,8},{1,5},{5,1},{9,13},{13,9},{2,6},{6,2},{1... | collective-permute-start | bytes 393224 | tf_op jit(solution)/shard_map/ppermute | solution.py:422
  21.5 11.0 %collective-permute-start.7 = (f32[16,2048]{1,0:T(8,128)S(1)}, f32[16,2048]{1,0:T(8,128)S(1)}, u32[]{:S(2)}, u32[]{:S(2)}) collective-permute-start(f32[16,2048]{1,0:T(8,128)S(1)} %get-tuple-element.60), channel_id=1, source_target_pairs={{0,12},{4,8},{8,4},{12,0},{1,13},{5,9},{9,5},{13,1},{2,14},{6,10},... | collective-permute-start | bytes 393224 | tf_op jit(solution)/shard_map/ppermute | solution.py:422
  23.7 8.8 %collective-permute-start.6 = (f32[8,2048]{1,0:T(8,128)S(1)}, f32[8,2048]{1,0:T(8,128)S(1)}, u32[]{:S(2)}, u32[]{:S(2)}) collective-permute-start(f32[8,2048]{1,0:T(8,128)S(1)} %get-tuple-element.59), channel_id=1, source_target_pairs={{0,8},{4,12},{8,0},{12,4},{1,9},{5,13},{9,1},{13,5},{2,10},{6,14},... | collective-permute-start | bytes 196616 | tf_op jit(solution)/shard_map/ppermute | solution.py:422
  33.6 4.4 %collective-permute-start.8 = (f32[152,256]{1,0:T(8,128)S(1)}, f32[152,256]{1,0:T(8,128)S(1)}, u32[]{:S(2)}, u32[]{:S(2)}) collective-permute-start(f32[152,256]{1,0:T(8,128)S(1)} %get-tuple-element.63), channel_id=1, source_target_pairs={{0,1},{1,0},{2,3},{3,2},{4,5},{5,4},{6,7},{7,6},{8,9},{9,8},{10,11... | collective-permute-start | bytes 466952 | tf_op jit(solution)/shard_map/ppermute | solution.py:417
  34.7 6.5 %collective-permute-start.9 = (f32[152,256]{1,0:T(8,128)S(1)}, f32[152,256]{1,0:T(8,128)S(1)}, u32[]{:S(2)}, u32[]{:S(2)}) collective-permute-start(f32[152,256]{1,0:T(8,128)S(1)} %get-tuple-element.64), channel_id=1, source_target_pairs={{1,2},{2,1},{5,6},{6,5},{9,10},{10,9},{13,14},{14,13},{17,18},{18,... | collective-permute-start | bytes 466952 | tf_op jit(solution)/shard_map/ppermute | solution.py:417
  44.8 6.5 %collective-permute-start.10 = (f32[8,3072]{1,0:T(8,128)S(1)}, f32[8,3072]{1,0:T(8,128)S(1)}, u32[]{:S(2)}, u32[]{:S(2)}) collective-permute-start(f32[8,3072]{1,0:T(8,128)S(1)} %get-tuple-element.68), channel_id=1, source_target_pairs={{0,4},{4,0},{8,12},{12,8},{1,5},{5,1},{9,13},{13,9},{2,6},{6,2},{1... | collective-permute-start | bytes 294920 | tf_op jit(solution)/shard_map/ppermute | solution.py:422
  44.9 6.4 %collective-permute-start.12 = (f32[8,3072]{1,0:T(8,128)S(1)}, f32[8,3072]{1,0:T(8,128)S(1)}, u32[]{:S(2)}, u32[]{:S(2)}) collective-permute-start(f32[8,3072]{1,0:T(8,128)S(1)} %get-tuple-element.70), channel_id=1, source_target_pairs={{0,12},{4,8},{8,4},{12,0},{1,13},{5,9},{9,5},{13,1},{2,14},{6,10},... | collective-permute-start | bytes 294920 | tf_op jit(solution)/shard_map/ppermute | solution.py:422
  45.6 5.7 %collective-permute-start.11 = (f32[8,1024]{1,0:T(8,128)S(1)}, f32[8,1024]{1,0:T(8,128)S(1)}, u32[]{:S(2)}, u32[]{:S(2)}) collective-permute-start(f32[8,1024]{1,0:T(8,128)S(1)} %get-tuple-element.69), channel_id=1, source_target_pairs={{0,8},{4,12},{8,0},{12,4},{1,9},{5,13},{9,1},{13,5},{2,10},{6,14},... | collective-permute-start | bytes 98312 | tf_op jit(solution)/shard_map/ppermute | solution.py:422

commit v2 on v1

--- a/solution.py
+++ b/solution.py
@@ -72,6 +72,10 @@
     return np.concatenate([head for head, _ in pairs] + [tail for _, tail in pairs], axis=axis)
 
 
+def turns(spans):
+    return list(range(spans - 1, 0, -1))
+
+
 @functools.lru_cache(maxsize=None)
 def slab_factors(order, spans):
     slab = order // spans
@@ -79,9 +83,9 @@
         return None
     full = cheb_exact(order)
     block = lambda s, t: full[s * slab : (s + 1) * slab, t * slab : (t + 1) * slab]
-    near = [any(abs(s - (s ^ x)) == 1 for s in range(spans)) for x in range(1, spans)]
-    ranks = [near_rows if close else far_rows for close in near]
-    joint_ranks = [joint_near_rows if close else joint_far_rows for close in near]
+    near = {x: any(abs(s - (s ^ x)) == 1 for s in range(spans)) for x in turns(spans)}
+    ranks = {x: near_rows if close else far_rows for x, close in near.items()}
+    joint_ranks = {x: joint_near_rows if close else joint_far_rows for x, close in near.items()}
     first, joint = {}, {}
     carried, onward, left = {}, {}, {}
     for s in range(spans):
@@ -92,9 +96,9 @@
         carried[s] = {t: rows[:, i * slab : (i + 1) * slab] for i, t in enumerate(others)}
         onward[s] = sum(carried[s][t] @ full[t * slab : (t + 1) * slab] for t in others)
         for t in others:
-            first[s, t] = row_basis(block(s, t), ranks[(s ^ t) - 1])
+            first[s, t] = row_basis(block(s, t), ranks[s ^ t])
             joint[s, t] = row_basis(
-                np.concatenate([block(s, t), onward[s][:, t * slab : (t + 1) * slab]], axis=0), joint_ranks[(s ^ t) - 1]
+                np.concatenate([block(s, t), onward[s][:, t * slab : (t + 1) * slab]], axis=0), joint_ranks[s ^ t]
             )
     sets = {}
 
@@ -102,7 +106,7 @@
         sets.setdefault(name, []).append(as_left(matrix))
 
     for s in range(spans):
-        partners = [s ^ x for x in range(1, spans)]
+        partners = [s ^ x for x in turns(spans)]
         cut = lambda t: slice(t * slab, (t + 1) * slab)
         firsts = [np.concatenate([block(s, t), carried[s][t]], axis=0) @ first[s, t].T for t in partners]
         joints = [np.concatenate([block(s, t), onward[s][:, cut(t)]], axis=0) @ joint[s, t].T for t in partners]
@@ -115,7 +119,7 @@
         add("local", np.concatenate([block(s, s), onward[s][:, cut(s)]], axis=0))
         add("onward", np.concatenate([block(s, s), left[s]], axis=1))
     return dict(
-        ranks=ranks, joint_ranks=joint_ranks, sets={name: np.stack(parts) for name, parts in sets.items()}
+        ranks=list(ranks.values()), joint_ranks=list(joint_ranks.values()), sets={name: np.stack(parts) for name, parts in sets.items()}
     )
 
 
@@ -158,7 +162,7 @@
 
 
 def sides():
-    first = 1 - lax.axis_index("xs") % 2
+    first = lax.axis_index("xs") % 2
     return first, 1 - first
 
 
@@ -330,12 +334,36 @@
         store_rows(left_product(send[...], value), outs, piece)
 
 
-def local_kernel(field, carried, flux, mask, local, out):
+def rim_matrix(table, weight, mask, block_matrix, own_blocks, high, low):
+    width = block_matrix.shape[0]
+    slots, blocks = table.shape
+    for piece in chunks(mask.shape[1]):
+        block = (piece.start + lax.broadcasted_iota(jnp.int32, (blocks, piece.stop - piece.start), 1)) // width
+        pick = jnp.where(block == lax.broadcasted_iota(jnp.int32, block.shape, 0), 1.0, 0.0)
+        spread_out = lambda rows: jnp.dot(
+            rows, pick, precision=lax.Precision.HIGHEST, preferred_element_type=jnp.float32
+        )
+        index = spread_out(table[...].astype(jnp.float32))
+        value = spread_out(weight[...]) * mask[:, piece]
+        wide = jnp.concatenate([block_matrix[...]] * (block.shape[1] // width), axis=1)
+        for received in range(high.shape[0] // width):
+            hit = jnp.where(jnp.abs(index - (own_blocks + received)) < 0.5, value, 0.0)
+            gain = jnp.sum(hit[1:slots], axis=0, keepdims=True)
+            rows = slice(received * width, (received + 1) * width)
+            high[rows, piece], low[rows, piece] = split(wide * gain)
+
+
+def local_kernel(lookup, conductance, matrix, field, carried, flux, mask, local, out, high, low, *scratch):
+    table, weight, block_matrix, sems = scratch
     slab = field.shape[0]
+    got = load([(lookup, table), (conductance, weight), (matrix, block_matrix)], sems)
     for piece in chunks(field.shape[1]):
         step = axial_step * mask[:, piece] * left_product(local[...], flux[:, piece])
         out[:slab, piece] = field[:, piece] + step[:slab]
         out[slab:, piece] = carried[:, piece] + step[slab:]
+    for copy in got:
+        copy.wait()
+    rim_matrix(table, weight, mask, block_matrix, field.shape[1] // block_matrix.shape[0], high, low)
 
 
 def rim_kernel(spans, exported, base, mask, far, *refs):
@@ -347,25 +375,40 @@
         out[...] = take_face(base, faces, side) + axial_step * take_face(mask, faces, side) * left_product(far[...], rows)
 
 
-def close_kernel(spans, base, mask, far, onward, *refs):
-    got, (out, slope) = refs[: spans - 1], refs[spans - 1 :]
-    slab = out.shape[0]
-    for piece in chunks(base.shape[1]):
+def close_kernel(spans, lookup, conductance, base, mask, spread, far, onward, *refs):
+    got, (out, slope, table, weight, extended, gathered, sems) = refs[: spans - 1], refs[spans - 1 :]
+    slab, nodes = out.shape
+    copies = load([(lookup, table), (conductance, weight)], sems)
+    for piece in chunks(nodes):
         values = base[:, piece] + axial_step * mask[:, piece] * left_product(far[...], stacked(got, piece))
         out[:, piece] = values[:slab]
-        slope[:, piece] = left_product(onward[...], values)
-
-
-def second_kernel(lookup, conductance, slope, first, second, mask, spread, kappa, onward, *refs):
-    sends, flux, outs, (table, weight, extended, gathered, sems) = refs[:2], refs[2], refs[3:-5], refs[-5:]
-    nodes = slope.shape[1]
-    got = load([(lookup, table), (conductance, weight)], sems)
-    fill_own(extended, slope)
-    fill_rim(extended, left_product(onward[...], first[...]), left_product(onward[...], second[...]))
-    for copy in got:
+        own = left_product(onward[...], values)
+        for tile in range(piece.start // lanes, piece.stop // lanes):
+            fill(extended, tile, own[:, tile * lanes - piece.start : (tile + 1) * lanes - piece.start])
+    for tile in range(nodes // lanes, extended.shape[1]):
+        extended[0, tile] = jnp.zeros(extended.shape[2:], jnp.float32)
+        extended[1, tile] = jnp.zeros(extended.shape[2:], jnp.float32)
+    for copy in copies:
         copy.wait()
     for piece, values in conducted(table, weight, mask, spread, extended, gathered, chunks(nodes)):
-        value = kappa[:, piece] * values
+        slope[:, piece] = values
+
+
+def second_kernel(slope, first, second, high, low, kappa, onward, *refs):
+    sends, flux, outs = refs[:2], refs[2], refs[3:]
+    slab, nodes = slope.shape
+    rim = first.shape[1]
+    received = []
+    for side, values in zip(sides(), (first, second)):
+        top, bottom = split(left_product(onward[...], values[...]))
+        received.append((pl.ds(pl.multiple_of(side * rim, rim), rim), top, jnp.concatenate([top, bottom], axis=0)))
+    for piece in chunks(nodes):
+        total = slope[:, piece]
+        for rows, top, both in received:
+            main = jnp.dot(both, high[rows, piece], preferred_element_type=jnp.float32)
+            total = total + (main[:slab] + main[slab:])
+            total = total + jnp.dot(top, low[rows, piece], preferred_element_type=jnp.float32)
+        value = kappa[:, piece] * total
         flux[:, piece] = value
         half = piece.start // (nodes // 2)
         store_folded(left_product(sends[half][...], value), outs, piece, nodes)
@@ -384,25 +427,31 @@
 
 
 def last_kernel(spans, base, mask, *refs):
-    fars, got, (out,) = refs[:2], refs[2 : spans + 1], refs[spans + 1 :]
+    fars, got, (out, values, sems) = refs[:2], refs[2 : spans + 1], refs[spans + 1 :]
     slab, nodes = base.shape
-    for piece in chunks(nodes):
+    copies = []
+    for i, piece in enumerate(chunks(nodes)):
         half, rows = load_folded(got, piece, nodes)
-        out[:, piece] = base[:, piece] + axial_step * mask[:, piece] * left_product(fars[half][:slab], rows)
+        values[:, piece] = base[:, piece] + axial_step * mask[:, piece] * left_product(fars[half][:slab], rows)
+        part = pl.ds(piece.start, piece.stop - piece.start)
+        copies.append(pltpu.make_async_copy(values.at[:, part], out.at[:, part], sems.at[i]))
+        copies[-1].start()
+    for copy in copies:
+        copy.wait()
 
 
 def in_place(array):
     return pltpu.with_memory_space_constraint(array, pltpu.HBM)
 
 
-def call(kernel, far, near, outs, scratch=(), flops=0, name=None, scalars=()):
+def call(kernel, far, near, outs, scratch=(), flops=0, name=None, scalars=(), out_space=pltpu.VMEM):
     outs = [out if isinstance(out, jax.ShapeDtypeStruct) else jax.ShapeDtypeStruct(out, jnp.float32) for out in outs]
     size = sum(4 * array.size for array in [*near, *outs])
     spaces = [(scalars, pltpu.SMEM), (far, pltpu.HBM), (near, pltpu.VMEM)]
     return pl.pallas_call(
         kernel,
         in_specs=[pl.BlockSpec(memory_space=space) for arrays, space in spaces for _ in arrays],
-        out_specs=[pl.BlockSpec(memory_space=pltpu.VMEM)] * len(outs),
+        out_specs=[pl.BlockSpec(memory_space=out_space)] * len(outs),
         out_shape=outs,
         scratch_shapes=list(scratch),
         compiler_params=pltpu.CompilerParams(vmem_limit_bytes=24 * 2**20),
@@ -414,12 +463,12 @@
 def trade_faces(first, second):
     count = lax.axis_size("xs")
     swap = lambda start: [pair for i in range(start, count - 1, 2) for pair in ((i, i + 1), (i + 1, i))]
-    return lax.ppermute(first, "xs", swap(0)), lax.ppermute(second, "xs", swap(1))
+    return lax.ppermute(first, "xs", swap(1)), lax.ppermute(second, "xs", swap(0))
 
 
 def trade_slabs(parts):
     count = lax.axis_size("hgt")
-    return [lax.ppermute(part, "hgt", [(i, i ^ x) for i in range(count)]) for x, part in enumerate(parts, 1)]
+    return [lax.ppermute(part, "hgt", [(i, i ^ x) for i in range(count)]) for x, part in zip(turns(count), parts)]
 
 
 def slab_body(factors, field, kappa, lookup, conductance, exported, totals, pipe, matrix):
@@ -499,7 +548,21 @@
         name="flux",
     )
     joint = trade_slabs(joint)
-    (base,) = call(local_kernel, [], [state, carried, flux, mask, own["local"]], [(tall, nodes)], flops=work, name="local")
+    half_matrix = jax.ShapeDtypeStruct((2 * rim, nodes), jnp.bfloat16)
+    base, high, low = call(
+        local_kernel,
+        [*tables, matrix],
+        [state, carried, flux, mask, own["local"]],
+        [(tall, nodes), half_matrix, half_matrix],
+        [
+            pltpu.VMEM(tables[0].shape, jnp.int32),
+            pltpu.VMEM(tables[1].shape, jnp.float32),
+            pltpu.VMEM(matrix.shape, jnp.float32),
+            pltpu.SemaphoreType.DMA((3,)),
+        ],
+        2 * work,
+        "local",
+    )
     first, second = call(
         functools.partial(rim_kernel, spans),
         [exported],
@@ -511,18 +574,18 @@
     left, right = trade_faces(first, second)
     state, slope = call(
         functools.partial(close_kernel, spans),
-        [],
-        [base, mask, own["far_joint"], own["onward"], *joint],
+        tables,
+        [base, mask, spread, own["far_joint"], own["onward"], *joint],
         [whole, whole],
-        flops=work,
-        name="close",
+        conduct_scratch(slab),
+        2 * work,
+        "close",
     )
     flux, *parts = call(
         second_kernel,
-        tables,
-        [slope, left, right, mask, spread, kappa, own["onward"], *sends],
+        [],
+        [slope, left, right, high, low, kappa, own["onward"], *sends],
         [whole] + sent,
-        conduct_scratch(slab),
         name="second",
     )
     parts = trade_slabs(parts)
@@ -535,7 +598,15 @@
         2 * work,
         "rest",
     )
-    (state,) = call(functools.partial(last_kernel, spans), [], [base, mask, *fars, *parts], [whole], name="last")
+    (state,) = call(
+        functools.partial(last_kernel, spans),
+        [],
+        [base, mask, *fars, *parts],
+        [whole],
+        [pltpu.VMEM(whole, jnp.float32), pltpu.SemaphoreType.DMA((len(chunks(nodes)),))],
+        name="last",
+        out_space=pltpu.HBM,
+    )
     return state
 
 

time: 52.9 us -> 53.1 us (level)
  the two profiles are of different devices: /device:TPU:1 before, /device:TPU:0 now
where the time goes in v2:
time: 53.1 us; the launch traced here: 52.7 us
  Pallas kernels  24 us (45%)
  starting transfers between devices  20.8 us (39%)
  waiting for transfers between devices  6.96 us (13%)
  between operations  0.96 us (2%)
    pallas_call x11, Pallas kernels, call(): pl.pallas_call(kernel, in_specs=[pl.BlockSpec(memory_space=space) for arr...  24 us
    ppermute x9, starting transfers between devices, trade_slabs(): lax.ppermute(part, 'hgt', [(i, i ^ x) for i in range(count)])  13.3 us
    ppermute x9, waiting for transfers between devices, trade_slabs(): lax.ppermute(part, 'hgt', [(i, i ^ x) for i in range(count)])  6.95 us
    ppermute x2, starting transfers between devices, trade_faces(): lax.ppermute(second, 'xs', swap(0))  5.93 us
    ppermute x2, starting transfers between devices, trade_faces(): lax.ppermute(first, 'xs', swap(1))  1.52 us
  transfers between devices with their start and end apart: 13, of which 5 were waited for; matrix products, arithmetic and copies ran while one was open for 0% of the time, Pallas kernels for 28%

profile of v2, /device:TPU:0, one launch (start us, length us, event | category | flops | bytes accessed | tf_op | source)
XLA Modules:
  0.0 52.7 jit_solution(12696902808276000438)
XLA Ops:
  0.0 1.3 %faces.1 = (f32[128,256]{1,0:T(8,128)S(1)}, f32[128,256]{1,0:T(8,128)S(1)}) custom-call(s32[2,4]{1,0:T(2,128)} %bitcast.15, f32[128,2048]{1,0:T(8,128)} %field.3), custom_call_target="tpu_custom_call" | custom-call | bytes 262144 | tf_op jit(solution)/shard_map/faces/pallas_call | solution.py:451
  1.3 0.7 %collective-permute-start = (f32[128,256]{1,0:T(8,128)S(1)}, f32[128,256]{1,0:T(8,128)S(1)}, u32[]{:S(2)}, u32[]{:S(2)}) collective-permute-start(f32[128,256]{1,0:T(8,128)S(1)} %get-tuple-element.42), channel_id=1, source_target_pairs={{1,2},{2,1},{5,6},{6,5},{9,10},{10,9},{13,14},{14,13},{17,18},{18,... | collective-permute-start | bytes 393224 | tf_op jit(solution)/shard_map/ppermute | solution.py:466
  1.9 4.4 %collective-permute-start.1 = (f32[128,256]{1,0:T(8,128)S(1)}, f32[128,256]{1,0:T(8,128)S(1)}, u32[]{:S(2)}, u32[]{:S(2)}) collective-permute-start(f32[128,256]{1,0:T(8,128)S(1)} %get-tuple-element.43), channel_id=1, source_target_pairs={{0,1},{1,0},{2,3},{3,2},{4,5},{5,4},{6,7},{7,6},{8,9},{9,8},{10,11... | collective-permute-start | bytes 393224 | tf_op jit(solution)/shard_map/ppermute | solution.py:466
  7.0 2.1 %prepare.1 = (f32[1,2048]{1,0:T(1,128)S(1)}, bf16[768,256]{1,0:T(8,128)(2,1)S(1)}, f32[128,2048]{1,0:T(8,128)S(1)}, f32[40,2048]{1,0:T(8,128)S(1)}, bf16[40,384]...) custom-call(s32[1]{0:T(128)S(6)} %copy.18.total, ...), custom_call_target="tpu_custom_call" | custom-call | flops 67108864 | bytes 3158528 | tf_op jit(solution)/shard_map/prepare/pallas_call | solution.py:451
  9.0 0.0 copy-start
  9.0 0.0 collective-permute-done.first
  9.0 0.0 collective-permute-done.1.second
  9.1 2.4 %moments.1 = (f32[8,3072]{1,0:T(8,128)S(1)}, f32[8,1024]{1,0:T(8,128)S(1)}, f32[8,3072]{1,0:T(8,128)S(1)}) custom-call(s32[6,32]{1,0:T(8,128)} %bitcast.4, f32[6,32]{1,0:T(8,128)} %bitcast.9, f32[40,2048]{1,0:T(8,128)S(1)} %get-tuple-element.49.moments, f32[128,256]{1,0:T(8,128)S(1)} %collective-permute-done.first, ...), custom_call_target="tpu_custom_call" | custom-call | bytes 1675264 | tf_op jit(solution)/shard_map/moments/pallas_call | solution.py:451
  11.5 3.7 %collective-permute-start.2 = (f32[8,3072]{1,0:T(8,128)S(1)}, f32[8,3072]{1,0:T(8,128)S(1)}, u32[]{:S(2)}, u32[]{:S(2)}) collective-permute-start(f32[8,3072]{1,0:T(8,128)S(1)} %get-tuple-element.51), channel_id=1, source_target_pairs={{0,12},{4,8},{8,4},{12,0},{1,13},{5,9},{9,5},{13,1},{2,14},{6,10},... | collective-permute-start | bytes 294920 | tf_op jit(solution)/shard_map/ppermute | solution.py:471
  15.1 0.0 collective-permute-start.4
  15.1 0.8 %collective-permute-start.3 = (f32[8,1024]{1,0:T(8,128)S(1)}, f32[8,1024]{1,0:T(8,128)S(1)}, u32[]{:S(2)}, u32[]{:S(2)}) collective-permute-start(f32[8,1024]{1,0:T(8,128)S(1)} %get-tuple-element.52), channel_id=1, source_target_pairs={{0,8},{4,12},{8,0},{12,4},{1,9},{5,13},{9,1},{13,5},{2,10},{6,14},... | collective-permute-start | bytes 98312 | tf_op jit(solution)/shard_map/ppermute | solution.py:471
  15.9 3.9 %first.1 = (f32[128,2048]{1,0:T(8,128)S(1)}, f32[128,2048]{1,0:T(8,128)S(1)}) custom-call(s32[6,32]{1,0:T(8,128)} %bitcast.5, f32[6,32]{1,0:T(8,128)} %bitcast.10, f32[128,2048]{1,0:T(8,128)S(1)} %get-tuple-element.41.field, f32[128,256]{1,0:T(8,128)S(1)} %collective-permute-done.first, f32[128,256]{1,0:T(8,128)S(1)} %collective-permute-done.1.second, ...), custom_call_target="tpu_custom_call" | custom-call | flops 134217728 | bytes 4435968 | tf_op jit(solution)/shard_map/first/pallas_call | solution.py:451
  19.8 0.6 %collective-permute-done.3.refs_1_ = f32[8,1024]{1,0:T(8,128)S(1)} collective-permute-done((f32[8,1024]{1,0:T(8,128)S(1)}, f32[8,1024]{1,0:T(8,128)S(1)}, u32[]{:S(2)}, u32[]{:S(2)}) %collective-permute-start.3) | collective-permute-done | bytes 32800 | tf_op jit(solution)/shard_map/ppermute | solution.py:471
  20.4 0.0 collective-permute-done.2.refs_0_
  20.4 0.6 %collective-permute-done.4.refs_2_ = f32[8,3072]{1,0:T(8,128)S(1)} collective-permute-done((f32[8,3072]{1,0:T(8,128)S(1)}, f32[8,3072]{1,0:T(8,128)S(1)}, u32[]{:S(2)}, u32[]{:S(2)}) %collective-permute-start.4) | collective-permute-done | bytes 98336 | tf_op jit(solution)/shard_map/ppermute | solution.py:471
  21.1 0.0 copy-done
  21.1 1.0 %flux.1 = (f32[128,2048]{1,0:T(8,128)S(1)}, f32[24,2048]{1,0:T(8,128)S(1)}, f32[16,2048]{1,0:T(8,128)S(1)}, f32[8,2048]{1,0:T(8,128)S(1)}, f32[16,2048]{1,0:T(8,128)S(1)}) custom-call(f32[128,2048]{1,0:T(8,128)S(1)} %get-tuple-element.48.slope, f32[8,3072]{1,0:T(8,128)S(1)} %collective-permute-done.2.refs_0_, f32[8,1024]{1,0:T(8,128)S(1)} %collective-permute-done.3.refs_1_, ...), custom_call_target="tpu_custom_call" | custom-call | bytes 4135936 | tf_op jit(solution)/shard_map/flux/pallas_call | solution.py:451
  22.1 2.4 %collective-permute-start.5 = (f32[16,2048]{1,0:T(8,128)S(1)}, f32[16,2048]{1,0:T(8,128)S(1)}, u32[]{:S(2)}, u32[]{:S(2)}) collective-permute-start(f32[16,2048]{1,0:T(8,128)S(1)} %get-tuple-element.62), channel_id=1, source_target_pairs={{0,12},{4,8},{8,4},{12,0},{1,13},{5,9},{9,5},{13,1},{2,14},{6,10},... | collective-permute-start | bytes 393224 | tf_op jit(solution)/shard_map/ppermute | solution.py:471
  24.5 0.7 %collective-permute-start.7 = (f32[16,2048]{1,0:T(8,128)S(1)}, f32[16,2048]{1,0:T(8,128)S(1)}, u32[]{:S(2)}, u32[]{:S(2)}) collective-permute-start(f32[16,2048]{1,0:T(8,128)S(1)} %get-tuple-element.64), channel_id=1, source_target_pairs={{0,4},{4,0},{8,12},{12,8},{1,5},{5,1},{9,13},{13,9},{2,6},{6,2},{1... | collective-permute-start | bytes 393224 | tf_op jit(solution)/shard_map/ppermute | solution.py:471
  25.2 1.3 %collective-permute-start.6 = (f32[8,2048]{1,0:T(8,128)S(1)}, f32[8,2048]{1,0:T(8,128)S(1)}, u32[]{:S(2)}, u32[]{:S(2)}) collective-permute-start(f32[8,2048]{1,0:T(8,128)S(1)} %get-tuple-element.63), channel_id=1, source_target_pairs={{0,8},{4,12},{8,0},{12,4},{1,9},{5,13},{9,1},{13,5},{2,10},{6,14},... | collective-permute-start | bytes 196616 | tf_op jit(solution)/shard_map/ppermute | solution.py:471
  26.5 1.9 %local.1 = (f32[152,2048]{1,0:T(8,128)S(1)}, bf16[512,2048]{1,0:T(8,128)(2,1)S(1)}, bf16[512,2048]{1,0:T(8,128)(2,1)S(1)}) custom-call(s32[6,32]{1,0:T(8,128)} %bitcast.6, f32[6,32]{1,0:T(8,128)} %bitcast.11, f32[64,64]{1,0:T(8,128)} %matrix.3, f32[128,2048]{1,0:T(8,128)S(1)} %get-tuple-element.47.field, f32[24,2048]{1,0:T(8,128)S(1)} %get-tuple-element.57.carried, ...), custom_call_target="tpu_custom_call" | custom-call | flops 134217728 | bytes 12169216 | tf_op jit(solution)/shard_map/local/pallas_call | solution.py:451
  28.4 3.8 %collective-permute-done.6.refs_1_ = f32[8,2048]{1,0:T(8,128)S(1)} collective-permute-done((f32[8,2048]{1,0:T(8,128)S(1)}, f32[8,2048]{1,0:T(8,128)S(1)}, u32[]{:S(2)}, u32[]{:S(2)}) %collective-permute-start.6) | collective-permute-done | bytes 65568 | tf_op jit(solution)/shard_map/ppermute | solution.py:471
  32.3 0.0 collective-permute-done.5.refs_0_
  32.3 0.6 %collective-permute-done.7.refs_2_ = f32[16,2048]{1,0:T(8,128)S(1)} collective-permute-done((f32[16,2048]{1,0:T(8,128)S(1)}, f32[16,2048]{1,0:T(8,128)S(1)}, u32[]{:S(2)}, u32[]{:S(2)}) %collective-permute-start.7) | collective-permute-done | bytes 131104 | tf_op jit(solution)/shard_map/ppermute | solution.py:471
  32.9 1.1 %rim.1 = (f32[152,256]{1,0:T(8,128)S(1)}, f32[152,256]{1,0:T(8,128)S(1)}) custom-call(s32[2,4]{1,0:T(2,128)} %bitcast.16, f32[152,2048]{1,0:T(8,128)S(1)} %get-tuple-element.59.base, f32[1,2048]{1,0:T(1,128)S(1)} %get-tuple-element.44.mask, bf16[152,144]{1,0:T(8,128)(2,1)S(1)} %get-tuple-element.60.far, f32[16,2048]{1,0:T(8,128)S(1)} %collective-permute-done.5.refs_0_, ...), custom_call_target="tpu_custom_call" | custom-call | bytes 1979904 | tf_op jit(solution)/shard_map/rim/pallas_call | solution.py:451
  34.0 0.9 %collective-permute-start.8 = (f32[152,256]{1,0:T(8,128)S(1)}, f32[152,256]{1,0:T(8,128)S(1)}, u32[]{:S(2)}, u32[]{:S(2)}) collective-permute-start(f32[152,256]{1,0:T(8,128)S(1)} %get-tuple-element.67), channel_id=1, source_target_pairs={{1,2},{2,1},{5,6},{6,5},{9,10},{10,9},{13,14},{14,13},{17,18},{18,... | collective-permute-start | bytes 466952 | tf_op jit(solution)/shard_map/ppermute | solution.py:466
  34.8 1.6 %collective-permute-start.9 = (f32[152,256]{1,0:T(8,128)S(1)}, f32[152,256]{1,0:T(8,128)S(1)}, u32[]{:S(2)}, u32[]{:S(2)}) collective-permute-start(f32[152,256]{1,0:T(8,128)S(1)} %get-tuple-element.68), channel_id=1, source_target_pairs={{0,1},{1,0},{2,3},{3,2},{4,5},{5,4},{6,7},{7,6},{8,9},{9,8},{10,11... | collective-permute-start | bytes 466952 | tf_op jit(solution)/shard_map/ppermute | solution.py:466
  36.4 3.8 %close.1 = (f32[128,2048]{1,0:T(8,128)S(1)}, f32[128,2048]{1,0:T(8,128)S(1)}) custom-call(s32[6,32]{1,0:T(8,128)} %bitcast.7, f32[6,32]{1,0:T(8,128)} %bitcast.12, f32[152,2048]{1,0:T(8,128)S(1)} %get-tuple-element.59.base, f32[1,2048]{1,0:T(1,128)S(1)} %get-tuple-element.44.mask, bf16[768,256]{1,0:T(8,128)(2,1)S(1)} %get-tuple-element.45.spread, ...), custom_call_target="tpu_custom_call" | custom-call | flops 134217728 | bytes 4797952 | tf_op jit(solution)/shard_map/close/pallas_call | solution.py:451
  40.2 0.0 collective-permute-done.8.first
  40.2 0.0 collective-permute-done.9.second
  40.2 2.0 %second.1 = (f32[128,2048]{1,0:T(8,128)S(1)}, f32[8,3072]{1,0:T(8,128)S(1)}, f32[8,1024]{1,0:T(8,128)S(1)}, f32[8,3072]{1,0:T(8,128)S(1)}) custom-call(f32[128,2048]{1,0:T(8,128)S(1)} %get-tuple-element.66.slope, f32[152,256]{1,0:T(8,128)S(1)} %collective-permute-done.8.first, f32[152,256]{1,0:T(8,128)S(1)} %collective-permute-done.9.second, ...), custom_call_target="tpu_custom_call" | custom-call | bytes 12443648 | tf_op jit(solution)/shard_map/second/pallas_call | solution.py:451
  42.2 1.9 %collective-permute-start.10 = (f32[8,3072]{1,0:T(8,128)S(1)}, f32[8,3072]{1,0:T(8,128)S(1)}, u32[]{:S(2)}, u32[]{:S(2)}) collective-permute-start(f32[8,3072]{1,0:T(8,128)S(1)} %get-tuple-element.74), channel_id=1, source_target_pairs={{0,12},{4,8},{8,4},{12,0},{1,13},{5,9},{9,5},{13,1},{2,14},{6,10},... | collective-permute-start | bytes 294920 | tf_op jit(solution)/shard_map/ppermute | solution.py:471
  44.1 0.4 collective-permute-start.12
  44.4 2.2 %collective-permute-start.11 = (f32[8,1024]{1,0:T(8,128)S(1)}, f32[8,1024]{1,0:T(8,128)S(1)}, u32[]{:S(2)}, u32[]{:S(2)}) collective-permute-start(f32[8,1024]{1,0:T(8,128)S(1)} %get-tuple-element.75), channel_id=1, source_target_pairs={{0,8},{4,12},{8,0},{12,4},{1,9},{5,13},{9,1},{13,5},{2,10},{6,14},... | collective-permute-start | bytes 98312 | tf_op jit(solution)/shard_map/ppermute | solution.py:471
  46.6 3.4 %rest.1.base = f32[128,2048]{1,0:T(8,128)S(1)} custom-call(s32[6,32]{1,0:T(8,128)} %bitcast.8, f32[6,32]{1,0:T(8,128)} %bitcast.13, f32[128,2048]{1,0:T(8,128)S(1)} %get-tuple-element.65.field, f32[128,2048]{1,0:T(8,128)S(1)} %get-tuple-element.73.flux, f32[152,256]{1,0:T(8,128)S(1)} %collective-permute-done.8.first, ...), custom_call_target="tpu_custom_call" | custom-call | flops 134217728 | bytes 4485120 | tf_op jit(solution)/shard_map/rest/pallas_call | solution.py:451
  50.0 0.0 collective-permute-done.11.refs_3_
  50.0 0.0 collective-permute-done.10.refs_2_
  50.0 1.3 %collective-permute-done.12.refs_4_ = f32[8,3072]{1,0:T(8,128)S(1)} collective-permute-done((f32[8,3072]{1,0:T(8,128)S(1)}, f32[8,3072]{1,0:T(8,128)S(1)}, u32[]{:S(2)}, u32[]{:S(2)}) %collective-permute-start.12) | collective-permute-done | bytes 98336 | tf_op jit(solution)/shard_map/ppermute | solution.py:471
  51.3 1.2 %last.1 = f32[128,2048]{1,0:T(8,128)} custom-call(f32[128,2048]{1,0:T(8,128)S(1)} %rest.1.base, f32[1,2048]{1,0:T(1,128)S(1)} %get-tuple-element.44.mask, bf16[152,144]{1,0:T(8,128)(2,1)S(1)} %get-tuple-element.55.refs_5_.refs_0_, bf16[152,144]{1,0:T(8,128)(2,1)S(1)} %get-tuple-element.56.refs_6_.refs_1_, f32[8,3072]{1,0:T(8,128)S(1)} %collective-permute-done.10.refs_2_, ...), custom_call_target="tpu_custom_call" | custom-call | bytes 2509824 | tf_op jit(solution)/shard_map/last/pallas_call | solution.py:451
Async XLA Ops:
  1.3 7.8 %collective-permute-start = (f32[128,256]{1,0:T(8,128)S(1)}, f32[128,256]{1,0:T(8,128)S(1)}, u32[]{:S(2)}, u32[]{:S(2)}) collective-permute-start(f32[128,256]{1,0:T(8,128)S(1)} %get-tuple-element.42), channel_id=1, source_target_pairs={{1,2},{2,1},{5,6},{6,5},{9,10},{10,9},{13,14},{14,13},{17,18},{18,... | collective-permute-start | bytes 393224 | tf_op jit(solution)/shard_map/ppermute | solution.py:466
  1.9 7.1 %collective-permute-start.1 = (f32[128,256]{1,0:T(8,128)S(1)}, f32[128,256]{1,0:T(8,128)S(1)}, u32[]{:S(2)}, u32[]{:S(2)}) collective-permute-start(f32[128,256]{1,0:T(8,128)S(1)} %get-tuple-element.43), channel_id=1, source_target_pairs={{0,1},{1,0},{2,3},{3,2},{4,5},{5,4},{6,7},{7,6},{8,9},{9,8},{10,11... | collective-permute-start | bytes 393224 | tf_op jit(solution)/shard_map/ppermute | solution.py:466
  9.0 12.0 %copy-start = (f32[128,2048]{1,0:T(8,128)S(1)}, f32[128,2048]{1,0:T(8,128)}, u32[]{:S(2)}) copy-start(f32[128,2048]{1,0:T(8,128)} %kappa.1) | copy-start | bytes 3145732
  11.5 9.0 %collective-permute-start.2 = (f32[8,3072]{1,0:T(8,128)S(1)}, f32[8,3072]{1,0:T(8,128)S(1)}, u32[]{:S(2)}, u32[]{:S(2)}) collective-permute-start(f32[8,3072]{1,0:T(8,128)S(1)} %get-tuple-element.51), channel_id=1, source_target_pairs={{0,12},{4,8},{8,4},{12,0},{1,13},{5,9},{9,5},{13,1},{2,14},{6,10},... | collective-permute-start | bytes 294920 | tf_op jit(solution)/shard_map/ppermute | solution.py:471
  15.1 5.9 %collective-permute-start.4 = (f32[8,3072]{1,0:T(8,128)S(1)}, f32[8,3072]{1,0:T(8,128)S(1)}, u32[]{:S(2)}, u32[]{:S(2)}) collective-permute-start(f32[8,3072]{1,0:T(8,128)S(1)} %get-tuple-element.53), channel_id=1, source_target_pairs={{0,4},{4,0},{8,12},{12,8},{1,5},{5,1},{9,13},{13,9},{2,6},{6,2},{1... | collective-permute-start | bytes 294920 | tf_op jit(solution)/shard_map/ppermute | solution.py:471
  15.1 5.3 %collective-permute-start.3 = (f32[8,1024]{1,0:T(8,128)S(1)}, f32[8,1024]{1,0:T(8,128)S(1)}, u32[]{:S(2)}, u32[]{:S(2)}) collective-permute-start(f32[8,1024]{1,0:T(8,128)S(1)} %get-tuple-element.52), channel_id=1, source_target_pairs={{0,8},{4,12},{8,0},{12,4},{1,9},{5,13},{9,1},{13,5},{2,10},{6,14},... | collective-permute-start | bytes 98312 | tf_op jit(solution)/shard_map/ppermute | solution.py:471
  22.1 10.2 %collective-permute-start.5 = (f32[16,2048]{1,0:T(8,128)S(1)}, f32[16,2048]{1,0:T(8,128)S(1)}, u32[]{:S(2)}, u32[]{:S(2)}) collective-permute-start(f32[16,2048]{1,0:T(8,128)S(1)} %get-tuple-element.62), channel_id=1, source_target_pairs={{0,12},{4,8},{8,4},{12,0},{1,13},{5,9},{9,5},{13,1},{2,14},{6,10},... | collective-permute-start | bytes 393224 | tf_op jit(solution)/shard_map/ppermute | solution.py:471
  24.5 8.4 %collective-permute-start.7 = (f32[16,2048]{1,0:T(8,128)S(1)}, f32[16,2048]{1,0:T(8,128)S(1)}, u32[]{:S(2)}, u32[]{:S(2)}) collective-permute-start(f32[16,2048]{1,0:T(8,128)S(1)} %get-tuple-element.64), channel_id=1, source_target_pairs={{0,4},{4,0},{8,12},{12,8},{1,5},{5,1},{9,13},{13,9},{2,6},{6,2},{1... | collective-permute-start | bytes 393224 | tf_op jit(solution)/shard_map/ppermute | solution.py:471
  25.2 7.0 %collective-permute-start.6 = (f32[8,2048]{1,0:T(8,128)S(1)}, f32[8,2048]{1,0:T(8,128)S(1)}, u32[]{:S(2)}, u32[]{:S(2)}) collective-permute-start(f32[8,2048]{1,0:T(8,128)S(1)} %get-tuple-element.63), channel_id=1, source_target_pairs={{0,8},{4,12},{8,0},{12,4},{1,9},{5,13},{9,1},{13,5},{2,10},{6,14},... | collective-permute-start | bytes 196616 | tf_op jit(solution)/shard_map/ppermute | solution.py:471
  34.0 6.2 %collective-permute-start.8 = (f32[152,256]{1,0:T(8,128)S(1)}, f32[152,256]{1,0:T(8,128)S(1)}, u32[]{:S(2)}, u32[]{:S(2)}) collective-permute-start(f32[152,256]{1,0:T(8,128)S(1)} %get-tuple-element.67), channel_id=1, source_target_pairs={{1,2},{2,1},{5,6},{6,5},{9,10},{10,9},{13,14},{14,13},{17,18},{18,... | collective-permute-start | bytes 466952 | tf_op jit(solution)/shard_map/ppermute | solution.py:466
  34.8 5.4 %collective-permute-start.9 = (f32[152,256]{1,0:T(8,128)S(1)}, f32[152,256]{1,0:T(8,128)S(1)}, u32[]{:S(2)}, u32[]{:S(2)}) collective-permute-start(f32[152,256]{1,0:T(8,128)S(1)} %get-tuple-element.68), channel_id=1, source_target_pairs={{0,1},{1,0},{2,3},{3,2},{4,5},{5,4},{6,7},{7,6},{8,9},{9,8},{10,11... | collective-permute-start | bytes 466952 | tf_op jit(solution)/shard_map/ppermute | solution.py:466
  42.2 7.8 %collective-permute-start.10 = (f32[8,3072]{1,0:T(8,128)S(1)}, f32[8,3072]{1,0:T(8,128)S(1)}, u32[]{:S(2)}, u32[]{:S(2)}) collective-permute-start(f32[8,3072]{1,0:T(8,128)S(1)} %get-tuple-element.74), channel_id=1, source_target_pairs={{0,12},{4,8},{8,4},{12,0},{1,13},{5,9},{9,5},{13,1},{2,14},{6,10},... | collective-permute-start | bytes 294920 | tf_op jit(solution)/shard_map/ppermute | solution.py:471
  44.1 7.2 %collective-permute-start.12 = (f32[8,3072]{1,0:T(8,128)S(1)}, f32[8,3072]{1,0:T(8,128)S(1)}, u32[]{:S(2)}, u32[]{:S(2)}) collective-permute-start(f32[8,3072]{1,0:T(8,128)S(1)} %get-tuple-element.76), channel_id=1, source_target_pairs={{0,4},{4,0},{8,12},{12,8},{1,5},{5,1},{9,13},{13,9},{2,6},{6,2},{1... | collective-permute-start | bytes 294920 | tf_op jit(solution)/shard_map/ppermute | solution.py:471
  44.4 5.6 %collective-permute-start.11 = (f32[8,1024]{1,0:T(8,128)S(1)}, f32[8,1024]{1,0:T(8,128)S(1)}, u32[]{:S(2)}, u32[]{:S(2)}) collective-permute-start(f32[8,1024]{1,0:T(8,128)S(1)} %get-tuple-element.75), channel_id=1, source_target_pairs={{0,8},{4,12},{8,0},{12,4},{1,9},{5,13},{9,1},{13,5},{2,10},{6,14},... | collective-permute-start | bytes 98312 | tf_op jit(solution)/shard_map/ppermute | solution.py:471

commit v3 on v2

--- a/solution.py
+++ b/solution.py
@@ -115,7 +115,9 @@
             add("far_half%d" % half, folded(firsts, half, 1))
         add("send_rows", folded([first[t, s] for t in partners], 0, 0))
         add("send_joint", np.concatenate([joint[t, s] for t in partners], axis=0))
-        add("far_joint", np.concatenate(joints, axis=1))
+        joint_far = np.concatenate(joints, axis=1)
+        add("far_joint", joint_far)
+        add("onward_far", axial_step * np.concatenate([block(s, s), left[s]], axis=1) @ joint_far)
         add("local", np.concatenate([block(s, s), onward[s][:, cut(s)]], axis=0))
         add("onward", np.concatenate([block(s, s), left[s]], axis=1))
     return dict(
@@ -172,8 +174,8 @@
         parts = []
         for place in range(2):
             index = exported[side, 2 * tile + place]
-            value = source[:, pl.ds(pl.multiple_of(index // 2 * lanes, lanes), lanes)]
-            parts.append(jnp.where(index % 2 == place, value, pltpu.roll(value, lanes // 2, 1)))
+            value = source[:, pl.ds(pl.multiple_of((index >> 1) * lanes, lanes), lanes)]
+            parts.append(jnp.where(index & 1 == place, value, pltpu.roll(value, lanes // 2, 1)))
         tiles.append(jnp.where(low_half(), parts[0], parts[1]))
     return jnp.concatenate(tiles, axis=1)
 
@@ -213,23 +215,27 @@
 
 
 def fill(extended, tile, value):
-    extended[0, tile] = value
-    extended[1, tile] = pltpu.roll(value, lanes // 2, 1)
+    extended[2 * tile] = value
+    extended[2 * tile + 1] = pltpu.roll(value, lanes // 2, 1)
 
 
 def fill_own(extended, own):
-    tiles = own.shape[1] // lanes
-    for tile in range(tiles):
+    for tile in range(own.shape[1] // lanes):
         fill(extended, tile, own[:, tile_at(tile)])
-    fill(extended, extended.shape[1] - 1, jnp.zeros(extended.shape[2:], jnp.float32))
+
+
+def clear_from(extended, start):
+    for entry in range(start, extended.shape[0]):
+        extended[entry] = jnp.zeros(extended.shape[1:], jnp.float32)
 
 
 def fill_rim(extended, first, second):
     rim = first.shape[1] // lanes
-    start = extended.shape[1] - 1 - 2 * rim
+    start = extended.shape[0] // 2 - 1 - 2 * rim
     for side, values in zip(sides(), (first, second)):
         for tile in range(rim):
             fill(extended, start + side * rim + tile, values[:, tile_at(tile)])
+    clear_from(extended, extended.shape[0] - 2)
 
 
 def conducted(lookup, conductance, mask, spread, extended, gathered, pieces):
@@ -239,16 +245,16 @@
         start = piece.start // lanes
         for tile in range(start, piece.stop // lanes):
             low, high = 2 * tile, 2 * tile + 1
-            total = jnp.where(half, conductance[0, low], conductance[0, high]) * extended[0, tile]
+            total = jnp.where(half, conductance[0, low], conductance[0, high]) * extended[2 * tile]
             for slot in range(1, lookup.shape[0]):
                 one, two = lookup[slot, low], lookup[slot, high]
-                value = jnp.where(half, extended[one % 2, one // 2], extended[1 - two % 2, two // 2])
+                value = jnp.where(half, extended[one], extended[two ^ 1])
                 total = total + jnp.where(half, conductance[slot, low], conductance[slot, high]) * value
             gathered[:, tile_at(tile)] = total
         moved = []
         for tile in range(start, piece.stop // lanes, per):
             part = slice(tile * lanes, (tile + per) * lanes)
-            own = jnp.concatenate([extended[0, tile + i] for i in range(per)], axis=1)
+            own = jnp.concatenate([extended[2 * (tile + i)] for i in range(per)], axis=1)
             moved.append(own + mask[:, part] * right_product(gathered[:, part], spread[...]))
         yield piece, jnp.concatenate(moved, axis=1)
 
@@ -353,17 +359,24 @@
             high[rows, piece], low[rows, piece] = split(wide * gain)
 
 
-def local_kernel(lookup, conductance, matrix, field, carried, flux, mask, local, out, high, low, *scratch):
-    table, weight, block_matrix, sems = scratch
-    slab = field.shape[0]
-    got = load([(lookup, table), (conductance, weight), (matrix, block_matrix)], sems)
-    for piece in chunks(field.shape[1]):
+def local_kernel(lookup, conductance, matrix, field, carried, flux, mask, spread, local, onward, *refs):
+    out, slope, high, low, table, weight, rows_table, rows_weight, block_matrix, extended, gathered, sems = refs
+    slab, nodes = field.shape
+    tables = [(lookup, table), (conductance, weight), (lookup, rows_table), (conductance, rows_weight)]
+    got = load([*tables, (matrix, block_matrix)], sems)
+    for piece in chunks(nodes):
         step = axial_step * mask[:, piece] * left_product(local[...], flux[:, piece])
-        out[:slab, piece] = field[:, piece] + step[:slab]
-        out[slab:, piece] = carried[:, piece] + step[slab:]
+        values = jnp.concatenate([field[:, piece] + step[:slab], carried[:, piece] + step[slab:]], axis=0)
+        out[:, piece] = values
+        own = left_product(onward[...], values)
+        for tile in range(piece.start // lanes, piece.stop // lanes):
+            fill(extended, tile, own[:, tile * lanes - piece.start : (tile + 1) * lanes - piece.start])
+    clear_from(extended, 2 * (nodes // lanes))
     for copy in got:
         copy.wait()
-    rim_matrix(table, weight, mask, block_matrix, field.shape[1] // block_matrix.shape[0], high, low)
+    for piece, values in conducted(table, weight, mask, spread, extended, gathered, chunks(nodes)):
+        slope[:, piece] = values
+    rim_matrix(rows_table, rows_weight, mask, block_matrix, nodes // block_matrix.shape[0], high, low)
 
 
 def rim_kernel(spans, exported, base, mask, far, *refs):
@@ -375,23 +388,17 @@
         out[...] = take_face(base, faces, side) + axial_step * take_face(mask, faces, side) * left_product(far[...], rows)
 
 
-def close_kernel(spans, lookup, conductance, base, mask, spread, far, onward, *refs):
-    got, (out, slope, table, weight, extended, gathered, sems) = refs[: spans - 1], refs[spans - 1 :]
-    slab, nodes = out.shape
+def close_kernel(spans, lookup, conductance, slope, mask, spread, onward_far, *refs):
+    got, (out, table, weight, extended, gathered, sems) = refs[: spans - 1], refs[spans - 1 :]
+    nodes = out.shape[1]
     copies = load([(lookup, table), (conductance, weight)], sems)
-    for piece in chunks(nodes):
-        values = base[:, piece] + axial_step * mask[:, piece] * left_product(far[...], stacked(got, piece))
-        out[:, piece] = values[:slab]
-        own = left_product(onward[...], values)
-        for tile in range(piece.start // lanes, piece.stop // lanes):
-            fill(extended, tile, own[:, tile * lanes - piece.start : (tile + 1) * lanes - piece.start])
-    for tile in range(nodes // lanes, extended.shape[1]):
-        extended[0, tile] = jnp.zeros(extended.shape[2:], jnp.float32)
-        extended[1, tile] = jnp.zeros(extended.shape[2:], jnp.float32)
+    for tile in range(nodes // lanes):
+        fill(extended, tile, mask[:, tile_at(tile)] * stacked(got, tile_at(tile)))
+    clear_from(extended, 2 * (nodes // lanes))
     for copy in copies:
         copy.wait()
     for piece, values in conducted(table, weight, mask, spread, extended, gathered, chunks(nodes)):
-        slope[:, piece] = values
+        out[:, piece] = slope[:, piece] + left_product(onward_far[...], values)
 
 
 def second_kernel(slope, first, second, high, low, kappa, onward, *refs):
@@ -414,15 +421,18 @@
         store_folded(left_product(sends[half][...], value), outs, piece, nodes)
 
 
-def rest_kernel(lookup, conductance, field, flux, first, second, mask, spread, local, out, *scratch):
-    table, weight, extended, gathered, sems = scratch
-    slab = field.shape[0]
-    got = load([(lookup, table), (conductance, weight)], sems)
-    fill_own(extended, field)
+def rest_kernel(spans, lookup, conductance, base, flux, first, second, mask, spread, local, far, *refs):
+    got, (out, table, weight, extended, gathered, sems) = refs[: spans - 1], refs[spans - 1 :]
+    slab, nodes = flux.shape
+    copies = load([(lookup, table), (conductance, weight)], sems)
+    for piece in chunks(nodes):
+        own = base[:slab, piece] + axial_step * mask[:, piece] * left_product(far[:slab], stacked(got, piece))
+        for tile in range(piece.start // lanes, piece.stop // lanes):
+            fill(extended, tile, own[:, tile * lanes - piece.start : (tile + 1) * lanes - piece.start])
     fill_rim(extended, first[:slab], second[:slab])
-    for copy in got:
+    for copy in copies:
         copy.wait()
-    for piece, values in conducted(table, weight, mask, spread, extended, gathered, chunks(field.shape[1])):
+    for piece, values in conducted(table, weight, mask, spread, extended, gathered, chunks(nodes)):
         out[:, piece] = values + axial_step * mask[:, piece] * left_product(local[:slab], flux[:, piece])
 
 
@@ -485,13 +495,14 @@
     whole = (slab, nodes)
     work = 2 * nodes * slab * slab
 
-    def conduct_scratch(height):
+    def conduct_scratch(height, copies=2, more=()):
         return [
             pltpu.SMEM(tables[0].shape, jnp.int32),
             pltpu.SMEM(tables[1].shape, jnp.float32),
-            pltpu.VMEM((2, tiles, height, lanes), jnp.float32),
+            *more,
+            pltpu.VMEM((2 * tiles, height, lanes), jnp.float32),
             pltpu.VMEM((height, nodes), jnp.float32),
-            pltpu.SemaphoreType.DMA((2,)),
+            pltpu.SemaphoreType.DMA((copies,)),
         ]
 
     face_scratch = pltpu.SMEM(faces, jnp.int32)
@@ -549,18 +560,21 @@
     )
     joint = trade_slabs(joint)
     half_matrix = jax.ShapeDtypeStruct((2 * rim, nodes), jnp.bfloat16)
-    base, high, low = call(
+    base, slope, high, low = call(
         local_kernel,
         [*tables, matrix],
-        [state, carried, flux, mask, own["local"]],
-        [(tall, nodes), half_matrix, half_matrix],
-        [
-            pltpu.VMEM(tables[0].shape, jnp.int32),
-            pltpu.VMEM(tables[1].shape, jnp.float32),
-            pltpu.VMEM(matrix.shape, jnp.float32),
-            pltpu.SemaphoreType.DMA((3,)),
-        ],
-        2 * work,
+        [state, carried, flux, mask, spread, own["local"], own["onward"]],
+        [(tall, nodes), whole, half_matrix, half_matrix],
+        conduct_scratch(
+            slab,
+            5,
+            [
+                pltpu.VMEM(tables[0].shape, jnp.int32),
+                pltpu.VMEM(tables[1].shape, jnp.float32),
+                pltpu.VMEM(matrix.shape, jnp.float32),
+            ],
+        ),
+        4 * work,
         "local",
     )
     first, second = call(
@@ -572,13 +586,13 @@
         name="rim",
     )
     left, right = trade_faces(first, second)
-    state, slope = call(
+    (slope,) = call(
         functools.partial(close_kernel, spans),
         tables,
-        [base, mask, spread, own["far_joint"], own["onward"], *joint],
-        [whole, whole],
-        conduct_scratch(slab),
-        2 * work,
+        [slope, mask, spread, own["onward_far"], *joint],
+        [whole],
+        conduct_scratch(sum(rank for rank, _ in sent_joint)),
+        work,
         "close",
     )
     flux, *parts = call(
@@ -589,10 +603,10 @@
         name="second",
     )
     parts = trade_slabs(parts)
-    (base,) = call(
-        rest_kernel,
+    (state,) = call(
+        functools.partial(rest_kernel, spans),
         tables,
-        [state, flux, left, right, mask, spread, own["local"]],
+        [base, flux, left, right, mask, spread, own["local"], own["far_joint"], *joint],
         [whole],
         conduct_scratch(slab),
         2 * work,
@@ -601,7 +615,7 @@
     (state,) = call(
         functools.partial(last_kernel, spans),
         [],
-        [base, mask, *fars, *parts],
+        [state, mask, *fars, *parts],
         [whole],
         [pltpu.VMEM(whole, jnp.float32), pltpu.SemaphoreType.DMA((len(chunks(nodes)),))],
         name="last",

time: 53.1 us -> 51.5 us (0.970)
  the two profiles are of different devices: /device:TPU:0 before, /device:TPU:1 now
where the time goes in v3:
time: 51.5 us; the launch traced here: 50.5 us
  Pallas kernels  22.9 us (44%)
  starting transfers between devices  17.7 us (34%)
  waiting for transfers between devices  8.98 us (17%)
  between operations  0.95 us (2%)
    pallas_call x11, Pallas kernels, call(): pl.pallas_call(kernel, in_specs=[pl.BlockSpec(memory_space=space) for arr...  22.9 us
    ppermute x9, starting transfers between devices, trade_slabs(): lax.ppermute(part, 'hgt', [(i, i ^ x) for i in range(count)])  10.9 us
    ppermute x9, waiting for transfers between devices, trade_slabs(): lax.ppermute(part, 'hgt', [(i, i ^ x) for i in range(count)])  6.82 us
    ppermute x2, starting transfers between devices, trade_faces(): lax.ppermute(first, 'xs', swap(1))  6.64 us
    ppermute x2, waiting for transfers between devices, trade_faces(): lax.ppermute(first, 'xs', swap(1))  2.15 us
  transfers between devices with their start and end apart: 13, of which 6 were waited for; matrix products, arithmetic and copies ran while one was open for 0% of the time, Pallas kernels for 29%

profile of v3, /device:TPU:1, one launch (start us, length us, event | category | flops | bytes accessed | tf_op | source)
XLA Modules:
  0.0 50.5 jit_solution(17157594235176031062)
XLA Ops:
  0.0 1.3 %faces.1 = (f32[128,256]{1,0:T(8,128)S(1)}, f32[128,256]{1,0:T(8,128)S(1)}) custom-call(s32[2,4]{1,0:T(2,128)} %bitcast.15, f32[128,2048]{1,0:T(8,128)} %field.3), custom_call_target="tpu_custom_call" | custom-call | bytes 262144 | tf_op jit(solution)/shard_map/faces/pallas_call | solution.py:461
  1.3 4.5 %collective-permute-start = (f32[128,256]{1,0:T(8,128)S(1)}, f32[128,256]{1,0:T(8,128)S(1)}, u32[]{:S(2)}, u32[]{:S(2)}) collective-permute-start(f32[128,256]{1,0:T(8,128)S(1)} %get-tuple-element.42), channel_id=1, source_target_pairs={{1,2},{2,1},{5,6},{6,5},{9,10},{10,9},{13,14},{14,13},{17,18},{18,... | collective-permute-start | bytes 393224 | tf_op jit(solution)/shard_map/ppermute | solution.py:476
  5.8 0.1 collective-permute-start.1
  6.5 2.1 %prepare.1 = (f32[1,2048]{1,0:T(1,128)S(1)}, bf16[768,256]{1,0:T(8,128)(2,1)S(1)}, f32[128,2048]{1,0:T(8,128)S(1)}, f32[40,2048]{1,0:T(8,128)S(1)}, bf16[40,384]...) custom-call(s32[1]{0:T(128)S(6)} %copy.19.total, ...), custom_call_target="tpu_custom_call" | custom-call | flops 67108864 | bytes 3232256 | tf_op jit(solution)/shard_map/prepare/pallas_call | solution.py:461
  8.6 0.0 copy-start
  8.6 0.0 collective-permute-done.first
  8.6 0.0 collective-permute-done.1.second
  8.6 1.7 %moments.1 = (f32[8,3072]{1,0:T(8,128)S(1)}, f32[8,1024]{1,0:T(8,128)S(1)}, f32[8,3072]{1,0:T(8,128)S(1)}) custom-call(s32[6,32]{1,0:T(8,128)} %bitcast.4, f32[6,32]{1,0:T(8,128)} %bitcast.9, f32[40,2048]{1,0:T(8,128)S(1)} %get-tuple-element.49.moments, f32[128,256]{1,0:T(8,128)S(1)} %collective-permute-done.first, ...), custom_call_target="tpu_custom_call" | custom-call | bytes 1675264 | tf_op jit(solution)/shard_map/moments/pallas_call | solution.py:461
  10.3 3.4 %collective-permute-start.2 = (f32[8,3072]{1,0:T(8,128)S(1)}, f32[8,3072]{1,0:T(8,128)S(1)}, u32[]{:S(2)}, u32[]{:S(2)}) collective-permute-start(f32[8,3072]{1,0:T(8,128)S(1)} %get-tuple-element.51), channel_id=1, source_target_pairs={{0,12},{4,8},{8,4},{12,0},{1,13},{5,9},{9,5},{13,1},{2,14},{6,10},... | collective-permute-start | bytes 294920 | tf_op jit(solution)/shard_map/ppermute | solution.py:481
  13.7 0.0 collective-permute-start.4
  13.7 0.4 collective-permute-start.3
  14.1 3.1 %first.1 = (f32[128,2048]{1,0:T(8,128)S(1)}, f32[128,2048]{1,0:T(8,128)S(1)}) custom-call(s32[6,32]{1,0:T(8,128)} %bitcast.5, f32[6,32]{1,0:T(8,128)} %bitcast.10, f32[128,2048]{1,0:T(8,128)S(1)} %get-tuple-element.41.field, f32[128,256]{1,0:T(8,128)S(1)} %collective-permute-done.first, f32[128,256]{1,0:T(8,128)S(1)} %collective-permute-done.1.second, ...), custom_call_target="tpu_custom_call" | custom-call | flops 134217728 | bytes 4435968 | tf_op jit(solution)/shard_map/first/pallas_call | solution.py:461
  17.2 1.0 %collective-permute-done.3.refs_1_ = f32[8,1024]{1,0:T(8,128)S(1)} collective-permute-done((f32[8,1024]{1,0:T(8,128)S(1)}, f32[8,1024]{1,0:T(8,128)S(1)}, u32[]{:S(2)}, u32[]{:S(2)}) %collective-permute-start.3) | collective-permute-done | bytes 32800 | tf_op jit(solution)/shard_map/ppermute | solution.py:481
  18.2 0.0 collective-permute-done.2.refs_0_
  18.2 1.0 %collective-permute-done.4.refs_2_ = f32[8,3072]{1,0:T(8,128)S(1)} collective-permute-done((f32[8,3072]{1,0:T(8,128)S(1)}, f32[8,3072]{1,0:T(8,128)S(1)}, u32[]{:S(2)}, u32[]{:S(2)}) %collective-permute-start.4) | collective-permute-done | bytes 98336 | tf_op jit(solution)/shard_map/ppermute | solution.py:481
  19.2 0.0 copy-done
  19.2 1.1 %flux.1 = (f32[128,2048]{1,0:T(8,128)S(1)}, f32[24,2048]{1,0:T(8,128)S(1)}, f32[16,2048]{1,0:T(8,128)S(1)}, f32[8,2048]{1,0:T(8,128)S(1)}, f32[16,2048]{1,0:T(8,128)S(1)}) custom-call(f32[128,2048]{1,0:T(8,128)S(1)} %get-tuple-element.48.slope, f32[8,3072]{1,0:T(8,128)S(1)} %collective-permute-done.2.refs_0_, f32[8,1024]{1,0:T(8,128)S(1)} %collective-permute-done.3.refs_1_, ...), custom_call_target="tpu_custom_call" | custom-call | bytes 4135936 | tf_op jit(solution)/shard_map/flux/pallas_call | solution.py:461
  20.3 1.8 %collective-permute-start.5 = (f32[16,2048]{1,0:T(8,128)S(1)}, f32[16,2048]{1,0:T(8,128)S(1)}, u32[]{:S(2)}, u32[]{:S(2)}) collective-permute-start(f32[16,2048]{1,0:T(8,128)S(1)} %get-tuple-element.63), channel_id=1, source_target_pairs={{0,12},{4,8},{8,4},{12,0},{1,13},{5,9},{9,5},{13,1},{2,14},{6,10},... | collective-permute-start | bytes 393224 | tf_op jit(solution)/shard_map/ppermute | solution.py:481
  22.1 0.3 collective-permute-start.7
  22.4 1.5 %collective-permute-start.6 = (f32[8,2048]{1,0:T(8,128)S(1)}, f32[8,2048]{1,0:T(8,128)S(1)}, u32[]{:S(2)}, u32[]{:S(2)}) collective-permute-start(f32[8,2048]{1,0:T(8,128)S(1)} %get-tuple-element.64), channel_id=1, source_target_pairs={{0,8},{4,12},{8,0},{12,4},{1,9},{5,13},{9,1},{13,5},{2,10},{6,14},... | collective-permute-start | bytes 196616 | tf_op jit(solution)/shard_map/ppermute | solution.py:481
  23.9 4.5 %local.1 = (f32[152,2048]{1,0:T(8,128)S(1)}, f32[128,2048]{1,0:T(8,128)S(1)}, bf16[512,2048]{1,0:T(8,128)(2,1)S(1)}, bf16[512,2048]{1,0:T(8,128)(2,1)S(1)}) custom-call(s32[6,32]{1,0:T(8,128)} %bitcast.6, f32[6,32]{1,0:T(8,128)} %bitcast.11, f32[64,64]{1,0:T(8,128)} %matrix.3, f32[128,2048]{1,0:T(8,128)S(1)} %get-tuple-element.47.field, ...), custom_call_target="tpu_custom_call" | custom-call | flops 268435456 | bytes 14249984 | tf_op jit(solution)/shard_map/local/pallas_call | solution.py:461
  28.4 1.0 %collective-permute-done.6.refs_1_ = f32[8,2048]{1,0:T(8,128)S(1)} collective-permute-done((f32[8,2048]{1,0:T(8,128)S(1)}, f32[8,2048]{1,0:T(8,128)S(1)}, u32[]{:S(2)}, u32[]{:S(2)}) %collective-permute-start.6) | collective-permute-done | bytes 65568 | tf_op jit(solution)/shard_map/ppermute | solution.py:481
  29.3 0.0 collective-permute-done.5.refs_0_
  29.3 2.3 %collective-permute-done.7.refs_2_ = f32[16,2048]{1,0:T(8,128)S(1)} collective-permute-done((f32[16,2048]{1,0:T(8,128)S(1)}, f32[16,2048]{1,0:T(8,128)S(1)}, u32[]{:S(2)}, u32[]{:S(2)}) %collective-permute-start.7) | collective-permute-done | bytes 131104 | tf_op jit(solution)/shard_map/ppermute | solution.py:481
  31.6 1.0 %rim.1 = (f32[152,256]{1,0:T(8,128)S(1)}, f32[152,256]{1,0:T(8,128)S(1)}) custom-call(s32[2,4]{1,0:T(2,128)} %bitcast.16, f32[152,2048]{1,0:T(8,128)S(1)} %get-tuple-element.60.base, f32[1,2048]{1,0:T(1,128)S(1)} %get-tuple-element.44.mask, bf16[152,144]{1,0:T(8,128)(2,1)S(1)} %get-tuple-element.66.far, f32[16,2048]{1,0:T(8,128)S(1)} %collective-permute-done.5.refs_0_, ...), custom_call_target="tpu_custom_call" | custom-call | bytes 1979904 | tf_op jit(solution)/shard_map/rim/pallas_call | solution.py:461
  32.7 2.1 %collective-permute-start.8 = (f32[152,256]{1,0:T(8,128)S(1)}, f32[152,256]{1,0:T(8,128)S(1)}, u32[]{:S(2)}, u32[]{:S(2)}) collective-permute-start(f32[152,256]{1,0:T(8,128)S(1)} %get-tuple-element.67), channel_id=1, source_target_pairs={{1,2},{2,1},{5,6},{6,5},{9,10},{10,9},{13,14},{14,13},{17,18},{18,... | collective-permute-start | bytes 466952 | tf_op jit(solution)/shard_map/ppermute | solution.py:476
  34.8 0.1 collective-permute-start.9
  34.9 2.2 %close.1.slope = f32[128,2048]{1,0:T(8,128)S(1)} custom-call(s32[6,32]{1,0:T(8,128)} %bitcast.7, f32[6,32]{1,0:T(8,128)} %bitcast.12, f32[128,2048]{1,0:T(8,128)S(1)} %get-tuple-element.61.slope, f32[1,2048]{1,0:T(1,128)S(1)} %get-tuple-element.44.mask, bf16[768,256]{1,0:T(8,128)(2,1)S(1)} %get-tuple-element.45.spread, ...), custom_call_target="tpu_custom_call" | custom-call | flops 67108864 | bytes 3293184 | tf_op jit(solution)/shard_map/close/pallas_call | solution.py:461
  37.1 2.1 %collective-permute-done.8.first = f32[152,256]{1,0:T(8,128)S(1)} collective-permute-done((f32[152,256]{1,0:T(8,128)S(1)}, f32[152,256]{1,0:T(8,128)S(1)}, u32[]{:S(2)}, u32[]{:S(2)}) %collective-permute-start.8) | collective-permute-done | bytes 155680 | tf_op jit(solution)/shard_map/ppermute | solution.py:476
  39.2 0.0 collective-permute-done.9.second
  39.2 2.0 %second.1 = (f32[128,2048]{1,0:T(8,128)S(1)}, f32[8,3072]{1,0:T(8,128)S(1)}, f32[8,1024]{1,0:T(8,128)S(1)}, f32[8,3072]{1,0:T(8,128)S(1)}) custom-call(f32[128,2048]{1,0:T(8,128)S(1)} %close.1.slope, f32[152,256]{1,0:T(8,128)S(1)} %collective-permute-done.8.first, f32[152,256]{1,0:T(8,128)S(1)} %collective-permute-done.9.second, ...), custom_call_target="tpu_custom_call" | custom-call | bytes 12443648 | tf_op jit(solution)/shard_map/second/pallas_call | solution.py:461
  41.2 0.6 %collective-permute-start.10 = (f32[8,3072]{1,0:T(8,128)S(1)}, f32[8,3072]{1,0:T(8,128)S(1)}, u32[]{:S(2)}, u32[]{:S(2)}) collective-permute-start(f32[8,3072]{1,0:T(8,128)S(1)} %get-tuple-element.74), channel_id=1, source_target_pairs={{0,12},{4,8},{8,4},{12,0},{1,13},{5,9},{9,5},{13,1},{2,14},{6,10},... | collective-permute-start | bytes 294920 | tf_op jit(solution)/shard_map/ppermute | solution.py:481
  41.8 0.0 collective-permute-start.12
  41.8 3.0 %collective-permute-start.11 = (f32[8,1024]{1,0:T(8,128)S(1)}, f32[8,1024]{1,0:T(8,128)S(1)}, u32[]{:S(2)}, u32[]{:S(2)}) collective-permute-start(f32[8,1024]{1,0:T(8,128)S(1)} %get-tuple-element.75), channel_id=1, source_target_pairs={{0,8},{4,12},{8,0},{12,4},{1,9},{5,13},{9,1},{13,5},{2,10},{6,14},... | collective-permute-start | bytes 98312 | tf_op jit(solution)/shard_map/ppermute | solution.py:481
  44.9 2.8 %rest.1.base = f32[128,2048]{1,0:T(8,128)S(1)} custom-call(s32[6,32]{1,0:T(8,128)} %bitcast.8, f32[6,32]{1,0:T(8,128)} %bitcast.13, f32[152,2048]{1,0:T(8,128)S(1)} %get-tuple-element.60.base, f32[128,2048]{1,0:T(8,128)S(1)} %get-tuple-element.73.flux, f32[152,256]{1,0:T(8,128)S(1)} %collective-permute-done.8.first, ...), custom_call_target="tpu_custom_call" | custom-call | flops 134217728 | bytes 5096960 | tf_op jit(solution)/shard_map/rest/pallas_call | solution.py:461
  47.7 0.0 collective-permute-done.11.refs_3_
  47.7 0.0 collective-permute-done.10.refs_2_
  47.7 1.5 %collective-permute-done.12.refs_4_ = f32[8,3072]{1,0:T(8,128)S(1)} collective-permute-done((f32[8,3072]{1,0:T(8,128)S(1)}, f32[8,3072]{1,0:T(8,128)S(1)}, u32[]{:S(2)}, u32[]{:S(2)}) %collective-permute-start.12) | collective-permute-done | bytes 98336 | tf_op jit(solution)/shard_map/ppermute | solution.py:481
  49.2 1.2 %last.1 = f32[128,2048]{1,0:T(8,128)} custom-call(f32[128,2048]{1,0:T(8,128)S(1)} %rest.1.base, f32[1,2048]{1,0:T(1,128)S(1)} %get-tuple-element.44.mask, bf16[152,144]{1,0:T(8,128)(2,1)S(1)} %get-tuple-element.55.refs_5_.refs_0_, bf16[152,144]{1,0:T(8,128)(2,1)S(1)} %get-tuple-element.56.refs_6_.refs_1_, f32[8,3072]{1,0:T(8,128)S(1)} %collective-permute-done.10.refs_2_, ...), custom_call_target="tpu_custom_call" | custom-call | bytes 2509824 | tf_op jit(solution)/shard_map/last/pallas_call | solution.py:461
Async XLA Ops:
  1.3 7.3 %collective-permute-start = (f32[128,256]{1,0:T(8,128)S(1)}, f32[128,256]{1,0:T(8,128)S(1)}, u32[]{:S(2)}, u32[]{:S(2)}) collective-permute-start(f32[128,256]{1,0:T(8,128)S(1)} %get-tuple-element.42), channel_id=1, source_target_pairs={{1,2},{2,1},{5,6},{6,5},{9,10},{10,9},{13,14},{14,13},{17,18},{18,... | collective-permute-start | bytes 393224 | tf_op jit(solution)/shard_map/ppermute | solution.py:476
  5.8 2.8 %collective-permute-start.1 = (f32[128,256]{1,0:T(8,128)S(1)}, f32[128,256]{1,0:T(8,128)S(1)}, u32[]{:S(2)}, u32[]{:S(2)}) collective-permute-start(f32[128,256]{1,0:T(8,128)S(1)} %get-tuple-element.43), channel_id=1, source_target_pairs={{0,1},{1,0},{2,3},{3,2},{4,5},{5,4},{6,7},{7,6},{8,9},{9,8},{10,11... | collective-permute-start | bytes 393224 | tf_op jit(solution)/shard_map/ppermute | solution.py:476
  8.6 10.6 %copy-start = (f32[128,2048]{1,0:T(8,128)S(1)}, f32[128,2048]{1,0:T(8,128)}, u32[]{:S(2)}) copy-start(f32[128,2048]{1,0:T(8,128)} %kappa.1) | copy-start | bytes 3145732
  10.3 7.9 %collective-permute-start.2 = (f32[8,3072]{1,0:T(8,128)S(1)}, f32[8,3072]{1,0:T(8,128)S(1)}, u32[]{:S(2)}, u32[]{:S(2)}) collective-permute-start(f32[8,3072]{1,0:T(8,128)S(1)} %get-tuple-element.51), channel_id=1, source_target_pairs={{0,12},{4,8},{8,4},{12,0},{1,13},{5,9},{9,5},{13,1},{2,14},{6,10},... | collective-permute-start | bytes 294920 | tf_op jit(solution)/shard_map/ppermute | solution.py:481
  13.7 5.5 %collective-permute-start.4 = (f32[8,3072]{1,0:T(8,128)S(1)}, f32[8,3072]{1,0:T(8,128)S(1)}, u32[]{:S(2)}, u32[]{:S(2)}) collective-permute-start(f32[8,3072]{1,0:T(8,128)S(1)} %get-tuple-element.53), channel_id=1, source_target_pairs={{0,4},{4,0},{8,12},{12,8},{1,5},{5,1},{9,13},{13,9},{2,6},{6,2},{1... | collective-permute-start | bytes 294920 | tf_op jit(solution)/shard_map/ppermute | solution.py:481
  13.7 4.5 %collective-permute-start.3 = (f32[8,1024]{1,0:T(8,128)S(1)}, f32[8,1024]{1,0:T(8,128)S(1)}, u32[]{:S(2)}, u32[]{:S(2)}) collective-permute-start(f32[8,1024]{1,0:T(8,128)S(1)} %get-tuple-element.52), channel_id=1, source_target_pairs={{0,8},{4,12},{8,0},{12,4},{1,9},{5,13},{9,1},{13,5},{2,10},{6,14},... | collective-permute-start | bytes 98312 | tf_op jit(solution)/shard_map/ppermute | solution.py:481
  20.3 9.0 %collective-permute-start.5 = (f32[16,2048]{1,0:T(8,128)S(1)}, f32[16,2048]{1,0:T(8,128)S(1)}, u32[]{:S(2)}, u32[]{:S(2)}) collective-permute-start(f32[16,2048]{1,0:T(8,128)S(1)} %get-tuple-element.63), channel_id=1, source_target_pairs={{0,12},{4,8},{8,4},{12,0},{1,13},{5,9},{9,5},{13,1},{2,14},{6,10},... | collective-permute-start | bytes 393224 | tf_op jit(solution)/shard_map/ppermute | solution.py:481
  22.1 9.5 %collective-permute-start.7 = (f32[16,2048]{1,0:T(8,128)S(1)}, f32[16,2048]{1,0:T(8,128)S(1)}, u32[]{:S(2)}, u32[]{:S(2)}) collective-permute-start(f32[16,2048]{1,0:T(8,128)S(1)} %get-tuple-element.65), channel_id=1, source_target_pairs={{0,4},{4,0},{8,12},{12,8},{1,5},{5,1},{9,13},{13,9},{2,6},{6,2},{1... | collective-permute-start | bytes 393224 | tf_op jit(solution)/shard_map/ppermute | solution.py:481
  22.4 6.9 %collective-permute-start.6 = (f32[8,2048]{1,0:T(8,128)S(1)}, f32[8,2048]{1,0:T(8,128)S(1)}, u32[]{:S(2)}, u32[]{:S(2)}) collective-permute-start(f32[8,2048]{1,0:T(8,128)S(1)} %get-tuple-element.64), channel_id=1, source_target_pairs={{0,8},{4,12},{8,0},{12,4},{1,9},{5,13},{9,1},{13,5},{2,10},{6,14},... | collective-permute-start | bytes 196616 | tf_op jit(solution)/shard_map/ppermute | solution.py:481
  32.7 6.5 %collective-permute-start.8 = (f32[152,256]{1,0:T(8,128)S(1)}, f32[152,256]{1,0:T(8,128)S(1)}, u32[]{:S(2)}, u32[]{:S(2)}) collective-permute-start(f32[152,256]{1,0:T(8,128)S(1)} %get-tuple-element.67), channel_id=1, source_target_pairs={{1,2},{2,1},{5,6},{6,5},{9,10},{10,9},{13,14},{14,13},{17,18},{18,... | collective-permute-start | bytes 466952 | tf_op jit(solution)/shard_map/ppermute | solution.py:476
  34.8 4.4 %collective-permute-start.9 = (f32[152,256]{1,0:T(8,128)S(1)}, f32[152,256]{1,0:T(8,128)S(1)}, u32[]{:S(2)}, u32[]{:S(2)}) collective-permute-start(f32[152,256]{1,0:T(8,128)S(1)} %get-tuple-element.68), channel_id=1, source_target_pairs={{0,1},{1,0},{2,3},{3,2},{4,5},{5,4},{6,7},{7,6},{8,9},{9,8},{10,11... | collective-permute-start | bytes 466952 | tf_op jit(solution)/shard_map/ppermute | solution.py:476
  41.2 6.4 %collective-permute-start.10 = (f32[8,3072]{1,0:T(8,128)S(1)}, f32[8,3072]{1,0:T(8,128)S(1)}, u32[]{:S(2)}, u32[]{:S(2)}) collective-permute-start(f32[8,3072]{1,0:T(8,128)S(1)} %get-tuple-element.74), channel_id=1, source_target_pairs={{0,12},{4,8},{8,4},{12,0},{1,13},{5,9},{9,5},{13,1},{2,14},{6,10},... | collective-permute-start | bytes 294920 | tf_op jit(solution)/shard_map/ppermute | solution.py:481
  41.8 7.4 %collective-permute-start.12 = (f32[8,3072]{1,0:T(8,128)S(1)}, f32[8,3072]{1,0:T(8,128)S(1)}, u32[]{:S(2)}, u32[]{:S(2)}) collective-permute-start(f32[8,3072]{1,0:T(8,128)S(1)} %get-tuple-element.76), channel_id=1, source_target_pairs={{0,4},{4,0},{8,12},{12,8},{1,5},{5,1},{9,13},{13,9},{2,6},{6,2},{1... | collective-permute-start | bytes 294920 | tf_op jit(solution)/shard_map/ppermute | solution.py:481
  41.8 5.8 %collective-permute-start.11 = (f32[8,1024]{1,0:T(8,128)S(1)}, f32[8,1024]{1,0:T(8,128)S(1)}, u32[]{:S(2)}, u32[]{:S(2)}) collective-permute-start(f32[8,1024]{1,0:T(8,128)S(1)} %get-tuple-element.75), channel_id=1, source_target_pairs={{0,8},{4,12},{8,0},{12,4},{1,9},{5,13},{9,1},{13,5},{2,10},{6,14},... | collective-permute-start | bytes 98312 | tf_op jit(solution)/shard_map/ppermute | solution.py:481

commit v4 on v3

--- a/solution.py
+++ b/solution.py
@@ -164,7 +164,7 @@
 
 
 def sides():
-    first = lax.axis_index("xs") % 2
+    first = 1 - lax.axis_index("xs") % 2
     return first, 1 - first
 
 
@@ -473,7 +473,7 @@
 def trade_faces(first, second):
     count = lax.axis_size("xs")
     swap = lambda start: [pair for i in range(start, count - 1, 2) for pair in ((i, i + 1), (i + 1, i))]
-    return lax.ppermute(first, "xs", swap(1)), lax.ppermute(second, "xs", swap(0))
+    return lax.ppermute(first, "xs", swap(0)), lax.ppermute(second, "xs", swap(1))
 
 
 def trade_slabs(parts):

time: 51.5 us -> 48.5 us (0.942); the launches traced: 50.5 us -> 48.2 us
  waiting for transfers between devices: 8.98 us -> 6.03 us
  starting transfers between devices: 17.7 us -> 18.3 us
    ppermute x9, waiting for transfers between devices: 6.82 us -> 4.06 us  [trade_slabs(): lax.ppermute(part, 'hgt', [(i, i ^ x) for i in range(count)])]
  transfers between devices with their start and end apart: 13 -> 13, of which waited for: 6 -> 7; matrix products, arithmetic and copies ran while one was open for 0% -> 0% of each run, Pallas kernels for 29% -> 30%
where the time goes in v4:
time: 48.5 us; the launch traced here: 48.2 us
  Pallas kernels  22.9 us (47%)
  starting transfers between devices  18.3 us (38%)
  waiting for transfers between devices  6.03 us (12%)
  between operations  0.94 us (2%)
    pallas_call x11, Pallas kernels, call(): pl.pallas_call(kernel, in_specs=[pl.BlockSpec(memory_space=space) for arr...  22.9 us
    ppermute x9, starting transfers between devices, trade_slabs(): lax.ppermute(part, 'hgt', [(i, i ^ x) for i in range(count)])  11.3 us
    ppermute x2, starting transfers between devices, trade_faces(): lax.ppermute(second, 'xs', swap(1))  6.84 us
    ppermute x9, waiting for transfers between devices, trade_slabs(): lax.ppermute(part, 'hgt', [(i, i ^ x) for i in range(count)])  4.06 us
    ppermute x2, waiting for transfers between devices, trade_faces(): lax.ppermute(second, 'xs', swap(1))  1.97 us
  transfers between devices with their start and end apart: 13, of which 7 were waited for; matrix products, arithmetic and copies ran while one was open for 0% of the time, Pallas kernels for 30%

profile of v4, /device:TPU:1, one launch (start us, length us, event | category | flops | bytes accessed | tf_op | source)
XLA Modules:
  0.0 48.2 jit_solution(6477835829671834729)
XLA Ops:
  0.0 1.3 %faces.1 = (f32[128,256]{1,0:T(8,128)S(1)}, f32[128,256]{1,0:T(8,128)S(1)}) custom-call(s32[2,4]{1,0:T(2,128)} %bitcast.15, f32[128,2048]{1,0:T(8,128)} %field.3), custom_call_target="tpu_custom_call" | custom-call | bytes 262144 | tf_op jit(solution)/shard_map/faces/pallas_call | solution.py:461
  1.3 0.1 collective-permute-start
  1.4 4.5 %collective-permute-start.1 = (f32[128,256]{1,0:T(8,128)S(1)}, f32[128,256]{1,0:T(8,128)S(1)}, u32[]{:S(2)}, u32[]{:S(2)}) collective-permute-start(f32[128,256]{1,0:T(8,128)S(1)} %get-tuple-element.43), channel_id=1, source_target_pairs={{1,2},{2,1},{5,6},{6,5},{9,10},{10,9},{13,14},{14,13},{17,18},{18,... | collective-permute-start | bytes 393224 | tf_op jit(solution)/shard_map/ppermute | solution.py:476
  6.5 2.1 %prepare.1 = (f32[1,2048]{1,0:T(1,128)S(1)}, bf16[768,256]{1,0:T(8,128)(2,1)S(1)}, f32[128,2048]{1,0:T(8,128)S(1)}, f32[40,2048]{1,0:T(8,128)S(1)}, bf16[40,384]...) custom-call(s32[1]{0:T(128)S(6)} %copy.19.total, ...), custom_call_target="tpu_custom_call" | custom-call | flops 67108864 | bytes 3232256 | tf_op jit(solution)/shard_map/prepare/pallas_call | solution.py:461
  8.6 0.0 copy-start
  8.6 0.0 collective-permute-done.first
  8.6 0.0 collective-permute-done.1.second
  8.6 1.7 %moments.1 = (f32[8,3072]{1,0:T(8,128)S(1)}, f32[8,1024]{1,0:T(8,128)S(1)}, f32[8,3072]{1,0:T(8,128)S(1)}) custom-call(s32[6,32]{1,0:T(8,128)} %bitcast.4, f32[6,32]{1,0:T(8,128)} %bitcast.9, f32[40,2048]{1,0:T(8,128)S(1)} %get-tuple-element.49.moments, f32[128,256]{1,0:T(8,128)S(1)} %collective-permute-done.first, ...), custom_call_target="tpu_custom_call" | custom-call | bytes 1675264 | tf_op jit(solution)/shard_map/moments/pallas_call | solution.py:461
  10.3 3.7 %collective-permute-start.2 = (f32[8,3072]{1,0:T(8,128)S(1)}, f32[8,3072]{1,0:T(8,128)S(1)}, u32[]{:S(2)}, u32[]{:S(2)}) collective-permute-start(f32[8,3072]{1,0:T(8,128)S(1)} %get-tuple-element.51), channel_id=1, source_target_pairs={{0,12},{4,8},{8,4},{12,0},{1,13},{5,9},{9,5},{13,1},{2,14},{6,10},... | collective-permute-start | bytes 294920 | tf_op jit(solution)/shard_map/ppermute | solution.py:481
  14.1 0.0 collective-permute-start.4
  14.1 0.4 collective-permute-start.3
  14.4 3.1 %first.1 = (f32[128,2048]{1,0:T(8,128)S(1)}, f32[128,2048]{1,0:T(8,128)S(1)}) custom-call(s32[6,32]{1,0:T(8,128)} %bitcast.5, f32[6,32]{1,0:T(8,128)} %bitcast.10, f32[128,2048]{1,0:T(8,128)S(1)} %get-tuple-element.41.field, f32[128,256]{1,0:T(8,128)S(1)} %collective-permute-done.first, f32[128,256]{1,0:T(8,128)S(1)} %collective-permute-done.1.second, ...), custom_call_target="tpu_custom_call" | custom-call | flops 134217728 | bytes 4435968 | tf_op jit(solution)/shard_map/first/pallas_call | solution.py:461
  17.5 0.4 collective-permute-done.3.refs_1_
  18.0 0.0 collective-permute-done.2.refs_0_
  18.0 0.4 collective-permute-done.4.refs_2_
  18.4 0.0 copy-done
  18.4 1.1 %flux.1 = (f32[128,2048]{1,0:T(8,128)S(1)}, f32[24,2048]{1,0:T(8,128)S(1)}, f32[16,2048]{1,0:T(8,128)S(1)}, f32[8,2048]{1,0:T(8,128)S(1)}, f32[16,2048]{1,0:T(8,128)S(1)}) custom-call(f32[128,2048]{1,0:T(8,128)S(1)} %get-tuple-element.48.slope, f32[8,3072]{1,0:T(8,128)S(1)} %collective-permute-done.2.refs_0_, f32[8,1024]{1,0:T(8,128)S(1)} %collective-permute-done.3.refs_1_, ...), custom_call_target="tpu_custom_call" | custom-call | bytes 4135936 | tf_op jit(solution)/shard_map/flux/pallas_call | solution.py:461
  19.4 2.4 %collective-permute-start.5 = (f32[16,2048]{1,0:T(8,128)S(1)}, f32[16,2048]{1,0:T(8,128)S(1)}, u32[]{:S(2)}, u32[]{:S(2)}) collective-permute-start(f32[16,2048]{1,0:T(8,128)S(1)} %get-tuple-element.63), channel_id=1, source_target_pairs={{0,12},{4,8},{8,4},{12,0},{1,13},{5,9},{9,5},{13,1},{2,14},{6,10},... | collective-permute-start | bytes 393224 | tf_op jit(solution)/shard_map/ppermute | solution.py:481
  21.8 0.0 collective-permute-start.7
  21.8 1.2 %collective-permute-start.6 = (f32[8,2048]{1,0:T(8,128)S(1)}, f32[8,2048]{1,0:T(8,128)S(1)}, u32[]{:S(2)}, u32[]{:S(2)}) collective-permute-start(f32[8,2048]{1,0:T(8,128)S(1)} %get-tuple-element.64), channel_id=1, source_target_pairs={{0,8},{4,12},{8,0},{12,4},{1,9},{5,13},{9,1},{13,5},{2,10},{6,14},... | collective-permute-start | bytes 196616 | tf_op jit(solution)/shard_map/ppermute | solution.py:481
  23.0 4.5 %local.1 = (f32[152,2048]{1,0:T(8,128)S(1)}, f32[128,2048]{1,0:T(8,128)S(1)}, bf16[512,2048]{1,0:T(8,128)(2,1)S(1)}, bf16[512,2048]{1,0:T(8,128)(2,1)S(1)}) custom-call(s32[6,32]{1,0:T(8,128)} %bitcast.6, f32[6,32]{1,0:T(8,128)} %bitcast.11, f32[64,64]{1,0:T(8,128)} %matrix.3, f32[128,2048]{1,0:T(8,128)S(1)} %get-tuple-element.47.field, ...), custom_call_target="tpu_custom_call" | custom-call | flops 268435456 | bytes 14249984 | tf_op jit(solution)/shard_map/local/pallas_call | solution.py:461
  27.5 1.8 %collective-permute-done.6.refs_1_ = f32[8,2048]{1,0:T(8,128)S(1)} collective-permute-done((f32[8,2048]{1,0:T(8,128)S(1)}, f32[8,2048]{1,0:T(8,128)S(1)}, u32[]{:S(2)}, u32[]{:S(2)}) %collective-permute-start.6) | collective-permute-done | bytes 65568 | tf_op jit(solution)/shard_map/ppermute | solution.py:481
  29.3 0.0 collective-permute-done.5.refs_0_
  29.3 0.9 %collective-permute-done.7.refs_2_ = f32[16,2048]{1,0:T(8,128)S(1)} collective-permute-done((f32[16,2048]{1,0:T(8,128)S(1)}, f32[16,2048]{1,0:T(8,128)S(1)}, u32[]{:S(2)}, u32[]{:S(2)}) %collective-permute-start.7) | collective-permute-done | bytes 131104 | tf_op jit(solution)/shard_map/ppermute | solution.py:481
  30.2 1.0 %rim.1 = (f32[152,256]{1,0:T(8,128)S(1)}, f32[152,256]{1,0:T(8,128)S(1)}) custom-call(s32[2,4]{1,0:T(2,128)} %bitcast.16, f32[152,2048]{1,0:T(8,128)S(1)} %get-tuple-element.60.base, f32[1,2048]{1,0:T(1,128)S(1)} %get-tuple-element.44.mask, bf16[152,144]{1,0:T(8,128)(2,1)S(1)} %get-tuple-element.66.far, f32[16,2048]{1,0:T(8,128)S(1)} %collective-permute-done.5.refs_0_, ...), custom_call_target="tpu_custom_call" | custom-call | bytes 1979904 | tf_op jit(solution)/shard_map/rim/pallas_call | solution.py:461
  31.2 0.1 collective-permute-start.8
  31.3 2.4 %collective-permute-start.9 = (f32[152,256]{1,0:T(8,128)S(1)}, f32[152,256]{1,0:T(8,128)S(1)}, u32[]{:S(2)}, u32[]{:S(2)}) collective-permute-start(f32[152,256]{1,0:T(8,128)S(1)} %get-tuple-element.68), channel_id=1, source_target_pairs={{1,2},{2,1},{5,6},{6,5},{9,10},{10,9},{13,14},{14,13},{17,18},{18,... | collective-permute-start | bytes 466952 | tf_op jit(solution)/shard_map/ppermute | solution.py:476
  33.7 2.2 %close.1.slope = f32[128,2048]{1,0:T(8,128)S(1)} custom-call(s32[6,32]{1,0:T(8,128)} %bitcast.7, f32[6,32]{1,0:T(8,128)} %bitcast.12, f32[128,2048]{1,0:T(8,128)S(1)} %get-tuple-element.61.slope, f32[1,2048]{1,0:T(1,128)S(1)} %get-tuple-element.44.mask, bf16[768,256]{1,0:T(8,128)(2,1)S(1)} %get-tuple-element.45.spread, ...), custom_call_target="tpu_custom_call" | custom-call | flops 67108864 | bytes 3293184 | tf_op jit(solution)/shard_map/close/pallas_call | solution.py:461
  35.9 0.0 collective-permute-done.8.first
  35.9 2.0 %collective-permute-done.9.second = f32[152,256]{1,0:T(8,128)S(1)} collective-permute-done((f32[152,256]{1,0:T(8,128)S(1)}, f32[152,256]{1,0:T(8,128)S(1)}, u32[]{:S(2)}, u32[]{:S(2)}) %collective-permute-start.9) | collective-permute-done | bytes 155680 | tf_op jit(solution)/shard_map/ppermute | solution.py:476
  37.9 2.0 %second.1 = (f32[128,2048]{1,0:T(8,128)S(1)}, f32[8,3072]{1,0:T(8,128)S(1)}, f32[8,1024]{1,0:T(8,128)S(1)}, f32[8,3072]{1,0:T(8,128)S(1)}) custom-call(f32[128,2048]{1,0:T(8,128)S(1)} %close.1.slope, f32[152,256]{1,0:T(8,128)S(1)} %collective-permute-done.8.first, f32[152,256]{1,0:T(8,128)S(1)} %collective-permute-done.9.second, ...), custom_call_target="tpu_custom_call" | custom-call | bytes 12443648 | tf_op jit(solution)/shard_map/second/pallas_call | solution.py:461
  39.9 2.3 %collective-permute-start.10 = (f32[8,3072]{1,0:T(8,128)S(1)}, f32[8,3072]{1,0:T(8,128)S(1)}, u32[]{:S(2)}, u32[]{:S(2)}) collective-permute-start(f32[8,3072]{1,0:T(8,128)S(1)} %get-tuple-element.74), channel_id=1, source_target_pairs={{0,12},{4,8},{8,4},{12,0},{1,13},{5,9},{9,5},{13,1},{2,14},{6,10},... | collective-permute-start | bytes 294920 | tf_op jit(solution)/shard_map/ppermute | solution.py:481
  42.2 0.0 collective-permute-start.12
  42.2 1.3 %collective-permute-start.11 = (f32[8,1024]{1,0:T(8,128)S(1)}, f32[8,1024]{1,0:T(8,128)S(1)}, u32[]{:S(2)}, u32[]{:S(2)}) collective-permute-start(f32[8,1024]{1,0:T(8,128)S(1)} %get-tuple-element.75), channel_id=1, source_target_pairs={{0,8},{4,12},{8,0},{12,4},{1,9},{5,13},{9,1},{13,5},{2,10},{6,14},... | collective-permute-start | bytes 98312 | tf_op jit(solution)/shard_map/ppermute | solution.py:481
  43.5 2.8 %rest.1.base = f32[128,2048]{1,0:T(8,128)S(1)} custom-call(s32[6,32]{1,0:T(8,128)} %bitcast.8, f32[6,32]{1,0:T(8,128)} %bitcast.13, f32[152,2048]{1,0:T(8,128)S(1)} %get-tuple-element.60.base, f32[128,2048]{1,0:T(8,128)S(1)} %get-tuple-element.73.flux, f32[152,256]{1,0:T(8,128)S(1)} %collective-permute-done.8.first, ...), custom_call_target="tpu_custom_call" | custom-call | flops 134217728 | bytes 5096960 | tf_op jit(solution)/shard_map/rest/pallas_call | solution.py:461
  46.3 0.1 collective-permute-done.11.refs_3_
  46.5 0.0 collective-permute-done.10.refs_2_
  46.5 0.4 collective-permute-done.12.refs_4_
  46.8 1.2 %last.1 = f32[128,2048]{1,0:T(8,128)} custom-call(f32[128,2048]{1,0:T(8,128)S(1)} %rest.1.base, f32[1,2048]{1,0:T(1,128)S(1)} %get-tuple-element.44.mask, bf16[152,144]{1,0:T(8,128)(2,1)S(1)} %get-tuple-element.55.refs_5_.refs_0_, bf16[152,144]{1,0:T(8,128)(2,1)S(1)} %get-tuple-element.56.refs_6_.refs_1_, f32[8,3072]{1,0:T(8,128)S(1)} %collective-permute-done.10.refs_2_, ...), custom_call_target="tpu_custom_call" | custom-call | bytes 2509824 | tf_op jit(solution)/shard_map/last/pallas_call | solution.py:461
Async XLA Ops:
  1.3 7.3 %collective-permute-start = (f32[128,256]{1,0:T(8,128)S(1)}, f32[128,256]{1,0:T(8,128)S(1)}, u32[]{:S(2)}, u32[]{:S(2)}) collective-permute-start(f32[128,256]{1,0:T(8,128)S(1)} %get-tuple-element.42), channel_id=1, source_target_pairs={{0,1},{1,0},{2,3},{3,2},{4,5},{5,4},{6,7},{7,6},{8,9},{9,8},{10,11... | collective-permute-start | bytes 393224 | tf_op jit(solution)/shard_map/ppermute | solution.py:476
  1.4 7.2 %collective-permute-start.1 = (f32[128,256]{1,0:T(8,128)S(1)}, f32[128,256]{1,0:T(8,128)S(1)}, u32[]{:S(2)}, u32[]{:S(2)}) collective-permute-start(f32[128,256]{1,0:T(8,128)S(1)} %get-tuple-element.43), channel_id=1, source_target_pairs={{1,2},{2,1},{5,6},{6,5},{9,10},{10,9},{13,14},{14,13},{17,18},{18,... | collective-permute-start | bytes 393224 | tf_op jit(solution)/shard_map/ppermute | solution.py:476
  8.6 9.8 %copy-start = (f32[128,2048]{1,0:T(8,128)S(1)}, f32[128,2048]{1,0:T(8,128)}, u32[]{:S(2)}) copy-start(f32[128,2048]{1,0:T(8,128)} %kappa.1) | copy-start | bytes 3145732
  10.3 7.6 %collective-permute-start.2 = (f32[8,3072]{1,0:T(8,128)S(1)}, f32[8,3072]{1,0:T(8,128)S(1)}, u32[]{:S(2)}, u32[]{:S(2)}) collective-permute-start(f32[8,3072]{1,0:T(8,128)S(1)} %get-tuple-element.51), channel_id=1, source_target_pairs={{0,12},{4,8},{8,4},{12,0},{1,13},{5,9},{9,5},{13,1},{2,14},{6,10},... | collective-permute-start | bytes 294920 | tf_op jit(solution)/shard_map/ppermute | solution.py:481
  14.1 4.3 %collective-permute-start.4 = (f32[8,3072]{1,0:T(8,128)S(1)}, f32[8,3072]{1,0:T(8,128)S(1)}, u32[]{:S(2)}, u32[]{:S(2)}) collective-permute-start(f32[8,3072]{1,0:T(8,128)S(1)} %get-tuple-element.53), channel_id=1, source_target_pairs={{0,4},{4,0},{8,12},{12,8},{1,5},{5,1},{9,13},{13,9},{2,6},{6,2},{1... | collective-permute-start | bytes 294920 | tf_op jit(solution)/shard_map/ppermute | solution.py:481
  14.1 3.9 %collective-permute-start.3 = (f32[8,1024]{1,0:T(8,128)S(1)}, f32[8,1024]{1,0:T(8,128)S(1)}, u32[]{:S(2)}, u32[]{:S(2)}) collective-permute-start(f32[8,1024]{1,0:T(8,128)S(1)} %get-tuple-element.52), channel_id=1, source_target_pairs={{0,8},{4,12},{8,0},{12,4},{1,9},{5,13},{9,1},{13,5},{2,10},{6,14},... | collective-permute-start | bytes 98312 | tf_op jit(solution)/shard_map/ppermute | solution.py:481
  19.4 9.9 %collective-permute-start.5 = (f32[16,2048]{1,0:T(8,128)S(1)}, f32[16,2048]{1,0:T(8,128)S(1)}, u32[]{:S(2)}, u32[]{:S(2)}) collective-permute-start(f32[16,2048]{1,0:T(8,128)S(1)} %get-tuple-element.63), channel_id=1, source_target_pairs={{0,12},{4,8},{8,4},{12,0},{1,13},{5,9},{9,5},{13,1},{2,14},{6,10},... | collective-permute-start | bytes 393224 | tf_op jit(solution)/shard_map/ppermute | solution.py:481
  21.8 8.3 %collective-permute-start.7 = (f32[16,2048]{1,0:T(8,128)S(1)}, f32[16,2048]{1,0:T(8,128)S(1)}, u32[]{:S(2)}, u32[]{:S(2)}) collective-permute-start(f32[16,2048]{1,0:T(8,128)S(1)} %get-tuple-element.65), channel_id=1, source_target_pairs={{0,4},{4,0},{8,12},{12,8},{1,5},{5,1},{9,13},{13,9},{2,6},{6,2},{1... | collective-permute-start | bytes 393224 | tf_op jit(solution)/shard_map/ppermute | solution.py:481
  21.8 7.5 %collective-permute-start.6 = (f32[8,2048]{1,0:T(8,128)S(1)}, f32[8,2048]{1,0:T(8,128)S(1)}, u32[]{:S(2)}, u32[]{:S(2)}) collective-permute-start(f32[8,2048]{1,0:T(8,128)S(1)} %get-tuple-element.64), channel_id=1, source_target_pairs={{0,8},{4,12},{8,0},{12,4},{1,9},{5,13},{9,1},{13,5},{2,10},{6,14},... | collective-permute-start | bytes 196616 | tf_op jit(solution)/shard_map/ppermute | solution.py:481
  31.2 4.7 %collective-permute-start.8 = (f32[152,256]{1,0:T(8,128)S(1)}, f32[152,256]{1,0:T(8,128)S(1)}, u32[]{:S(2)}, u32[]{:S(2)}) collective-permute-start(f32[152,256]{1,0:T(8,128)S(1)} %get-tuple-element.67), channel_id=1, source_target_pairs={{0,1},{1,0},{2,3},{3,2},{4,5},{5,4},{6,7},{7,6},{8,9},{9,8},{10,11... | collective-permute-start | bytes 466952 | tf_op jit(solution)/shard_map/ppermute | solution.py:476
  31.3 6.5 %collective-permute-start.9 = (f32[152,256]{1,0:T(8,128)S(1)}, f32[152,256]{1,0:T(8,128)S(1)}, u32[]{:S(2)}, u32[]{:S(2)}) collective-permute-start(f32[152,256]{1,0:T(8,128)S(1)} %get-tuple-element.68), channel_id=1, source_target_pairs={{1,2},{2,1},{5,6},{6,5},{9,10},{10,9},{13,14},{14,13},{17,18},{18,... | collective-permute-start | bytes 466952 | tf_op jit(solution)/shard_map/ppermute | solution.py:476
  39.9 6.6 %collective-permute-start.10 = (f32[8,3072]{1,0:T(8,128)S(1)}, f32[8,3072]{1,0:T(8,128)S(1)}, u32[]{:S(2)}, u32[]{:S(2)}) collective-permute-start(f32[8,3072]{1,0:T(8,128)S(1)} %get-tuple-element.74), channel_id=1, source_target_pairs={{0,12},{4,8},{8,4},{12,0},{1,13},{5,9},{9,5},{13,1},{2,14},{6,10},... | collective-permute-start | bytes 294920 | tf_op jit(solution)/shard_map/ppermute | solution.py:481
  42.2 4.6 %collective-permute-start.12 = (f32[8,3072]{1,0:T(8,128)S(1)}, f32[8,3072]{1,0:T(8,128)S(1)}, u32[]{:S(2)}, u32[]{:S(2)}) collective-permute-start(f32[8,3072]{1,0:T(8,128)S(1)} %get-tuple-element.76), channel_id=1, source_target_pairs={{0,4},{4,0},{8,12},{12,8},{1,5},{5,1},{9,13},{13,9},{2,6},{6,2},{1... | collective-permute-start | bytes 294920 | tf_op jit(solution)/shard_map/ppermute | solution.py:481
  42.2 4.2 %collective-permute-start.11 = (f32[8,1024]{1,0:T(8,128)S(1)}, f32[8,1024]{1,0:T(8,128)S(1)}, u32[]{:S(2)}, u32[]{:S(2)}) collective-permute-start(f32[8,1024]{1,0:T(8,128)S(1)} %get-tuple-element.75), channel_id=1, source_target_pairs={{0,8},{4,12},{8,0},{12,4},{1,9},{5,13},{9,1},{13,5},{2,10},{6,14},... | collective-permute-start | bytes 98312 | tf_op jit(solution)/shard_map/ppermute | solution.py:481
